TPU v7x, 32 devices: a whole 2x2x4 slice. The times are simulated.
32 devices in a mesh: seq: 4 (over y, x), fsdp: 8 (over z, core).
Axes of the slice: x: 2, y: 2, z: 4, core: 2. Of those that a mesh axis runs over, the one named last changes fastest.
Arguments:
- tokens: bfloat16 [8, 2048, 1024], P('fsdp', 'seq'), may hold values from -6 to 6
- prompt_lens: int32 [8], P('fsdp'), may hold values from 512 to 1024, as said below
- cont_lens: int32 [8, 2], P('fsdp'), may hold values from 256 to 512, as said below
- gain_one: bfloat16 [1024], P('fsdp'), may hold values from 0.5 to 1.5
- shift_one: bfloat16 [1024], P('fsdp'), may hold values from -4 to 4
- w_qkv: bfloat16 [1024, 3072], P('fsdp'), may hold values from -0.25 to 0.25
- bias_qv: bfloat16 [2048], P('fsdp'), may hold values from -4 to 4
- w_out: bfloat16 [1024, 1024], P('fsdp'), may hold values from -0.375 to 0.375
- bias_out: bfloat16 [1024], P('fsdp'), may hold values from -4 to 4
- gain_two: bfloat16 [1024], P('fsdp'), may hold values from 0.5 to 1.5
- shift_two: bfloat16 [1024], P('fsdp'), may hold values from -4 to 4
- w_fc: bfloat16 [1024, 4096], P('fsdp'), may hold values from -0.1875 to 0.1875
- bias_fc: bfloat16 [4096], P('fsdp'), may hold values from -4 to 4
- w_proj: bfloat16 [4096, 1024], P('fsdp'), may hold values from -0.1875 to 0.1875
- bias_proj: bfloat16 [1024], P('fsdp'), may hold values from -4 to 4
- cotangent: bfloat16 [8, 2048, 1024], P('fsdp', 'seq'), may hold values from -6 to 6
Outputs:
- output: bfloat16 [8, 2048, 1024], P('fsdp', 'seq')
- input_grad: float32 [8, 2048, 1024], P('fsdp', 'seq')
- grad_gain_one: float32 [1024], P('fsdp')
- grad_shift_one: float32 [1024], P('fsdp')
- grad_w_qkv: float32 [1024, 3072], P('fsdp')
- grad_bias_qv: float32 [2048], P('fsdp')
- grad_w_out: float32 [1024, 1024], P('fsdp')
- grad_bias_out: float32 [1024], P('fsdp')
- grad_gain_two: float32 [1024], P('fsdp')
- grad_shift_two: float32 [1024], P('fsdp')
- grad_w_fc: float32 [1024, 4096], P('fsdp')
- grad_bias_fc: float32 [4096], P('fsdp')
- grad_w_proj: float32 [4096, 1024], P('fsdp')
- grad_bias_proj: float32 [1024], P('fsdp')
Inputs may be any that keep to these rules, and one draw needn't show every extreme that they name: `prompt_lens`: group 0's prompt has all 1024 tokens live. `cont_lens`: the first continuation of every group has all 512 tokens live.
All inputs are finite; a program needn't handle non-finite values.
Results may differ from a plain program's by a relative error of at most 0.02.
Values may be sent and summed in bfloat16 or wider, within the bound.
No kernel may reach another device: no remote copies, remote signals or barrier semaphores. Data moves between devices by JAX's collectives and lax.ppermute only.
A program may use at most 256 MiB of HBM per device.

v0:
```python
import jax
import jax.numpy as jnp
from jax import lax
from jax.sharding import PartitionSpec as P

H = 16
HD = 64
PROMPT = 1024
CONTLEN = 512
CONTS = 2


EPS = 1e-05
GELU_C = 0.7978845608028654
NEG = -1e30


def as_sent(shard):
    return jax.tree.map(lambda a: a.astype(jnp.bfloat16) if a.dtype == jnp.float32 else a, shard)


def layer_norm(values, gain, shift):
    center = values - jnp.mean(values, axis=-1, keepdims=True)
    spread = jnp.mean(center * center, axis=-1, keepdims=True)
    return center * lax.rsqrt(spread + EPS) * gain + shift


def gelu_tanh(values):
    return 0.5 * values * (1.0 + jnp.tanh(GELU_C * (values + 0.044715 * values * values * values)))


def describe(index, prompt_len, cont_len):
    in_prompt = index < PROMPT
    segment = jnp.where(in_prompt, 0, 1 + (index - PROMPT) // CONTLEN).astype(jnp.int32)
    offset = jnp.where(in_prompt, index, (index - PROMPT) % CONTLEN).astype(jnp.int32)
    slots = jnp.arange(1, CONTS + 1, dtype=jnp.int32)
    picked = jnp.sum(jnp.where(segment[:, None] == slots[None, :], cont_len[None, :], 0), axis=1)
    limit = jnp.where(in_prompt, prompt_len, picked)
    return (segment, offset < limit)


def mask_of(rows, cols, prompt_len, cont_len):
    seg_rows, live_rows = describe(rows, prompt_len, cont_len)
    seg_cols, live_cols = describe(cols, prompt_len, cont_len)
    causal = (seg_rows[:, None] == seg_cols[None, :]) & (cols[None, :] <= rows[:, None])
    shared = (seg_cols[None, :] == 0) & (seg_rows[:, None] > 0)
    itself = cols[None, :] == rows[:, None]
    return (causal | shared) & (live_cols[None, :] | itself)


def outer_sum(left, right):
    return lax.dot_general(
        left, right, (((0,), (0,)), ((), ())), preferred_element_type=jnp.float32
    )


def times_trans(left, right):
    return lax.dot_general(
        left, right, (((1,), (1,)), ((), ())), preferred_element_type=jnp.float32
    )


def block_plan(total):
    block_rows = min(512, total)
    plan = []
    for index_block in range(total // block_rows):
        start = index_block * block_rows
        end = start + block_rows
        if end <= PROMPT:
            pieces = [(0, end)]
        else:
            lower = PROMPT + (max(start, PROMPT) - PROMPT) // CONTLEN * CONTLEN
            pieces = [(0, end)] if lower <= PROMPT else [(0, PROMPT), (lower, end)]
        plan.append((start, block_rows, pieces))
    return plan


def take_pieces(values, pieces):
    return jnp.concatenate([values[low_edge:high_edge] for low_edge, high_edge in pieces], axis=0)


def piece_columns(pieces):
    return jnp.concatenate(
        [jnp.arange(low_edge, high_edge, dtype=jnp.int32) for low_edge, high_edge in pieces]
    )


def block_scores(query_block, key_block, start, cols, prompt_len, cont_len):
    rows = start + jnp.arange(query_block.shape[0], dtype=jnp.int32)
    allowed = mask_of(rows, cols, prompt_len, cont_len)
    scores = (
        jnp.einsum("qhd,khd->hqk", query_block, key_block, preferred_element_type=jnp.float32)
        * 0.125
    )
    return jnp.where(allowed[None], scores, NEG)


def attend_forward(queries, key_rows, value_rows, prompt_len, cont_len):
    total = key_rows.shape[0]
    mixed_parts = []
    norm_parts = []
    for start, block_rows, pieces in block_plan(total):
        query_block = queries[start : start + block_rows]
        key_block = take_pieces(key_rows, pieces)
        value_block = take_pieces(value_rows, pieces)
        scores = block_scores(
            query_block, key_block, start, piece_columns(pieces), prompt_len, cont_len
        )
        top = jnp.max(scores, axis=-1, keepdims=True)
        expo = jnp.exp(scores - top)
        denom = jnp.sum(expo, axis=-1, keepdims=True)
        probs_low = (expo / denom).astype(jnp.bfloat16)
        mixed = jnp.einsum(
            "hqk,khd->qhd", probs_low, value_block, preferred_element_type=jnp.float32
        )
        mixed_parts.append(mixed.astype(jnp.bfloat16))
        norm_parts.append((top + jnp.log(denom))[..., 0])
    mixed_all = jnp.concatenate(mixed_parts, axis=0)
    return (mixed_all.reshape(total, -1), jnp.stack(norm_parts))


def attend_backward(queries, key_rows, value_rows, grad_mixed, log_norm, prompt_len, cont_len):
    total = key_rows.shape[0]
    key_grad = jnp.zeros(key_rows.shape, jnp.float32)
    value_grad = jnp.zeros(key_rows.shape, jnp.float32)
    query_parts = []
    for number, (start, block_rows, pieces) in enumerate(block_plan(total)):
        query_block = queries[start : start + block_rows]
        grad_block = grad_mixed[start : start + block_rows]
        key_block = take_pieces(key_rows, pieces)
        value_block = take_pieces(value_rows, pieces)
        scores = block_scores(
            query_block, key_block, start, piece_columns(pieces), prompt_len, cont_len
        )
        probs = jnp.exp(scores - log_norm[number][..., None])
        grad_probs = jnp.einsum(
            "qhd,khd->hqk", grad_block, value_block, preferred_element_type=jnp.float32
        )
        inner = jnp.sum(probs * grad_probs, axis=-1, keepdims=True)
        grad_scores = (probs * (grad_probs - inner)).astype(jnp.bfloat16)
        query_parts.append(
            jnp.einsum("hqk,khd->qhd", grad_scores, key_block, preferred_element_type=jnp.float32)
            * 0.125
        )
        key_part = (
            jnp.einsum("hqk,qhd->khd", grad_scores, query_block, preferred_element_type=jnp.float32)
            * 0.125
        )
        value_part = jnp.einsum(
            "hqk,qhd->khd",
            probs.astype(jnp.bfloat16),
            grad_block,
            preferred_element_type=jnp.float32,
        )
        offset = 0
        for low_edge, high_edge in pieces:
            count = high_edge - low_edge
            key_grad = key_grad.at[low_edge:high_edge].add(key_part[offset : offset + count])
            value_grad = value_grad.at[low_edge:high_edge].add(value_part[offset : offset + count])
            offset = offset + count
    query_grad = jnp.concatenate(query_parts, axis=0)
    return (
        query_grad.reshape(total, -1).astype(jnp.bfloat16),
        key_grad.reshape(total, -1).astype(jnp.bfloat16),
        value_grad.reshape(total, -1).astype(jnp.bfloat16),
    )


def body(
    tokens,
    prompt_lens,
    cont_lens,
    gain_one,
    shift_one,
    w_qkv,
    bias_qv,
    w_out,
    bias_out,
    gain_two,
    shift_two,
    w_fc,
    bias_fc,
    w_proj,
    bias_proj,
    cotangent,
):
    groups, tok_rows, width = tokens.shape
    head_local = H // lax.axis_size("seq")
    gathered = (
        lax.all_gather(gain_one, "fsdp", axis=0, tiled=True),
        lax.all_gather(shift_one, "fsdp", axis=0, tiled=True),
        lax.all_gather(w_qkv, "fsdp", axis=0, tiled=True),
        lax.all_gather(bias_qv, "fsdp", axis=0, tiled=True),
        lax.all_gather(w_out, "fsdp", axis=0, tiled=True),
        lax.all_gather(bias_out, "fsdp", axis=0, tiled=True),
        lax.all_gather(gain_two, "fsdp", axis=0, tiled=True),
        lax.all_gather(shift_two, "fsdp", axis=0, tiled=True),
        lax.all_gather(w_fc, "fsdp", axis=0, tiled=True),
        lax.all_gather(bias_fc, "fsdp", axis=0, tiled=True),
        lax.all_gather(w_proj, "fsdp", axis=0, tiled=True),
        lax.all_gather(bias_proj, "fsdp", axis=0, tiled=True),
    )
    gain_first = gathered[0].astype(jnp.float32)
    shift_first = gathered[1].astype(jnp.float32)
    qkv_full = gathered[2]
    qv_vector = gathered[3].astype(jnp.float32)
    out_full = gathered[4]
    out_vector = gathered[5].astype(jnp.float32)
    gain_second = gathered[6].astype(jnp.float32)
    shift_second = gathered[7].astype(jnp.float32)
    fc_full = gathered[8]
    fc_vector = gathered[9].astype(jnp.float32)
    proj_full = gathered[10]
    proj_vector = gathered[11].astype(jnp.float32)

    def split_heads(values):
        return values.reshape(groups, values.shape[1], head_local, HD)

    inputs = tokens.reshape(-1, width).astype(jnp.float32)
    first = layer_norm(inputs, gain_first, shift_first).astype(jnp.bfloat16)
    bias_all = jnp.concatenate(
        [qv_vector[:width], jnp.zeros((width,), jnp.float32), qv_vector[width:]]
    )
    qkv = (jnp.dot(first, qkv_full, preferred_element_type=jnp.float32) + bias_all).astype(
        jnp.bfloat16
    )
    qkv = qkv.reshape(groups, tok_rows, 3 * width)
    head_q, head_k, head_v = (
        lax.all_to_all(qkv[..., :width], "seq", split_axis=2, concat_axis=1, tiled=True),
        lax.all_to_all(qkv[..., width : 2 * width], "seq", split_axis=2, concat_axis=1, tiled=True),
        lax.all_to_all(qkv[..., 2 * width :], "seq", split_axis=2, concat_axis=1, tiled=True),
    )
    head_q = split_heads(head_q)
    head_k = split_heads(head_k)
    head_v = split_heads(head_v)

    def group_forward(group_args):
        return attend_forward(
            group_args[0], group_args[1], group_args[2], group_args[3], group_args[4]
        )

    mixed_heads, log_norm = lax.map(group_forward, (head_q, head_k, head_v, prompt_lens, cont_lens))
    mixed_tokens = lax.all_to_all(
        as_sent(mixed_heads), "seq", split_axis=1, concat_axis=2, tiled=True
    ).astype(mixed_heads.dtype)
    mixed_flat = mixed_tokens.reshape(-1, width)
    hidden = inputs + jnp.dot(mixed_flat, out_full, preferred_element_type=jnp.float32) + out_vector
    second = layer_norm(hidden, gain_second, shift_second).astype(jnp.bfloat16)
    pre = jnp.dot(second, fc_full, preferred_element_type=jnp.float32) + fc_vector
    act = gelu_tanh(pre).astype(jnp.bfloat16)
    result = hidden + jnp.dot(act, proj_full, preferred_element_type=jnp.float32) + proj_vector
    output = result.astype(jnp.bfloat16).reshape(groups, tok_rows, width)
    qkv_back, out_back, fc_back, proj_back = (
        lax.all_gather(w_qkv, "fsdp", axis=0, tiled=True),
        lax.all_gather(w_out, "fsdp", axis=0, tiled=True),
        lax.all_gather(w_fc, "fsdp", axis=0, tiled=True),
        lax.all_gather(w_proj, "fsdp", axis=0, tiled=True),
    )
    grad_branch = cotangent.reshape(-1, width)
    grad_bias_proj = jnp.sum(grad_branch.astype(jnp.float32), axis=0)
    grad_w_proj = outer_sum(act, grad_branch)
    grad_act = times_trans(grad_branch, proj_back)
    gelu_value, gelu_pull = jax.vjp(gelu_tanh, pre)
    grad_pre = gelu_pull(grad_act)[0].astype(jnp.bfloat16)
    grad_w_fc = outer_sum(second, grad_pre)
    grad_bias_fc = jnp.sum(grad_pre.astype(jnp.float32), axis=0)
    grad_second = times_trans(grad_pre, fc_back)
    norm_value, norm_pull = jax.vjp(layer_norm, hidden, gain_second, shift_second)
    grad_hidden_norm, grad_gain_two, grad_shift_two = norm_pull(grad_second)
    grad_hidden = cotangent.reshape(-1, width).astype(jnp.float32) + grad_hidden_norm
    grad_attn = grad_hidden.astype(jnp.bfloat16)
    grad_bias_out = jnp.sum(grad_attn.astype(jnp.float32), axis=0)
    grad_w_out = outer_sum(mixed_flat, grad_attn)
    grad_mixed = (
        times_trans(grad_attn, out_back).astype(jnp.bfloat16).reshape(groups, tok_rows, width)
    )
    grad_heads = split_heads(
        lax.all_to_all(grad_mixed, "seq", split_axis=2, concat_axis=1, tiled=True)
    )

    def group_backward(group_args):
        return attend_backward(
            group_args[0],
            group_args[1],
            group_args[2],
            group_args[3],
            group_args[4],
            group_args[5],
            group_args[6],
        )

    grad_q, grad_k, grad_v = lax.map(
        group_backward, (head_q, head_k, head_v, grad_heads, log_norm, prompt_lens, cont_lens)
    )
    tok_q, tok_k, tok_v = (
        lax.all_to_all(as_sent(grad_q), "seq", split_axis=1, concat_axis=2, tiled=True).astype(
            grad_q.dtype
        ),
        lax.all_to_all(as_sent(grad_k), "seq", split_axis=1, concat_axis=2, tiled=True).astype(
            grad_k.dtype
        ),
        lax.all_to_all(as_sent(grad_v), "seq", split_axis=1, concat_axis=2, tiled=True).astype(
            grad_v.dtype
        ),
    )
    grad_qkv = jnp.concatenate([tok_q, tok_k, tok_v], axis=-1).reshape(-1, 3 * width)
    grad_w_qkv = outer_sum(first, grad_qkv)
    grad_bias_qv = jnp.concatenate(
        [
            jnp.sum(tok_q.reshape(-1, width).astype(jnp.float32), axis=0),
            jnp.sum(tok_v.reshape(-1, width).astype(jnp.float32), axis=0),
        ]
    )
    grad_first = times_trans(grad_qkv, qkv_back)
    first_value, first_pull = jax.vjp(layer_norm, inputs, gain_first, shift_first)
    grad_input_norm, grad_gain_one, grad_shift_one = first_pull(grad_first)
    input_grad = (grad_hidden + grad_input_norm).reshape(groups, tok_rows, width)
    owned = (
        lax.psum_scatter(
            grad_gain_one.astype(jnp.bfloat16), "fsdp", scatter_dimension=0, tiled=True
        ).astype(jnp.float32),
        lax.psum_scatter(
            grad_shift_one.astype(jnp.bfloat16), "fsdp", scatter_dimension=0, tiled=True
        ).astype(jnp.float32),
        lax.psum_scatter(
            grad_w_qkv.astype(jnp.bfloat16), "fsdp", scatter_dimension=0, tiled=True
        ).astype(jnp.float32),
        lax.psum_scatter(
            grad_bias_qv.astype(jnp.bfloat16), "fsdp", scatter_dimension=0, tiled=True
        ).astype(jnp.float32),
        lax.psum_scatter(
            grad_w_out.astype(jnp.bfloat16), "fsdp", scatter_dimension=0, tiled=True
        ).astype(jnp.float32),
        lax.psum_scatter(
            grad_bias_out.astype(jnp.bfloat16), "fsdp", scatter_dimension=0, tiled=True
        ).astype(jnp.float32),
        lax.psum_scatter(
            grad_gain_two.astype(jnp.bfloat16), "fsdp", scatter_dimension=0, tiled=True
        ).astype(jnp.float32),
        lax.psum_scatter(
            grad_shift_two.astype(jnp.bfloat16), "fsdp", scatter_dimension=0, tiled=True
        ).astype(jnp.float32),
        lax.psum_scatter(
            grad_w_fc.astype(jnp.bfloat16), "fsdp", scatter_dimension=0, tiled=True
        ).astype(jnp.float32),
        lax.psum_scatter(
            grad_bias_fc.astype(jnp.bfloat16), "fsdp", scatter_dimension=0, tiled=True
        ).astype(jnp.float32),
        lax.psum_scatter(
            grad_w_proj.astype(jnp.bfloat16), "fsdp", scatter_dimension=0, tiled=True
        ).astype(jnp.float32),
        lax.psum_scatter(
            grad_bias_proj.astype(jnp.bfloat16), "fsdp", scatter_dimension=0, tiled=True
        ).astype(jnp.float32),
    )
    summed = (
        lax.psum(owned[0].astype(jnp.bfloat16), "seq").astype(jnp.float32),
        lax.psum(owned[1].astype(jnp.bfloat16), "seq").astype(jnp.float32),
        lax.psum(owned[2].astype(jnp.bfloat16), "seq").astype(jnp.float32),
        lax.psum(owned[3].astype(jnp.bfloat16), "seq").astype(jnp.float32),
        lax.psum(owned[4].astype(jnp.bfloat16), "seq").astype(jnp.float32),
        lax.psum(owned[5].astype(jnp.bfloat16), "seq").astype(jnp.float32),
        lax.psum(owned[6].astype(jnp.bfloat16), "seq").astype(jnp.float32),
        lax.psum(owned[7].astype(jnp.bfloat16), "seq").astype(jnp.float32),
        lax.psum(owned[8].astype(jnp.bfloat16), "seq").astype(jnp.float32),
        lax.psum(owned[9].astype(jnp.bfloat16), "seq").astype(jnp.float32),
        lax.psum(owned[10].astype(jnp.bfloat16), "seq").astype(jnp.float32),
        lax.psum(owned[11].astype(jnp.bfloat16), "seq").astype(jnp.float32),
    )
    return (
        output,
        input_grad,
        summed[0],
        summed[1],
        summed[2],
        summed[3],
        summed[4],
        summed[5],
        summed[6],
        summed[7],
        summed[8],
        summed[9],
        summed[10],
        summed[11],
    )


def solution(mesh):
    placed = (
        P("fsdp", "seq", None),
        P("fsdp"),
        P("fsdp", None),
        P("fsdp"),
        P("fsdp"),
        P("fsdp", None),
        P("fsdp"),
        P("fsdp", None),
        P("fsdp"),
        P("fsdp"),
        P("fsdp"),
        P("fsdp", None),
        P("fsdp"),
        P("fsdp", None),
        P("fsdp"),
        P("fsdp", "seq", None),
    )
    return jax.shard_map(
        body,
        mesh=mesh,
        in_specs=placed,
        out_specs=(
            P("fsdp", "seq", None),
            P("fsdp", "seq", None),
            P("fsdp"),
            P("fsdp"),
            P("fsdp", None),
            P("fsdp"),
            P("fsdp", None),
            P("fsdp"),
            P("fsdp"),
            P("fsdp"),
            P("fsdp", None),
            P("fsdp"),
            P("fsdp", None),
            P("fsdp"),
        ),
        check_vma=False,
    )
```

profile of v0, /device:TPU:0, one launch (start us, length us, event | category | flops | bytes accessed | tf_op | source)
XLA Modules:
  0.0 898.4 jit_solution(12952376915148957828)
XLA Ops:
  13.3 13.5 %all-gather = bf16[8,1,128]{2,1,0:T(2,128)(2,1)S(1)} all-gather(bf16[1,1,128]{2,1,0:T(2,128)(2,1)S(1)} %bitcast.358), channel_id=1, replica_groups=mesh['seq'=4,'fsdp'=8] {'fsdp'}, dimensions={0}, use_global_device_ids=true | all-gather | bytes 2304 | tf_op jit(solution)/shard_map/all_gather | solution.py:190
  26.9 9.1 %all-gather.1 = bf16[8,1,128]{2,1,0:T(2,128)(2,1)S(1)} all-gather(bf16[1,1,128]{2,1,0:T(2,128)(2,1)S(1)} %bitcast.359), channel_id=1, replica_groups=mesh['seq'=4,'fsdp'=8] {'fsdp'}, dimensions={0}, use_global_device_ids=true | all-gather | bytes 2304 | tf_op jit(solution)/shard_map/all_gather | solution.py:191
  36.2 12.0 %all-gather.2 = bf16[8,1,256]{2,1,0:T(2,128)(2,1)S(1)} all-gather(bf16[1,1,256]{2,1,0:T(2,128)(2,1)S(1)} %reshape.1569), channel_id=1, replica_groups=mesh['seq'=4,'fsdp'=8] {'fsdp'}, dimensions={0}, use_global_device_ids=true | all-gather | bytes 4608 | tf_op jit(solution)/shard_map/all_gather | solution.py:193
  48.4 28.8 %all-gather.13.cloned.1.call-done = bf16[1024,3072]{1,0:T(8,128)(2,1)} async-done(((bf16[128,3072]{1,0:T(8,128)(2,1)}), bf16[1024,3072]{1,0:T(8,128)(2,1)}) %all-gather.13.cloned.1.call-update) | async-done | bytes 6291472 | tf_op jit(solution)/shard_map/all_gather | solution.py:192
  77.2 6.7 fusion.24
  85.7 4.6 copy.130
  90.8 8.0 reduce.41
  98.8 3.7 reshape.1603
  102.6 4.5 all-to-all-start
  109.0 4.6 copy.132
  113.6 8.0 reduce.40
  121.7 3.7 reshape.1601
  125.4 4.6 all-to-all-start.2
  132.5 4.6 copy.131
  137.1 8.0 reduce.39
  145.1 3.8 reshape.1599
  148.9 4.4 all-to-all-start.1
  176.3 4.2 reshape.1600
  190.1 6.7 fusion.225
  200.2 10.1 %fusion.1 = f32[4,512]{1,0:T(4,128)S(1)} fusion(f32[4,512,1536]{2,1,0:T(8,128)} %get-tuple-element.294, f32[4,512]{1,0:T(4,128)S(1)} %get-tuple-element.293), kind=kLoop, calls=%fused_computation.17 | loop fusion | flops 6289408 | bytes 12599296 | tf_op jit(solution)/shard_map/while/body/eval_jaxpr/reduce_sum | solution.py:111
  212.2 5.1 fusion.101
  217.4 6.1 fusion.100
  228.0 4.6 copy.138
  232.7 11.8 %reduce.42 = bf16[2048,256]{1,0:T(8,128)(2,1)} reduce(bf16[2048,1,256]{2,1,0:T(2,128)(2,1)S(1)} %bitcast.281, bf16[]{:T(256)} %broadcast.1799), dimensions={1}, to_apply=%bitcast.185.reduce_sub_computation | reduce | bytes 2097154
  247.9 4.2 all-to-all-start.3
  252.2 9.7 %all-gather.3 = bf16[8,1,128]{2,1,0:T(2,128)(2,1)S(1)} all-gather(bf16[1,1,128]{2,1,0:T(2,128)(2,1)S(1)} %bitcast.360), channel_id=1, replica_groups=mesh['seq'=4,'fsdp'=8] {'fsdp'}, dimensions={0}, use_global_device_ids=true | all-gather | bytes 2304 | tf_op jit(solution)/shard_map/all_gather | solution.py:195
  262.0 9.5 %all-gather.4 = bf16[8,1,128]{2,1,0:T(2,128)(2,1)S(1)} all-gather(bf16[1,1,128]{2,1,0:T(2,128)(2,1)S(1)} %bitcast.361), channel_id=1, replica_groups=mesh['seq'=4,'fsdp'=8] {'fsdp'}, dimensions={0}, use_global_device_ids=true | all-gather | bytes 2304 | tf_op jit(solution)/shard_map/all_gather | solution.py:196
  271.5 9.4 %all-gather.5 = bf16[8,1,128]{2,1,0:T(2,128)(2,1)S(1)} all-gather(bf16[1,1,128]{2,1,0:T(2,128)(2,1)S(1)} %bitcast.362), channel_id=1, replica_groups=mesh['seq'=4,'fsdp'=8] {'fsdp'}, dimensions={0}, use_global_device_ids=true | all-gather | bytes 2304 | tf_op jit(solution)/shard_map/all_gather | solution.py:197
  280.9 12.8 %all-gather.6 = bf16[8,1,512]{2,1,0:T(2,128)(2,1)S(1)} all-gather(bf16[1,1,512]{2,1,0:T(2,128)(2,1)S(1)} %reshape.1577), channel_id=1, replica_groups=mesh['seq'=4,'fsdp'=8] {'fsdp'}, dimensions={0}, use_global_device_ids=true | all-gather | bytes 9216 | tf_op jit(solution)/shard_map/all_gather | solution.py:199
  303.5 10.6 %fusion.213 = f32[512,4096]{1,0:T(8,128)} fusion(bf16[1024,4096]{1,0:T(8,128)(2,1)} %all-gather.17.cloned.1.call-done, f32[512,1024]{1,0:T(8,128)S(1)} %get-tuple-element.302, f32[1024]{0:T(1024)S(1)} %bitcast.355, f32[1024]{0:T(1024)S(1)} %bitcast.342, f32[512]{0:T(512)S(1)} %fusion.204, f32[512]{0:T(512)S(1)} %broadcast_multiply_fusion), kind=kOutput, calls=%fused_computation.336 | convolution fusion | flops 4297588736 | bytes 18886656 | tf_op jit(solution)/shard_map/dot_general | solution.py:249
  314.1 15.4 %fusion.230 = (bf16[4096]{0:T(1024)(128)(2,1)}, bf16[512,4096]{1,0:T(8,128)(2,1)S(1)}) fusion(bf16[4096,1024]{1,0:T(8,128)(2,1)} %all-gather.19.cloned.1.call-done, bf16[1,512,1024]{2,1,0:T(8,128)(2,1)S(1)} %copy-done.13, f32[512,4096]{1,0:T(8,128)} %fusion.213, f32[4096]{0:T(1024)S(1)} %bitcast.337), kind=kOutput, calls=%fused_computation.351 | convolution fusion | flops 4349489152 | bytes 22044672 | tf_op jit(solution)/shard_map/dot_general | solution.py:58
  329.5 5.5 multiply_reduce_fusion.4
  342.6 7.0 reduce.43
  351.6 4.0 all-to-all-start.4
  358.4 11.3 %all-to-all-done.4 = bf16[4,2,65536]{2,1,0:T(2,128)(2,1)S(1)} async-done(((bf16[4,2,65536]{2,1,0:T(2,128)(2,1)}), bf16[4,2,65536]{2,1,0:T(2,128)(2,1)S(1)}, u32[]{:S(2)}, u32[]{:S(2)}) %all-to-all-start.4) | async-done | bytes 1048608 | tf_op jit(solution)/shard_map/all_to_all | solution.py:278
  382.3 6.0 multiply_reduce_fusion
  389.7 5.1 multiply_reduce_fusion.2
  397.6 5.9 multiply_reduce_fusion.1
  408.5 10.6 %reduce.44 = bf16[2048,256]{1,0:T(8,128)(2,1)S(1)} reduce(bf16[2048,1,256]{2,1,0:T(2,128)(2,1)S(1)} %bitcast.283, bf16[]{:T(256)} %broadcast.1799), dimensions={1}, to_apply=%bitcast.189.reduce_sub_computation | reduce | bytes 2097154
  420.7 3.7 all-to-all-start.7
  425.8 9.8 %multiply_convert_fusion = bf16[4,512,1536]{2,1,0:T(8,128)(2,1)S(1)} fusion(f32[4,512,1536]{2,1,0:T(8,128)} %get-tuple-element.311, f32[4,512,1536]{2,1,0:T(8,128)} %get-tuple-element.294, f32[4,512]{1,0:T(4,128)S(1)} %get-tuple-element.310, f32[4,512]{1,0:T(4,128)S(1)} %log_add_fusion), kind=kLoop, calls=%fused_computation | loop fusion | flops 12582912 | bytes 31473664 | tf_op jit(solution)/shard_map/while/body/eval_jaxpr/convert_element_type | solution.py:140
  440.1 6.7 multiply_convert_fusion.1
  448.9 4.4 multiply_convert_fusion.2
  456.5 6.0 copy.142
  462.5 12.6 %reduce.46 = bf16[2048,256]{1,0:T(8,128)(2,1)} reduce(bf16[2048,1,256]{2,1,0:T(2,128)(2,1)} %bitcast.284, bf16[]{:T(256)} %broadcast.1799), dimensions={1}, to_apply=%bitcast.193.reduce_sub_computation | reduce | bytes 2097154
  478.6 5.3 fusion.33
  489.5 4.7 all-to-all-start.5
  500.5 10.6 %reduce.45 = bf16[2048,256]{1,0:T(8,128)(2,1)S(1)} reduce(bf16[2048,1,256]{2,1,0:T(2,128)(2,1)S(1)} %bitcast.278, bf16[]{:T(256)} %broadcast.1799), dimensions={1}, to_apply=%bitcast.191.reduce_sub_computation | reduce | bytes 2097154
  512.8 4.2 all-to-all-start.6
  519.7 4.0 reshape.1614
  530.4 4.0 reshape.1612
  537.7 8.0 convolution_convert_fusion.2
  547.0 13.9 %convolution_convert_fusion = bf16[4096,1024]{1,0:T(8,128)(2,1)} fusion(bf16[1,512,1024]{2,1,0:T(8,128)(2,1)S(1)} %copy-done.14, f32[512,4096]{1,0:T(8,128)} %fusion.213, f32[4096]{0:T(1024)S(1)} %bitcast.338), kind=kOutput, calls=%fused_computation.33 | convolution fusion | flops 4320133120 | bytes 17842176 | tf_op jit(solution)/shard_map/dot_general | solution.py:52
  562.5 9.1 %convolution_convert_fusion.1 = bf16[1024,4096]{1,0:T(8,128)(2,1)} fusion(bf16[512,4096]{1,0:T(8,128)(2,1)} %copy-done.88, f32[512,1024]{1,0:T(8,128)S(1)} %copy-done.12, f32[1024]{0:T(1024)S(1)} %bitcast.356, f32[1024]{0:T(1024)S(1)} %bitcast.345, f32[512]{0:T(512)S(1)} %fusion.204, f32[512]{0:T(512)S(1)} %broadcast_multiply_fusion), kind=kOutput, calls=%fused_computation.34 | convolution fusion | flops 4301783040 | bytes 14692352 | tf_op jit(solution)/shard_map/dot_general | solution.py:52
  576.3 8.9 all-gather.7
  585.2 28.1 %reduce-scatter.5.cloned.1.call-done = bf16[128,3072]{1,0:T(8,128)(2,1)} async-done(((bf16[1024,3072]{1,0:T(8,128)(2,1)}), bf16[128,3072]{1,0:T(8,128)(2,1)}) %reduce-scatter.5.cloned.1.call-update) | async-done | bytes 786448 | tf_op jit(solution)/shard_map/reduce_scatter | solution.py:325
  613.4 90.3 %reduce-scatter.11.cloned.1.call-done = bf16[512,1024]{1,0:T(8,128)(2,1)} async-done(((bf16[4096,1024]{1,0:T(8,128)(2,1)}), bf16[512,1024]{1,0:T(8,128)(2,1)}) %reduce-scatter.11.cloned.1.call-update) | async-done | bytes 1048592 | tf_op jit(solution)/shard_map/reduce_scatter | solution.py:349
  703.6 90.3 %reduce-scatter.9.cloned.1.call-done = bf16[128,4096]{1,0:T(8,128)(2,1)} async-done(((bf16[1024,4096]{1,0:T(8,128)(2,1)}), bf16[128,4096]{1,0:T(8,128)(2,1)}) %reduce-scatter.9.cloned.1.call-update) | async-done | bytes 1048592 | tf_op jit(solution)/shard_map/reduce_scatter | solution.py:343
  794.0 12.2 %fusion.76 = bf16[1,512,1024]{2,1,0:T(8,128)(2,1)} fusion(f32[512,1024]{1,0:T(8,128)S(1)} %copy-done.12, bf16[4096,1024]{1,0:T(8,128)(2,1)} %all-gather.19.cloned.1.call-done, f32[1024]{0:T(1024)S(1)} %bitcast.357, f32[512,4096]{1,0:T(8,128)} %fusion.213, f32[4096]{0:T(1024)S(1)} %bitcast.339), kind=kOutput, calls=%fused_computation.120 | convolution fusion | flops 4317511680 | bytes 19943424 | tf_op jit(solution)/shard_map/dot_general | solution.py:251
  809.0 7.4 fusion.214
  818.7 26.0 %all-reduce.10 = (bf16[1024]{0:T(1024)(128)(2,1)S(1)}, bf16[1024]{0:T(1024)(128)(2,1)S(1)}, bf16[2048]{0:T(1024)(128)(2,1)S(1)}, bf16[1024]{0:T(1024)(128)(2,1)S...) all-reduce(bf16[1024]{0:T(1024)(128)(2,1)S(1)} %get-tuple-element.2, ...), channel_id=2, replica_groups=mesh['seq'=4,'fsdp'=8] {'fsdp'}, use_global_device_ids=true, to_apply=%region_25.26.clone | all-reduce | flops 12288 | bytes 49152
  845.3 10.9 %all-reduce.11 = (bf16[128]{0:T(256)(128)(2,1)S(1)}, bf16[128]{0:T(256)(128)(2,1)S(1)}, bf16[256]{0:T(256)(128)(2,1)S(1)}, bf16[128]{0:T(256)(128)(2,1)S(1)}, bf...) all-reduce(bf16[128]{0:T(256)(128)(2,1)S(1)} %dynamic-slice.113, ...), channel_id=1, replica_groups=mesh['seq'=4,'fsdp'=8] {'seq'}, use_global_device_ids=true, to_apply=%region_26.27 | all-reduce | flops 1536 | bytes 6144 | tf_op jit(solution)/shard_map/psum | solution.py:357
  860.5 4.2 add_bitcast_fusion
  864.7 18.4 %all-reduce.15.cloned.1.call-done = (bf16[128,3072]{1,0:T(8,128)(2,1)}, bf16[128,1024]{1,0:T(8,128)(2,1)}, bf16[128,4096]{1,0:T(8,128)(2,1)}, bf16[512,1024]{1,0:T(8,128)(2,1)}) async-done(((bf16[128,3072]{1,0:T(8,128)(2,1)}, bf16[128,1024]{1,0:T(8,128)(2,1)}, bf16[128,4096]{1,0:T(8,128)(2,1)}, bf16[512,1024]{1,0:T(8,128)(2,1)}), (bf16[128,3072]{1,0:T(8,128)(2,1)}, bf16[128,1024]{1,0:T(8,128)(2,1)}, ...) | async-done | bytes 3145744 | tf_op jit(solution)/shard_map/psum | solution.py:359
  (404 shorter events, 167.8 us)
Async XLA Ops:
  7.2 19.7 %copy-start.81 = (bf16[128]{0:T(256)(128)(2,1)S(1)}, bf16[128]{0:T(256)(128)(2,1)}, u32[]{:S(2)}) copy-start(bf16[128]{0:T(256)(128)(2,1)} %param.40) | copy-start | bytes 772
  7.2 28.8 %copy-start.72 = (s32[1,2]{1,0:T(1,128)S(1)}, s32[1,2]{1,0:T(1,128)}, u32[]{:S(2)}) copy-start(s32[1,2]{1,0:T(1,128)} %param.38) | copy-start | bytes 28
  7.2 70.0 %all-gather.13.cloned.1.call-start = ((), (), s32[]{:S(2)}) async-start(), calls=%async_computation.12 | async-start | bytes 7077888 | tf_op jit(solution)/shard_map/all_gather | solution.py:192
  8.0 291.8 %all-gather.15.cloned.1.call-start = ((), (), s32[]{:S(2)}) async-start(), calls=%async_computation.13 | async-start | bytes 2359296 | tf_op jit(solution)/shard_map/all_gather | solution.py:194
  8.7 294.7 %all-gather.17.cloned.1.call-start = ((), (), s32[]{:S(2)}) async-start(), calls=%async_computation.14 | async-start | bytes 9437184 | tf_op jit(solution)/shard_map/all_gather | solution.py:198
  9.4 304.7 %all-gather.19.cloned.1.call-start = ((), (), s32[]{:S(2)}) async-start(), calls=%async_computation.15 | async-start | bytes 9437184 | tf_op jit(solution)/shard_map/all_gather | solution.py:200
  12.9 71.0 %copy-start.62 = (f32[512]{0:T(512)}, f32[512]{0:T(512)S(1)}, u32[]{:S(2)}) copy-start(f32[512]{0:T(512)S(1)} %broadcast_multiply_fusion.1) | copy-start | bytes 6148
  13.3 34.9 %copy-start.66 = (f32[512]{0:T(512)}, f32[512]{0:T(512)S(1)}, u32[]{:S(2)}) copy-start(f32[512]{0:T(512)S(1)} %fusion.54) | copy-start | bytes 6148
  13.3 70.6 %copy-start.68 = (f32[512]{0:T(512)}, f32[512]{0:T(512)S(1)}, u32[]{:S(2)}) copy-start(f32[512]{0:T(512)S(1)} %fusion.203) | copy-start | bytes 6148
  26.9 57.0 %copy-start.60 = (f32[8,1,128]{2,1,0:T(1,128)}, f32[8,1,128]{2,1,0:T(1,128)S(1)}, u32[]{:S(2)}) copy-start(f32[8,1,128]{2,1,0:T(1,128)S(1)} %convert_element_type.346) | copy-start | bytes 12292
  36.0 47.9 %copy-start.73 = (f32[8,1,128]{2,1,0:T(1,128)}, f32[8,1,128]{2,1,0:T(1,128)S(1)}, u32[]{:S(2)}) copy-start(f32[8,1,128]{2,1,0:T(1,128)S(1)} %convert_element_type.347) | copy-start | bytes 12292
  102.6 22.8 %all-to-all-start = ((bf16[4,2,65536]{2,1,0:T(2,128)(2,1)}), bf16[4,2,65536]{2,1,0:T(2,128)(2,1)}, u32[]{:S(2)}, u32[]{:S(2)}) async-start(bf16[4,2,65536]{2,1,0:T(2,128)(2,1)} %reshape.1603), calls=%async_computation | async-start | bytes 2097152 | tf_op jit(solution)/shard_map/all_to_all | solution.py:231
  125.4 23.5 %all-to-all-start.2 = ((bf16[4,2,65536]{2,1,0:T(2,128)(2,1)}), bf16[4,2,65536]{2,1,0:T(2,128)(2,1)}, u32[]{:S(2)}, u32[]{:S(2)}) async-start(bf16[4,2,65536]{2,1,0:T(2,128)(2,1)} %reshape.1601), calls=%async_computation.2 | async-start | bytes 2097152 | tf_op jit(solution)/shard_map/all_to_all | solution.py:230
  148.9 27.4 %all-to-all-start.1 = ((bf16[4,2,65536]{2,1,0:T(2,128)(2,1)}), bf16[4,2,65536]{2,1,0:T(2,128)(2,1)}, u32[]{:S(2)}, u32[]{:S(2)}) async-start(bf16[4,2,65536]{2,1,0:T(2,128)(2,1)} %reshape.1599), calls=%async_computation.1 | async-start | bytes 2097152 | tf_op jit(solution)/shard_map/all_to_all | solution.py:229
  171.9 18.3 %copy-start.17 = (bf16[1024,4,64]{0,2,1:T(8,128)(2,1)}, bf16[1024,4,64]{0,2,1:T(8,128)(2,1)S(1)}, u32[]{:S(2)}) copy-start(bf16[1024,4,64]{0,2,1:T(8,128)(2,1)S(1)} %slice.522) | copy-start | bytes 1572868
  173.5 8.9 copy-start.21
  176.3 20.5 %copy-start.24 = (bf16[1536,4,64]{0,2,1:T(8,128)(2,1)}, bf16[1536,4,64]{0,2,1:T(8,128)(2,1)S(1)}, u32[]{:S(2)}) copy-start(bf16[1536,4,64]{0,2,1:T(8,128)(2,1)S(1)} %slice.528) | copy-start | bytes 2359300
  183.2 16.1 %copy-start.54 = (bf16[1,1,512,256]{2,3,1,0:T(8,128)(2,1)}, bf16[1,1,512,256]{2,3,1,0:T(8,128)(2,1)S(1)}, u32[]{:S(2)}) copy-start(bf16[1,1,512,256]{2,3,1,0:T(8,128)(2,1)S(1)} %get-tuple-element.289) | copy-start | bytes 786436
  183.4 13.4 %copy-start.36 = (bf16[1,1,512,256]{2,3,1,0:T(8,128)(2,1)}, bf16[1,1,512,256]{2,3,1,0:T(8,128)(2,1)S(1)}, u32[]{:S(2)}) copy-start(bf16[1,1,512,256]{2,3,1,0:T(8,128)(2,1)S(1)} %get-tuple-element.287) | copy-start | bytes 786436
  184.3 15.0 %copy-start.2 = (f32[4,512,512]{1,2,0:T(8,128)}, f32[4,512,512]{1,2,0:T(8,128)S(1)}, u32[]{:S(2)}) copy-start(f32[4,512,512]{1,2,0:T(8,128)S(1)} %get-tuple-element.300) | copy-start | bytes 12582916
  199.3 24.1 %copy-start = (f32[4,512,1536]{2,1,0:T(8,128)}, f32[4,512,1536]{2,1,0:T(8,128)S(1)}, u32[]{:S(2)}) copy-start(f32[4,512,1536]{2,1,0:T(8,128)S(1)} %get-tuple-element.296) | copy-start | bytes 37748740
  232.6 19.6 %copy-start.79 = (bf16[512]{0:T(512)(128)(2,1)S(1)}, bf16[512]{0:T(512)(128)(2,1)}, u32[]{:S(2)}) copy-start(bf16[512]{0:T(512)(128)(2,1)} %param.48) | copy-start | bytes 3076
  232.6 19.6 %copy-start.82 = (bf16[128]{0:T(256)(128)(2,1)S(1)}, bf16[128]{0:T(256)(128)(2,1)}, u32[]{:S(2)}) copy-start(bf16[128]{0:T(256)(128)(2,1)} %param.44) | copy-start | bytes 772
  232.7 29.3 %copy-start.83 = (bf16[128]{0:T(256)(128)(2,1)S(1)}, bf16[128]{0:T(256)(128)(2,1)}, u32[]{:S(2)}) copy-start(bf16[128]{0:T(256)(128)(2,1)} %param.45) | copy-start | bytes 772
  232.7 38.8 %copy-start.84 = (bf16[128]{0:T(256)(128)(2,1)S(1)}, bf16[128]{0:T(256)(128)(2,1)}, u32[]{:S(2)}) copy-start(bf16[128]{0:T(256)(128)(2,1)} %param.46) | copy-start | bytes 772
  247.9 45.8 %all-to-all-start.3 = ((bf16[4,2,65536]{2,1,0:T(2,128)(2,1)}), bf16[4,2,65536]{2,1,0:T(2,128)(2,1)}, u32[]{:S(2)}, u32[]{:S(2)}) async-start(bf16[4,2,65536]{2,1,0:T(2,128)(2,1)} %reshape.1605), calls=%async_computation.3 | async-start | bytes 2097152 | tf_op jit(solution)/shard_map/all_to_all | solution.py:243
  280.9 22.6 %copy-start.75 = (f32[8,1,128]{2,1,0:T(1,128)}, f32[8,1,128]{2,1,0:T(1,128)S(1)}, u32[]{:S(2)}) copy-start(f32[8,1,128]{2,1,0:T(1,128)S(1)} %convert_element_type.351) | copy-start | bytes 12292
  303.0 31.9 %copy-start.11 = (f32[512,1024]{1,0:T(8,128)}, f32[512,1024]{1,0:T(8,128)S(1)}, u32[]{:S(2)}) copy-start(f32[512,1024]{1,0:T(8,128)S(1)} %get-tuple-element.302) | copy-start | bytes 6291460
  303.5 10.7 %copy-start.13 = (bf16[1,512,1024]{2,1,0:T(8,128)(2,1)S(1)}, bf16[1,512,1024]{2,1,0:T(8,128)(2,1)}, u32[]{:S(2)}) copy-start(bf16[1,512,1024]{2,1,0:T(8,128)(2,1)} %param.51) | copy-start | bytes 3145732
  314.1 15.4 %copy-start.86 = (bf16[1024,4096]{1,0:T(8,128)(2,1)S(1)}, bf16[1024,4096]{1,0:T(8,128)(2,1)}, u32[]{:S(2)}) copy-start(bf16[1024,4096]{1,0:T(8,128)(2,1)} %all-gather.17.cloned.1.call-done) | copy-start | bytes 25165828
  351.6 18.2 %all-to-all-start.4 = ((bf16[4,2,65536]{2,1,0:T(2,128)(2,1)}), bf16[4,2,65536]{2,1,0:T(2,128)(2,1)S(1)}, u32[]{:S(2)}, u32[]{:S(2)}) async-start(bf16[4,2,65536]{2,1,0:T(2,128)(2,1)} %reshape.1607), calls=%async_computation.4 | async-start | bytes 2097152 | tf_op jit(solution)/shard_map/all_to_all | solution.py:278
  355.6 229.6 %reduce-scatter.7.cloned.1.call-start = ((), (), s32[]{:S(2)}) async-start(), calls=%async_computation.17 | async-start | bytes 2359296 | tf_op jit(solution)/shard_map/reduce_scatter | solution.py:331
  380.0 9.6 %slice-start.6 = ((s8[8388608]{0:T(1024)(128)(4,1)}), s8[4194304]{0:T(1024)(128)(4,1)S(1)}, s32[]{:S(2)}) async-start(s8[8388608]{0:T(1024)(128)(4,1)} %bitcast.257), calls=%async_computation.27 | async-start | bytes 8388608
  382.3 7.3 slice-start.7
  420.7 68.8 %all-to-all-start.7 = ((bf16[4,2,65536]{2,1,0:T(2,128)(2,1)}), bf16[4,2,65536]{2,1,0:T(2,128)(2,1)S(1)}, u32[]{:S(2)}, u32[]{:S(2)}) async-start(bf16[4,2,65536]{2,1,0:T(2,128)(2,1)} %reshape.1609), calls=%async_computation.7 | async-start | bytes 2097152 | tf_op jit(solution)/shard_map/all_to_all | solution.py:302
  425.8 13.1 %slice-start.3 = ((s8[12582912]{0:T(1024)(128)(4,1)}), s8[4194304]{0:T(1024)(128)(4,1)S(1)}, s32[]{:S(2)}) async-start(s8[12582912]{0:T(1024)(128)(4,1)} %bitcast.255), calls=%async_computation.24 | async-start | bytes 8388608
  425.8 9.8 %copy-start.18 = (bf16[1024,4,64]{0,2,1:T(8,128)(2,1)S(1)}, bf16[1024,4,64]{0,2,1:T(8,128)(2,1)}, u32[]{:S(2)}) copy-start(bf16[1024,4,64]{0,2,1:T(8,128)(2,1)} %copy-done.17) | copy-start | bytes 1572868
  425.8 9.8 %copy-start.53 = (bf16[1,1,512,256]{2,3,1,0:T(8,128)(2,1)S(1)}, bf16[1,1,512,256]{2,3,1,0:T(8,128)(2,1)}, u32[]{:S(2)}) copy-start(bf16[1,1,512,256]{2,3,1,0:T(8,128)(2,1)} %copy-done.52) | copy-start | bytes 786436
  425.8 13.0 %slice-start.4 = ((s8[12582912]{0:T(1024)(128)(4,1)}), s8[4194304]{0:T(1024)(128)(4,1)S(1)}, s32[]{:S(2)}) async-start(s8[12582912]{0:T(1024)(128)(4,1)} %bitcast.255), calls=%async_computation.25 | async-start | bytes 8388608
  425.8 14.3 %slice-start.5 = ((s8[12582912]{0:T(1024)(128)(4,1)}), s8[4194304]{0:T(1024)(128)(4,1)S(1)}, s32[]{:S(2)}) async-start(s8[12582912]{0:T(1024)(128)(4,1)} %bitcast.255), calls=%async_computation.26 | async-start | bytes 8388608
  438.8 10.1 %slice-start.8 = ((s8[8388608]{0:T(1024)(128)(4,1)}), s8[4194304]{0:T(1024)(128)(4,1)S(1)}, s32[]{:S(2)}) async-start(s8[8388608]{0:T(1024)(128)(4,1)} %bitcast.259), calls=%async_computation.29 | async-start | bytes 8388608
  440.1 8.8 slice-start.9
  456.5 22.0 %copy-start.57 = (bf16[1,1,512,256]{2,3,1,0:T(8,128)(2,1)S(1)}, bf16[1,1,512,256]{2,3,1,0:T(8,128)(2,1)}, u32[]{:S(2)}) copy-start(bf16[1,1,512,256]{2,3,1,0:T(8,128)(2,1)} %copy-done.56) | copy-start | bytes 786436
  478.6 8.6 slice-start.13
  489.5 7.9 copy-start.28
  489.5 23.3 %all-to-all-start.5 = ((bf16[4,2,65536]{2,1,0:T(2,128)(2,1)}), bf16[4,2,65536]{2,1,0:T(2,128)(2,1)}, u32[]{:S(2)}, u32[]{:S(2)}) async-start(bf16[4,2,65536]{2,1,0:T(2,128)(2,1)} %reshape.1613), calls=%async_computation.5 | async-start | bytes 2097152 | tf_op jit(solution)/shard_map/all_to_all | solution.py:296
  512.8 17.7 %all-to-all-start.6 = ((bf16[4,2,65536]{2,1,0:T(2,128)(2,1)}), bf16[4,2,65536]{2,1,0:T(2,128)(2,1)}, u32[]{:S(2)}, u32[]{:S(2)}) async-start(bf16[4,2,65536]{2,1,0:T(2,128)(2,1)} %reshape.1611), calls=%async_computation.6 | async-start | bytes 2097152 | tf_op jit(solution)/shard_map/all_to_all | solution.py:299
  517.0 96.3 %reduce-scatter.5.cloned.1.call-start = ((), (), s32[]{:S(2)}) async-start(), calls=%async_computation.16 | async-start | bytes 7077888 | tf_op jit(solution)/shard_map/reduce_scatter | solution.py:325
  525.4 10.8 %copy-start.16 = (bf16[1,2048,256]{2,1,0:T(8,128)(2,1)}, bf16[1,2048,256]{2,1,0:T(8,128)(2,1)S(1)}, u32[]{:S(2)}) copy-start(bf16[1,2048,256]{2,1,0:T(8,128)(2,1)S(1)} %copy.159) | copy-start | bytes 3145732
  526.8 11.0 %copy-start.8 = (bf16[1,512,1024]{2,1,0:T(8,128)(2,1)S(1)}, bf16[1,512,1024]{2,1,0:T(8,128)(2,1)}, u32[]{:S(2)}) copy-start(bf16[1,512,1024]{2,1,0:T(8,128)(2,1)} %param.36) | copy-start | bytes 3145732
  526.8 11.0 %copy-start.61 = (f32[8,1,128]{2,1,0:T(1,128)S(1)}, f32[8,1,128]{2,1,0:T(1,128)}, u32[]{:S(2)}) copy-start(f32[8,1,128]{2,1,0:T(1,128)} %copy-done.60) | copy-start | bytes 12292
  526.8 11.0 %copy-start.63 = (f32[512]{0:T(512)S(1)}, f32[512]{0:T(512)}, u32[]{:S(2)}) copy-start(f32[512]{0:T(512)} %copy-done.62) | copy-start | bytes 6148
  526.8 11.0 %copy-start.69 = (f32[512]{0:T(512)S(1)}, f32[512]{0:T(512)}, u32[]{:S(2)}) copy-start(f32[512]{0:T(512)} %copy-done.68) | copy-start | bytes 6148
  526.8 11.0 %copy-start.74 = (f32[8,1,128]{2,1,0:T(1,128)S(1)}, f32[8,1,128]{2,1,0:T(1,128)}, u32[]{:S(2)}) copy-start(f32[8,1,128]{2,1,0:T(1,128)} %copy-done.73) | copy-start | bytes 12292
  545.8 157.8 %reduce-scatter.11.cloned.1.call-start = ((), (), s32[]{:S(2)}) async-start(), calls=%async_computation.19 | async-start | bytes 9437184 | tf_op jit(solution)/shard_map/reduce_scatter | solution.py:349
  561.0 233.0 %reduce-scatter.9.cloned.1.call-start = ((), (), s32[]{:S(2)}) async-start(), calls=%async_computation.18 | async-start | bytes 9437184 | tf_op jit(solution)/shard_map/reduce_scatter | solution.py:343
  571.7 311.3 %all-reduce.15.cloned.1.call-start = ((), (), s32[]{:S(2)}) async-start(), calls=%async_computation.20 | async-start | bytes 6291456 | tf_op jit(solution)/shard_map/psum | solution.py:359
  808.9 7.5 copy-start.67
  808.9 9.8 %copy-start.70 = (bf16[1024]{0:T(1024)(128)(2,1)S(1)}, bf16[1024]{0:T(1024)(128)(2,1)}, u32[]{:S(2)}) copy-start(bf16[1024]{0:T(1024)(128)(2,1)} %get-tuple-element.270) | copy-start | bytes 6148
  808.9 9.8 %copy-start.71 = (bf16[4096]{0:T(1024)(128)(2,1)S(1)}, bf16[4096]{0:T(1024)(128)(2,1)}, u32[]{:S(2)}) copy-start(bf16[4096]{0:T(1024)(128)(2,1)} %get-tuple-element.313) | copy-start | bytes 24580
  809.0 9.8 %copy-start.77 = (bf16[1024]{0:T(1024)(128)(2,1)S(1)}, bf16[1024]{0:T(1024)(128)(2,1)}, u32[]{:S(2)}) copy-start(bf16[1024]{0:T(1024)(128)(2,1)} %get-tuple-element.241) | copy-start | bytes 6148
  809.0 9.7 %copy-start.78 = (bf16[1024]{0:T(1024)(128)(2,1)S(1)}, bf16[1024]{0:T(1024)(128)(2,1)}, u32[]{:S(2)}) copy-start(bf16[1024]{0:T(1024)(128)(2,1)} %get-tuple-element.245) | copy-start | bytes 6148
  809.0 51.5 %copy-start.65 = (f32[512]{0:T(512)S(1)}, f32[512]{0:T(512)}, u32[]{:S(2)}) copy-start(f32[512]{0:T(512)} %copy-done.64) | copy-start | bytes 6148
  816.4 44.1 %copy-start.10 = (f32[512,1024]{1,0:T(8,128)S(1)}, f32[512,1024]{1,0:T(8,128)}, u32[]{:S(2)}) copy-start(f32[512,1024]{1,0:T(8,128)} %copy-done.9) | copy-start | bytes 6291460
  (57 other events, 208.9 us)
Sparse Core Ops, SparseCore 0:
  9.7 67.5 all-gather.12
  78.8 27.7 all-gather.14
  108.2 81.4 all-gather.16
  191.1 80.5 all-gather.18
  358.6 35.1 reduce-scatter.6
  545.9 67.3 reduce-scatter.4
  615.6 87.9 reduce-scatter.10
  705.9 87.9 reduce-scatter.8
  797.3 85.6 all-reduce.14
where the time goes:
time: 909 us; the launch traced here: 898 us
  waiting for transfers between devices  274 us (30%)
  matrix products  169 us (19%)
  other arithmetic  153 us (17%)
  local copies, waits for them, and re-layouts  128 us (14%)
  blocking collectives  122 us (13%)
  starting transfers between devices  35 us (4%)
  between operations  18.5 us (2%)
    reduce_scatter x1, waiting for transfers between devices, body(): lax.psum_scatter(grad_w_fc.astype(jnp.bfloat16), 'fsdp', scatter_dimensio...  90.3 us
    reduce_scatter x1, waiting for transfers between devices, body(): lax.psum_scatter(grad_w_proj.astype(jnp.bfloat16), 'fsdp', scatter_dimens...  90.3 us
    unnamed x14, other arithmetic  76.7 us
    unnamed x246, local copies, waits for them, and re-layouts  72.6 us
    dot_general x4, matrix products, outer_sum(): lax.dot_general(left, right, (((0,), (0,)), ((), ())), preferred_element_...  33.8 us
    dot_general x4, matrix products, times_trans(): lax.dot_general(left, right, (((1,), (1,)), ((), ())), preferred_element_...  29.5 us
    all_gather x1, waiting for transfers between devices, body(): lax.all_gather(w_qkv, 'fsdp', axis=0, tiled=True)  28.8 us
    reduce_scatter x1, waiting for transfers between devices, body(): lax.psum_scatter(grad_w_qkv.astype(jnp.bfloat16), 'fsdp', scatter_dimensi...  28.1 us
  transfers between devices with their start and end apart: 17, of which 7 were waited for; matrix products, arithmetic and copies ran while one was open for 43% of the time, Pallas kernels for 0%

commit v1 on v0

v1 whole, which is shorter than its diff:
```python
import functools

import jax
import jax.numpy as jnp
from jax import lax
from jax.experimental import pallas as pl
from jax.experimental.pallas import tpu as pltpu
from jax.sharding import PartitionSpec as P

H = 16
HD = 64
PROMPT = 1024
CONTLEN = 512
CONTS = 2

EPS = 1e-05
GELU_C = 0.7978845608028654
GELU_A = 0.044715
NEG = -1e30
BF = jnp.bfloat16
F32 = jnp.float32


def swap(values, axis, bits):
    size = lax.axis_size(axis)
    return lax.ppermute(values, axis, [(i, i ^ bits) for i in range(size)])


def xor_take(values, index, axis):
    size = values.shape[axis]
    bit = 1
    while bit < size:
        parts = [lax.slice_in_dim(values, i, i + 1, axis=axis) for i in range(size)]
        flipped = jnp.concatenate([parts[i ^ bit] for i in range(size)], axis=axis)
        values = jnp.where((index & bit) != 0, flipped, values)
        bit *= 2
    return values


def xor_blocks(values, index, count, axis):
    width = values.shape[axis] // count
    return jnp.concatenate(
        [
            lax.dynamic_slice_in_dim(values, (i ^ index) * width, width, axis=axis)
            for i in range(count)
        ],
        axis=axis,
    )


def plane_gather(values):
    size = lax.axis_size("seq")
    if size != 4:
        return [values] + [swap(values, "seq", k) for k in range(1, size)]
    half = values.shape[0] // 2
    one = swap(values, "seq", 1)
    two = swap(values, "seq", 2)
    three = jnp.concatenate(
        [swap(two[:half], "seq", 1), swap(one[half:], "seq", 2)], axis=0
    )
    return [values, one, two, three]


def plane_scatter(blocks):
    size = lax.axis_size("seq")
    if size != 4:
        total = blocks[0].astype(F32)
        for k in range(1, size):
            total = total + swap(blocks[k].astype(BF), "seq", k).astype(F32)
        return total
    half = blocks[0].shape[0] // 2
    sent_x = jnp.concatenate([blocks[1][:half], blocks[3][:half]], axis=0).astype(BF)
    sent_y = jnp.concatenate([blocks[2][half:], blocks[3][half:]], axis=0).astype(BF)
    got_x = swap(sent_x, "seq", 1).astype(F32)
    got_y = swap(sent_y, "seq", 2).astype(F32)
    next_y = (blocks[2][:half].astype(F32) + got_x[half:]).astype(BF)
    next_x = (blocks[1][half:].astype(F32) + got_y[half:]).astype(BF)
    last_y = swap(next_y, "seq", 2).astype(F32)
    last_x = swap(next_x, "seq", 1).astype(F32)
    upper = blocks[0][:half].astype(F32) + got_x[:half] + last_y
    lower = blocks[0][half:].astype(F32) + got_y[:half] + last_x
    return jnp.concatenate([upper, lower], axis=0)


def tile_rows(total, blocks):
    return min(256, total // blocks)


def rel_row(tile, rows, block_rows, me):
    per = block_rows // rows
    return pl.multiple_of(((tile // per) ^ me) * block_rows + (tile % per) * rows, rows)


def walk(tile, rows):
    prompt_tiles = PROMPT // rows
    cont_tiles = CONTLEN // rows
    in_prompt = tile < prompt_tiles
    inside = lax.rem(jnp.maximum(tile - prompt_tiles, 0), cont_tiles)
    count = jnp.where(in_prompt, tile, prompt_tiles + inside)
    return count, tile - inside - prompt_tiles


def key_limit(lens, tile, rows):
    prompt_tiles = PROMPT // rows
    cont_tiles = CONTLEN // rows
    past = jnp.maximum(tile - prompt_tiles, 0)
    cont = jnp.minimum(past // cont_tiles, CONTS - 1)
    length = lens[1]
    for i in range(1, CONTS):
        length = jnp.where(cont == i, lens[1 + i], length)
    return jnp.where(
        tile < prompt_tiles, lens[0] - tile * rows, length - lax.rem(past, cont_tiles) * rows
    )


def pair_stack(block, per_pair, scale=None):
    if scale is not None:
        block = block * scale
    if per_pair == 1:
        return block
    lane = lax.broadcasted_iota(jnp.int32, block.shape, 1) // HD
    return jnp.concatenate(
        [jnp.where(lane == h, block, jnp.zeros_like(block)) for h in range(per_pair)], axis=0
    )


def diagonal_mask(rows, per_pair, limit):
    key = lax.broadcasted_iota(jnp.int32, (rows, per_pair * rows), 0)
    query = lax.broadcasted_iota(jnp.int32, (rows, per_pair * rows), 1) % rows
    return ((key <= query) & (key < limit)) | (key == query)


def live_mask(rows, per_pair, limit):
    return lax.broadcasted_iota(jnp.int32, (rows, per_pair * rows), 0) < limit


def nt(left, right):
    return lax.dot_general(left, right, (((1,), (1,)), ((), ())), preferred_element_type=F32)


def nn(left, right):
    return lax.dot_general(left, right, (((1,), (0,)), ((), ())), preferred_element_type=F32)


def unstack(values, per_pair, rows):
    if per_pair == 1:
        return values
    return jnp.concatenate(
        [values[h * HD : (h + 1) * HD, h * rows : (h + 1) * rows] for h in range(per_pair)], axis=0
    )


def forward_kernel(rows, block_rows, per_pair, lens, q_ref, k_ref, v_ref, out_ref, norm_ref, vt_ref):
    tile = pl.program_id(1)
    me = lens[1 + CONTS]
    tiles = q_ref.shape[0] // rows

    @pl.when(tile == 0)
    def _():
        def turn(i, carry):
            at = rel_row(i, rows, block_rows, me)
            vt_ref[i] = v_ref[pl.ds(at, rows), :].T
            return carry

        lax.fori_loop(0, tiles, turn, 0)

    at = rel_row(tile, rows, block_rows, me)
    query = pair_stack(q_ref[pl.ds(at, rows), :], per_pair, jnp.asarray(0.125, BF))

    def scores(i):
        return nt(k_ref[pl.ds(rel_row(i, rows, block_rows, me), rows), :], query)

    first = jnp.where(
        diagonal_mask(rows, per_pair, key_limit(lens, tile, rows)), scores(tile), NEG
    )
    top = jnp.max(first, axis=0, keepdims=True)
    weights = jnp.exp(first - top)
    denom = jnp.sum(weights, axis=0, keepdims=True)
    total = nn(vt_ref[tile], weights.astype(BF))
    count, shift = walk(tile, rows)

    def step(i, carry):
        top, denom, total = carry
        key_tile = jnp.where(i < PROMPT // rows, i, i + shift)
        part = jnp.where(
            live_mask(rows, per_pair, key_limit(lens, key_tile, rows)), scores(key_tile), NEG
        )
        higher = jnp.maximum(top, jnp.max(part, axis=0, keepdims=True))
        scale = jnp.exp(top - higher)
        weights = jnp.exp(part - higher)
        denom = denom * scale + jnp.sum(weights, axis=0, keepdims=True)
        total = total * scale + nn(vt_ref[key_tile], weights.astype(BF))
        return higher, denom, total

    top, denom, total = lax.fori_loop(0, count, step, (top, denom, total))
    mixed = unstack(total / denom, per_pair, rows)
    out_ref[...] = mixed.T.astype(BF)
    norm_ref[0, 0] = top + jnp.log(denom)


def backward_kernel(
    rows, block_rows, per_pair, lens, q_ref, k_ref, v_ref, out_ref, grad_ref, norm_ref,
    dq_ref, dk_ref, dv_ref, kt_ref, dk_sum, dv_sum, dq_sum,
):
    tile = pl.program_id(1)
    me = lens[1 + CONTS]
    tiles = q_ref.shape[0] // rows
    width = q_ref.shape[1]

    @pl.when(tile == 0)
    def _():
        def turn(i, carry):
            at = rel_row(i, rows, block_rows, me)
            kt_ref[i] = k_ref[pl.ds(at, rows), :].T
            return carry

        lax.fori_loop(0, tiles, turn, 0)
        dk_sum[...] = jnp.zeros_like(dk_sum)
        dv_sum[...] = jnp.zeros_like(dv_sum)

    at = rel_row(tile, rows, block_rows, me)
    query = pair_stack(q_ref[pl.ds(at, rows), :], per_pair, jnp.asarray(0.125, BF))
    grad_block = grad_ref[pl.ds(at, rows), :]
    grad = pair_stack(grad_block, per_pair)
    product = (grad_block.astype(F32) * out_ref[pl.ds(at, rows), :].astype(F32)).T
    inner = jnp.concatenate(
        [
            jnp.sum(product[h * HD : (h + 1) * HD], axis=0, keepdims=True)
            for h in range(per_pair)
        ],
        axis=1,
    )
    norm = norm_ref[0, 0]

    def one(key_tile, mask):
        key_at = rel_row(key_tile, rows, block_rows, me)
        keys = pl.ds(key_at, rows)
        part = jnp.where(mask, nt(k_ref[keys, :], query), NEG)
        probs = jnp.exp(part - norm)
        slope = probs * (nt(v_ref[keys, :], grad) - inner)
        slope_low = slope.astype(BF)
        dv_sum[keys, :] += nn(probs.astype(BF), grad)
        dk_sum[keys, :] += nn(slope_low, query)
        return nn(kt_ref[key_tile], slope_low)

    dq_sum[...] = one(tile, diagonal_mask(rows, per_pair, key_limit(lens, tile, rows)))
    count, shift = walk(tile, rows)

    def step(i, carry):
        key_tile = jnp.where(i < PROMPT // rows, i, i + shift)
        dq_sum[...] += one(key_tile, live_mask(rows, per_pair, key_limit(lens, key_tile, rows)))
        return carry

    lax.fori_loop(0, count, step, 0)
    dq_ref[...] = (unstack(dq_sum[...], per_pair, rows).T * 0.125).astype(BF)

    @pl.when(tile == tiles - 1)
    def _():
        dk_ref[...] = dk_sum[...].astype(BF)
        dv_ref[...] = dv_sum[...].astype(BF)


def attention_plan(total, heads):
    blocks = lax.axis_size("seq")
    rows = tile_rows(total, blocks)
    per_pair = 2 if heads % 2 == 0 else 1
    return rows, total // blocks, per_pair, heads // per_pair, per_pair * HD


def thirds(qkv, width, pair_width):
    if pair_width % 128 == 0:
        per = width // pair_width
        return (qkv, qkv, qkv), (0, per, 2 * per)
    return tuple(qkv[:, i * width : (i + 1) * width] for i in range(3)), (0, 0, 0)


def row_block(rows, block_rows):
    per = block_rows // rows

    def index(pair, tile, lens):
        return ((tile // per) ^ lens[1 + CONTS]) * per + tile % per, pair

    return index


def attend_forward(lens, qkv, heads):
    total = qkv.shape[0]
    width = heads * HD
    rows, block_rows, per_pair, pairs, pair_width = attention_plan(total, heads)
    arrays, firsts = thirds(qkv, width, pair_width)
    tiles = total // rows

    def whole(first):
        return pl.BlockSpec((total, pair_width), lambda pair, tile, lens: (0, first + pair))

    return pl.pallas_call(
        functools.partial(forward_kernel, rows, block_rows, per_pair),
        out_shape=(
            jax.ShapeDtypeStruct((total, width), BF),
            jax.ShapeDtypeStruct((pairs, tiles, 1, per_pair * rows), F32),
        ),
        grid_spec=pltpu.PrefetchScalarGridSpec(
            num_scalar_prefetch=1,
            grid=(pairs, tiles),
            in_specs=[whole(first) for first in firsts],
            out_specs=(
                pl.BlockSpec((rows, pair_width), row_block(rows, block_rows)),
                pl.BlockSpec(
                    (1, 1, 1, per_pair * rows), lambda pair, tile, lens: (pair, tile, 0, 0)
                ),
            ),
            scratch_shapes=[pltpu.VMEM((tiles, pair_width, rows), BF)],
        ),
        name="attend_forward",
    )(lens, *arrays)


def attend_backward(lens, qkv, mixed, grad, norm, heads):
    total = qkv.shape[0]
    width = heads * HD
    rows, block_rows, per_pair, pairs, pair_width = attention_plan(total, heads)
    arrays, firsts = thirds(qkv, width, pair_width)
    tiles = total // rows

    def whole(first):
        return pl.BlockSpec((total, pair_width), lambda pair, tile, lens: (0, first + pair))

    return pl.pallas_call(
        functools.partial(backward_kernel, rows, block_rows, per_pair),
        out_shape=(jax.ShapeDtypeStruct((total, width), BF),) * 3,
        grid_spec=pltpu.PrefetchScalarGridSpec(
            num_scalar_prefetch=1,
            grid=(pairs, tiles),
            in_specs=[whole(first) for first in firsts]
            + [
                whole(0),
                whole(0),
                pl.BlockSpec(
                    (1, 1, 1, per_pair * rows), lambda pair, tile, lens: (pair, tile, 0, 0)
                ),
            ],
            out_specs=(
                pl.BlockSpec((rows, pair_width), row_block(rows, block_rows)),
                whole(0),
                whole(0),
            ),
            scratch_shapes=[
                pltpu.VMEM((tiles, pair_width, rows), BF),
                pltpu.VMEM((total, pair_width), F32),
                pltpu.VMEM((total, pair_width), F32),
                pltpu.VMEM((pair_width, per_pair * rows), F32),
            ],
        ),
        name="attend_backward",
    )(lens, *arrays, mixed, grad, norm)


def norm_stats(values):
    center = values - jnp.mean(values, axis=-1, keepdims=True)
    spread = jnp.mean(center * center, axis=-1, keepdims=True)
    scale = lax.rsqrt(spread + EPS)
    return center * scale, scale


def norm_pull(unit, scale, slope):
    return scale * (
        slope
        - jnp.mean(slope, axis=-1, keepdims=True)
        - unit * jnp.mean(slope * unit, axis=-1, keepdims=True)
    )


def gelu_both(values):
    square = values * values
    bent = jnp.tanh(GELU_C * (values + GELU_A * square * values))
    value = 0.5 * values * (1.0 + bent)
    slope = 0.5 * (1.0 + bent) + 0.5 * values * (1.0 - bent * bent) * GELU_C * (
        1.0 + 3.0 * GELU_A * square
    )
    return value, slope


def tn(left, right):
    return lax.dot_general(left, right, (((0,), (0,)), ((), ())), preferred_element_type=F32)


def pick(values, index, axis):
    return lax.dynamic_index_in_dim(values, index, axis, keepdims=False)


def by_core(core, mine, other, axis):
    return jnp.where(
        core == 0, jnp.stack([mine, other], axis=axis), jnp.stack([other, mine], axis=axis)
    )


def body_general(
    tokens,
    prompt_lens,
    cont_lens,
    gain_one,
    shift_one,
    w_qkv,
    bias_qv,
    w_out,
    bias_out,
    gain_two,
    shift_two,
    w_fc,
    bias_fc,
    w_proj,
    bias_proj,
    cotangent,
):
    ns = lax.axis_size("seq")
    nf = lax.axis_size("fsdp")
    nz = nf // 2
    me = lax.axis_index("seq")
    owner = lax.axis_index("fsdp")
    floor = owner // 2
    core = owner % 2
    toks, width = tokens.shape[1:]
    hidden_all = w_fc.shape[1]
    own = width // nf
    heads = H // ns
    local = width // ns
    hw = hidden_all // (nf * ns)
    cols = nz * hw

    token_block = tokens[0]
    branch = cotangent[0]

    token_blocks = plane_gather(token_block)
    vectors = [gain_one, shift_one, bias_qv, bias_out, gain_two, shift_two, bias_fc, bias_proj]
    packed = jnp.concatenate([v.reshape(-1, own) for v in vectors], axis=0)
    lines = packed.shape[0]
    packed_rows = -(-packed.size // (3 * local))
    packed = jnp.pad(packed.reshape(-1), (0, 16 * (-(-packed_rows // 16)) * 3 * local - packed.size))
    mine_qkv = pick(w_qkv.reshape(own, 3, ns, local), me, 2).reshape(own, 3 * local)
    sent_qkv = jnp.concatenate([mine_qkv, packed.reshape(-1, 3 * local)], axis=0)
    got_qkv = jnp.stack([sent_qkv] + [swap(sent_qkv, "fsdp", 2 * k) for k in range(1, nz)])
    got_qkv = xor_take(by_core(core, got_qkv, swap(got_qkv, "fsdp", 1), 1), floor, 0)
    qkv_mat = got_qkv[:, :, :own].reshape(width, 3 * local)
    small = got_qkv[:, :, own:].reshape(nf, -1)[:, : lines * own].reshape(nf, lines, own)
    at = 0
    full = []
    for v in vectors:
        count = v.shape[0] // own
        full.append(small[:, at : at + count].reshape(-1).astype(F32))
        at += count
    gain_a, shift_a, qv_vec, out_vec, gain_b, shift_b, fc_vec, proj_vec = full

    fc_cut = w_fc.reshape(own, nz, 2, ns, hw)
    fc_mine = pick(fc_cut, core, 2)
    fc_other = swap(pick(fc_cut, 1 - core, 2).reshape(own, -1), "fsdp", 1)
    fc_rows = by_core(core, fc_mine.reshape(own, -1), fc_other, 0).reshape(2 * own, nz, ns, hw)
    fc_rows = xor_take(xor_take(fc_rows, floor, 1), me, 2)
    proj_rows = xor_take(w_proj.reshape(ns, hw, width), me, 0)
    out_cols = xor_take(w_out.reshape(own, ns, local), me, 1)
    proj_parts = width // cols
    out_parts = max(1, cols // local)

    def share(q, k):
        fc = jnp.concatenate([fc_rows[:, j ^ k, q] for j in range(nz)], axis=1)
        proj = [proj_rows[q][:, i * cols : (i + 1) * cols] for i in range(proj_parts)]
        out = out_cols[:, q]
        if out_parts > 1:
            step = own // out_parts
            out = jnp.concatenate([out[i * step : (i + 1) * step] for i in range(out_parts)], axis=1)
        return fc, proj, out

    def message(k):
        fc, proj, out = share(0, k)
        return jnp.concatenate([fc, *proj, out.reshape(-1, cols)], axis=0)

    got = [swap(message(k), "fsdp", 2 * k) for k in range(1, nz)]
    rows_each = got[0].shape[0]
    planes = plane_gather(jnp.concatenate(got, axis=0))

    def parts_of(q, k):
        if k == 0:
            fc, proj, out = share(q, 0)
            return fc, jnp.concatenate(proj, axis=1), out_cols[:, q]
        block = planes[q][(k - 1) * rows_each : k * rows_each]
        fc = block[: 2 * own]
        proj = jnp.concatenate(
            [block[2 * own + i * hw : 2 * own + (i + 1) * hw] for i in range(proj_parts)], axis=1
        )
        out = block[2 * own + proj_parts * hw :]
        if out_parts > 1:
            out = jnp.concatenate(
                [out[:, i * local : (i + 1) * local] for i in range(out_parts)], axis=0
            )
        else:
            out = out.reshape(own, local)
        return fc, proj, out

    pieces = [[parts_of(q, k) for k in range(nz)] for q in range(ns)]
    out_half = jnp.stack(
        [jnp.stack([pieces[q][k][2] for q in range(ns)], axis=1) for k in range(nz)]
    )
    out_half = xor_take(out_half, me, 2).reshape(nz, own, width)
    out_both = by_core(core, out_half, swap(out_half, "fsdp", 1), 1)
    out_mat = xor_take(out_both, floor, 0).reshape(ns, local, width)
    out_mat = xor_take(out_mat, me, 0).reshape(width, width)
    fc_mat = jnp.concatenate(
        [jnp.concatenate([pieces[q][k][0] for k in range(nz)], axis=0) for q in range(ns)], axis=1
    )
    proj_mat = jnp.concatenate([pieces[q][k][1] for q in range(ns) for k in range(nz)], axis=0)
    fc_bias = pick(fc_vec.reshape(nz, 2, ns, hw), core, 1)
    fc_bias = xor_take(xor_take(fc_bias, floor, 0), me, 1).transpose(1, 0, 2).reshape(-1)

    all_tokens = jnp.concatenate(token_blocks, axis=0).astype(F32)
    unit_all, _ = norm_stats(all_tokens)
    first = (unit_all * gain_a + shift_a).astype(BF)
    bias_all = jnp.concatenate(
        [
            pick(qv_vec.reshape(2, ns, local)[0], me, 0),
            jnp.zeros((local,), F32),
            pick(qv_vec.reshape(2, ns, local)[1], me, 0),
        ]
    )
    qkv = (jnp.dot(first, qkv_mat, preferred_element_type=F32) + bias_all).astype(BF)
    lens = jnp.concatenate([prompt_lens, cont_lens[0], me.reshape(1)]).astype(jnp.int32)
    mixed_heads, log_norm = attend_forward(lens, qkv, heads)

    def to_tokens(values):
        return jnp.concatenate(
            [values[:toks]]
            + [swap(values[k * toks : (k + 1) * toks], "seq", k) for k in range(1, ns)],
            axis=1,
        )

    def to_heads(values):
        return jnp.concatenate(
            [values[:, :local]]
            + [swap(values[:, k * local : (k + 1) * local], "seq", k) for k in range(1, ns)],
            axis=0,
        )

    mixed = to_tokens(mixed_heads)
    hidden = token_block.astype(F32) + jnp.dot(mixed, out_mat, preferred_element_type=F32) + out_vec
    unit_two, scale_two = norm_stats(hidden)
    second = (unit_two * gain_b + shift_b).astype(BF)

    second_both = jnp.concatenate([second, swap(second, "fsdp", 1)], axis=0)
    second_both = xor_blocks(second_both, floor, nz, 1)
    branch_both = jnp.concatenate([branch, swap(branch, "fsdp", 1)], axis=0)
    pre = jnp.dot(second_both, fc_mat, preferred_element_type=F32) + fc_bias
    act_full, bend = gelu_both(pre)
    act = act_full.astype(BF)
    grad_act = nt(branch_both, proj_mat)
    grad_pre = (grad_act * bend).astype(BF)
    grad_second_both = nt(grad_pre, fc_mat)
    grad_second = grad_second_both[:toks] + swap(
        grad_second_both[toks:].astype(BF), "fsdp", 1
    ).astype(F32)
    grad_second = xor_blocks(grad_second, floor, nz, 1)
    out_sum = jnp.dot(act, proj_mat, preferred_element_type=F32)
    result = hidden + out_sum[:toks] + proj_vec
    result = result + swap(out_sum[toks:].astype(BF), "fsdp", 1).astype(F32)
    output = result.astype(BF)[None]

    grad_hidden = branch.astype(F32) + norm_pull(unit_two, scale_two, grad_second * gain_b)
    grad_attn = grad_hidden.astype(BF)
    grad_mixed = nt(grad_attn, out_mat).astype(BF)
    grad_heads = to_heads(grad_mixed)

    grad_q, grad_k, grad_v = attend_backward(lens, qkv, mixed_heads, grad_heads, log_norm, heads)
    grad_qkv = jnp.concatenate([grad_q, grad_k, grad_v], axis=1)
    grad_first_part = nt(grad_qkv, qkv_mat).astype(BF)
    grad_first = plane_scatter(
        [grad_first_part[k * toks : (k + 1) * toks] for k in range(ns)]
    )
    unit_one, scale_one = norm_stats(token_block.astype(F32))
    input_grad = (grad_hidden + norm_pull(unit_one, scale_one, grad_first * gain_a))[None]

    span = nz * hw
    grad_fc = [tn(second_both, grad_pre[:, q * span : (q + 1) * span]).astype(BF) for q in range(ns)]
    grad_proj = [tn(act[:, q * span : (q + 1) * span], branch_both).astype(BF) for q in range(ns)]
    fc_sum = plane_scatter(grad_fc)
    proj_sum = plane_scatter(grad_proj)

    def fc_for(k):
        block = fc_sum[k * 2 * own : (k + 1) * 2 * own].reshape(2 * own, nz, hw)
        return jnp.concatenate([block[:, j ^ k] for j in range(nz)], axis=1)

    def proj_for(k):
        block = proj_sum[k * hw : (k + 1) * hw]
        return jnp.concatenate(
            [block[:, i * span : (i + 1) * span] for i in range(proj_parts)], axis=0
        )

    both_sum = jnp.concatenate([fc_for(0), proj_for(0)], axis=0)
    for k in range(1, nz):
        sent = jnp.concatenate([fc_for(k), proj_for(k)], axis=0).astype(BF)
        both_sum = both_sum + swap(sent, "fsdp", 2 * k).astype(F32)
    fc_owned = both_sum[: 2 * own].reshape(2, own, span)
    fc_kept = pick(fc_owned, core, 0).astype(BF)
    fc_moved = swap(pick(fc_owned, 1 - core, 0).astype(BF), "fsdp", 1)
    final = jnp.concatenate([fc_kept, fc_moved, both_sum[2 * own :].astype(BF)], axis=0)
    finals = plane_gather(final)
    fc_kept_all = jnp.stack([v[:own].reshape(own, nz, hw) for v in finals], axis=2)
    fc_moved_all = jnp.stack([v[own : 2 * own].reshape(own, nz, hw) for v in finals], axis=2)
    grad_w_fc = by_core(core, fc_kept_all, fc_moved_all, 2)
    grad_w_fc = xor_take(xor_take(grad_w_fc, floor, 1), me, 3).reshape(own, hidden_all).astype(F32)
    grad_w_proj = jnp.stack(
        [
            jnp.concatenate(
                [v[2 * own + i * hw : 2 * own + (i + 1) * hw] for i in range(proj_parts)], axis=1
            )
            for v in finals
        ]
    )
    grad_w_proj = xor_take(grad_w_proj, me, 0).reshape(ns * hw, width).astype(F32)

    grad_out = tn(mixed, grad_attn).astype(BF).reshape(ns, local, width)
    grad_out = xor_take(grad_out, me, 0).reshape(nz, 2, own, width)
    grad_out = xor_take(grad_out, floor, 0)
    out_kept = pick(grad_out, core, 1).astype(F32) + swap(
        pick(grad_out, 1 - core, 1), "fsdp", 1
    ).astype(F32)
    out_owned = out_kept[0]
    for k in range(1, nz):
        out_owned = out_owned + swap(out_kept[k].astype(BF), "fsdp", 2 * k).astype(F32)
    bit = 1
    while bit < ns:
        out_owned = out_owned + swap(out_owned.astype(BF), "seq", bit).astype(F32)
        bit *= 2
    grad_w_out = out_owned

    grad_in = tn(first, grad_qkv).astype(BF).reshape(nz, 2, own, 3 * local)
    grad_in = xor_take(grad_in, floor, 0)
    in_kept = pick(grad_in, core, 1).astype(F32) + swap(
        pick(grad_in, 1 - core, 1), "fsdp", 1
    ).astype(F32)
    in_owned = in_kept[0]
    for k in range(1, nz):
        in_owned = in_owned + swap(in_kept[k].astype(BF), "fsdp", 2 * k).astype(F32)
    in_owned = in_owned.astype(BF)
    in_blocks = jnp.stack(
        [in_owned.reshape(own, 3, local)]
        + [swap(in_owned, "seq", k).reshape(own, 3, local) for k in range(1, ns)],
        axis=2,
    )
    grad_w_qkv = xor_take(in_blocks, me, 2).reshape(own, 3 * width).astype(F32)

    def placed(values, parts):
        slots = jnp.arange(parts)[:, None] == me
        return jnp.where(slots, values[None, :], 0.0).reshape(-1)

    part_f32 = grad_first_part.astype(F32)
    fc_bias_grad = jnp.sum(grad_pre.astype(F32), axis=0).reshape(ns, nz, hw).transpose(1, 0, 2)
    fc_bias_grad = xor_take(xor_take(fc_bias_grad, floor, 0), me, 1)
    fc_bias_grad = jnp.where(
        (jnp.arange(2) == core)[None, :, None, None], fc_bias_grad[:, None], 0.0
    ).reshape(-1)
    vector_grads = [
        jnp.sum(part_f32 * unit_all, axis=0),
        jnp.sum(part_f32, axis=0),
        placed(jnp.sum(grad_q.astype(F32), axis=0), ns),
        placed(jnp.sum(grad_v.astype(F32), axis=0), ns),
        jnp.sum(grad_attn.astype(F32), axis=0),
        jnp.sum(grad_second * unit_two, axis=0),
        jnp.sum(grad_second, axis=0),
        fc_bias_grad,
        jnp.sum(branch.astype(F32), axis=0),
    ]
    vector_sum = jnp.concatenate([v.reshape(-1, width) for v in vector_grads], axis=0)
    for axis, size in (("seq", ns), ("fsdp", nf)):
        bit = 1
        while bit < size:
            vector_sum = vector_sum + swap(vector_sum, axis, bit)
            bit *= 2
    vector_sum = vector_sum.reshape(-1)
    outs = []
    at = 0
    for v in vectors:
        count = v.shape[0]
        outs.append(lax.dynamic_slice_in_dim(vector_sum, at + owner * count, count))
        at += nf * count
    (g_gain_one, g_shift_one, g_bias_qv, g_bias_out, g_gain_two, g_shift_two, g_bias_fc, g_bias_proj) = outs

    return (
        output,
        input_grad,
        g_gain_one,
        g_shift_one,
        grad_w_qkv,
        g_bias_qv,
        grad_w_out,
        g_bias_out,
        g_gain_two,
        g_shift_two,
        grad_w_fc,
        g_bias_fc,
        grad_w_proj,
        g_bias_proj,
    )


UPPER = (0, 2, 1, 3)


def hidden_at(q, half, size):
    return half * 4 * size + (UPPER[q] if half == 0 else q) * size


def start_all(copies, sems):
    made = [
        pltpu.make_async_copy(source, target, sems.at[i]) for i, (source, target) in enumerate(copies)
    ]
    for copy in made:
        copy.start()
    return made


def aligned(value, size):
    return pl.multiple_of(value, size)


def pack_kernel(hw, place, fc_ref, proj_ref, mine_ref, other_ref, share_ref):
    me, core = place[0], place[2]
    for q in range(4):
        for z in range(4):
            target = hidden_at(q, z // 2, 2 * hw) + (z % 2) * hw
            for out_ref, which in ((mine_ref, core), (other_ref, 1 - core)):
                source = aligned(z * 8 * hw + which * 4 * hw + (me ^ q) * hw, hw)
                out_ref[:, target : target + hw] = fc_ref[:, pl.ds(source, hw)]
    share_ref[...] = proj_ref[...]


def pack(place, w_fc, w_proj):
    own, hidden_all = w_fc.shape
    hw, width = w_proj.shape[0] // 4, w_proj.shape[1]

    def whole(shape):
        return pl.BlockSpec(shape, lambda i, place: (0, 0))

    half = jax.ShapeDtypeStruct((own, hidden_all // 2), BF)
    return pl.pallas_call(
        functools.partial(pack_kernel, hw),
        out_shape=(half, half, jax.ShapeDtypeStruct((hw, width), BF)),
        grid_spec=pltpu.PrefetchScalarGridSpec(
            num_scalar_prefetch=1,
            grid=(1,),
            in_specs=[
                whole((own, hidden_all)),
                pl.BlockSpec((hw, width), lambda i, place: (place[0], 0)),
            ],
            out_specs=(whole(half.shape), whole(half.shape), whole((hw, width))),
        ),
        name="pack_shares",
    )(place, w_fc, w_proj)


def join_kernel(place, m0, m1, o0, o1, out_ref):
    core = place[2]
    own, chunk = m0.shape
    for refs, which in (((m0, m1), core), ((o0, o1), 1 - core)):
        rows = pl.ds(aligned(which * own, own), own)
        for half in range(2):
            out_ref[rows, half * chunk : (half + 1) * chunk] = refs[half][...]


def join(place, mine, other):
    own, hidden = mine.shape
    chunk = hidden // 8
    pieces = [
        pl.BlockSpec((own, chunk), lambda i, place, at=hidden_at(0, half, 1): (0, at))
        for half in range(2)
    ]
    return pl.pallas_call(
        join_kernel,
        out_shape=jax.ShapeDtypeStruct((2 * own, hidden // 4), BF),
        grid_spec=pltpu.PrefetchScalarGridSpec(
            num_scalar_prefetch=1,
            grid=(1,),
            in_specs=pieces * 2,
            out_specs=pl.BlockSpec((2 * own, hidden // 4), lambda i, place: (0, 0)),
        ),
        name="join_rows",
    )(place, mine, mine, other, other)


def project_kernel(
    place, own_ref, one_ref, two_ref, up_ref, low_ref, kept_ref, moved_ref, gain_ref, shift_ref,
    bias_ref, first_ref, unit_ref, qkv_ref, toks, mat, sems,
):
    step = pl.program_id(0)
    floor, core = place[1], place[2]
    block = own_ref.shape[0]
    half = block // 2
    own = mat.shape[0] // 8

    def copies():
        made = [
            (own_ref, toks.at[pl.ds(0, block), :]),
            (one_ref, toks.at[pl.ds(block, block), :]),
            (two_ref, toks.at[pl.ds(2 * block, block), :]),
            (up_ref, toks.at[pl.ds(3 * block, half), :]),
            (low_ref, toks.at[pl.ds(3 * block + half, half), :]),
        ]
        for k in range(4):
            for ref, which in ((kept_ref, core), (moved_ref, 1 - core)):
                row = aligned((floor ^ k) * 2 * own + which * own, own)
                made.append((ref.at[k, pl.ds(0, own), :], mat.at[pl.ds(row, own), :]))
        return made

    @pl.when(step == 0)
    def _():
        for copy in start_all(copies(), sems):
            copy.wait()

    rows = first_ref.shape[0]
    values = toks[pl.ds(aligned(step * rows, rows), rows), :].astype(F32)
    unit, _ = norm_stats(values)
    first = (unit * gain_ref[...] + shift_ref[...]).astype(BF)
    first_ref[...] = first
    unit_ref[...] = unit.astype(BF)
    qkv_ref[...] = (nn(first, mat[...]) + bias_ref[...]).astype(BF)


def project(place, blocks, kept, moved, gain, shift, bias):
    block, width = blocks[0].shape
    outs = kept.shape[2]
    total = 4 * block
    rows = 256
    raw = pl.BlockSpec(memory_space=pl.ANY)

    def line(size):
        return pl.BlockSpec((1, size), lambda i, place: (0, 0))

    def tile(size):
        return pl.BlockSpec((rows, size), lambda i, place: (i, 0))

    return pl.pallas_call(
        project_kernel,
        out_shape=(
            jax.ShapeDtypeStruct((total, width), BF),
            jax.ShapeDtypeStruct((total, width), BF),
            jax.ShapeDtypeStruct((total, outs), BF),
        ),
        grid_spec=pltpu.PrefetchScalarGridSpec(
            num_scalar_prefetch=1,
            grid=(total // rows,),
            in_specs=[raw] * 7 + [line(width), line(width), line(outs)],
            out_specs=(tile(width), tile(width), tile(outs)),
            scratch_shapes=[
                pltpu.VMEM((total, width), BF),
                pltpu.VMEM((width, outs), BF),
                pltpu.SemaphoreType.DMA((13,)),
            ],
        ),
        name="project",
    )(place, *blocks, kept, moved, gain, shift, bias)


def attn_out_kernel(
    place, m0, m1, m2, m3, kept_ref, moved_ref, token_ref, bias_ref, gain_ref, shift_ref,
    hidden_ref, second_ref, mixed_ref, mat_ref, mixed, sems,
):
    step = pl.program_id(0)
    me, floor, core = place[0], place[1], place[2]
    local = m1.shape[1]
    own = mat_ref.shape[0] // 8
    block = m1.shape[0]

    @pl.when(step == 0)
    def _():
        made = []
        for k, ref in enumerate((m0, m1, m2, m3)):
            lanes = pl.ds(aligned((me ^ k) * local, local), local)
            made.append((ref.at[pl.ds(0, block), :], mixed.at[:, lanes]))
        for k in range(4):
            for ref, which in ((kept_ref, core), (moved_ref, 1 - core)):
                row = aligned((floor ^ k) * 2 * own + which * own, own)
                made.append((ref.at[k], mat_ref.at[pl.ds(row, own), :]))
        for copy in start_all(made, sems):
            copy.wait()

    rows = hidden_ref.shape[0]
    here = mixed[pl.ds(aligned(step * rows, rows), rows), :]
    mixed_ref[...] = here
    hidden = token_ref[...].astype(F32) + nn(here, mat_ref[...]) + bias_ref[...]
    hidden_ref[...] = hidden
    unit, _ = norm_stats(hidden)
    second_ref[...] = (unit * gain_ref[...] + shift_ref[...]).astype(BF)


def attn_out(place, mixed, kept, moved, tokens, bias, gain, shift):
    block, width = tokens.shape
    rows = 256
    raw = pl.BlockSpec(memory_space=pl.ANY)
    line = pl.BlockSpec((1, width), lambda i, place: (0, 0))
    tile = pl.BlockSpec((rows, width), lambda i, place: (i, 0))
    return pl.pallas_call(
        attn_out_kernel,
        out_shape=(
            jax.ShapeDtypeStruct((block, width), F32),
            jax.ShapeDtypeStruct((block, width), BF),
            jax.ShapeDtypeStruct((block, width), BF),
            jax.ShapeDtypeStruct((width, width), BF),
        ),
        grid_spec=pltpu.PrefetchScalarGridSpec(
            num_scalar_prefetch=1,
            grid=(block // rows,),
            in_specs=[raw] * 6 + [tile, line, line, line],
            out_specs=(tile, tile, tile, pl.BlockSpec((width, width), lambda i, place: (0, 0))),
            scratch_shapes=[pltpu.VMEM((block, width), BF), pltpu.SemaphoreType.DMA((12,))],
        ),
        name="attn_out",
    )(place, *mixed, kept, moved, tokens, bias, gain, shift)


def feed_kernel(
    hw, place, second_ref, branch_ref, bias_ref, mine_ref, other_ref, a0, a1, a2, a3, proj_ref,
    b0, b1, b2, b3, act_ref, slope_ref, out_own, out_oth, back_own, back_oth, colsum_ref,
    fc, proj, sems,
):
    step = pl.program_id(0)
    me, floor, core = place[0], place[1], place[2]
    own = mine_ref.shape[0]
    chunk = 2 * hw
    steps = pl.num_programs(0)

    @pl.when(step == 0)
    def _():
        made = []
        for ref, which in ((mine_ref, core), (other_ref, 1 - core)):
            row = aligned(floor * 2 * own + which * own, own)
            made.append((ref, fc.at[pl.ds(row, own), :]))
        for q, ref in enumerate((a0, a1, a2, a3)):
            for k in range(1, 4):
                row = aligned((floor ^ k) * 2 * own, 2 * own)
                for half in range(2):
                    made.append(
                        (
                            ref.at[pl.ds((k - 1) * 2 * own, 2 * own), pl.ds(half * chunk, chunk)],
                            fc.at[pl.ds(row, 2 * own), pl.ds(hidden_at(q, half, chunk), chunk)],
                        )
                    )
        for q, ref in enumerate((b0, b1, b2, b3)):
            for k in range(4):
                z = floor ^ k
                row = jnp.where(z < 2, hidden_at(q, 0, chunk), hidden_at(q, 1, chunk)) + (z % 2) * hw
                if k == 0:
                    source = proj_ref.at[pl.ds(aligned((me ^ q) * hw, hw), hw), :]
                else:
                    source = ref.at[pl.ds((k - 1) * hw, hw), :]
                made.append((source, proj.at[pl.ds(aligned(row, hw), hw), :]))
        for copy in start_all(made, sems):
            copy.wait()

    second = second_ref[...]
    branch = branch_ref[...]
    total = None
    back = None
    span = 4 * hw
    for q in range(fc.shape[1] // span):
        here = pl.ds(q * span, span)
        pre = nn(second, fc[:, here]) + bias_ref[:, here]
        value, bend = gelu_both(pre)
        act = value.astype(BF)
        act_ref[:, here] = act
        slope_full = nt(branch, proj[here, :]) * bend
        slope = slope_full.astype(BF)
        slope_ref[:, here] = slope
        partial = jnp.sum(slope_full, axis=0, keepdims=True)

        @pl.when(step == 0)
        def _():
            colsum_ref[:, here] = partial

        @pl.when(step > 0)
        def _():
            colsum_ref[:, here] += partial

        more = nn(act, proj[here, :])
        total = more if total is None else total + more
        more = nt(slope, fc[:, here])
        back = more if back is None else back + more

    @pl.when(step < steps // 2)
    def _():
        out_oth[...] = total.astype(BF)
        back_oth[...] = back.astype(BF)

    @pl.when(step >= steps // 2)
    def _():
        out_own[...] = total
        back_own[...] = back


def feed(place, second, branch, bias, mine, other, shares, w_proj, proj_shares):
    both, width = second.shape
    hidden = mine.shape[1]
    hw = hidden // 16
    rows = 256
    steps = both // rows
    half = steps // 2
    raw = pl.BlockSpec(memory_space=pl.ANY)

    def tile(size):
        return pl.BlockSpec((rows, size), lambda i, place: (i, 0))

    line = pl.BlockSpec((1, hidden), lambda i, place: (0, 0))
    early = pl.BlockSpec((rows, width), lambda i, place: (jnp.minimum(i, half - 1), 0))
    late = pl.BlockSpec((rows, width), lambda i, place: (jnp.maximum(i - half, 0), 0))
    return pl.pallas_call(
        functools.partial(feed_kernel, hw),
        out_shape=(
            jax.ShapeDtypeStruct((both, hidden), BF),
            jax.ShapeDtypeStruct((both, hidden), BF),
            jax.ShapeDtypeStruct((both // 2, width), F32),
            jax.ShapeDtypeStruct((both // 2, width), BF),
            jax.ShapeDtypeStruct((both // 2, width), F32),
            jax.ShapeDtypeStruct((both // 2, width), BF),
            jax.ShapeDtypeStruct((1, hidden), F32),
        ),
        grid_spec=pltpu.PrefetchScalarGridSpec(
            num_scalar_prefetch=1,
            grid=(steps,),
            in_specs=[tile(width), tile(width), line] + [raw] * 11,
            out_specs=(tile(hidden), tile(hidden), late, early, late, early, line),
            scratch_shapes=[
                pltpu.VMEM((width, hidden), BF),
                pltpu.VMEM((hidden, width), BF),
                pltpu.SemaphoreType.DMA((42,)),
            ],
        ),
        name="feed",
    )(place, second, branch, bias, mine, other, *shares, w_proj, *proj_shares)


def mixed_back_kernel(
    place, own_ref, oth_ref, hidden_ref, branch_ref, gain_ref, mat_ref,
    full_ref, low_ref, g0, g1, g2, g3, sums_ref,
):
    step = pl.program_id(0)
    me = place[0]
    local = g0.shape[1]
    slope = own_ref[...] + oth_ref[...].astype(F32)
    unit, scale = norm_stats(hidden_ref[...])
    full = branch_ref[...].astype(F32) + norm_pull(unit, scale, slope * gain_ref[...])
    low = full.astype(BF)
    full_ref[...] = full
    low_ref[...] = low
    for k, ref in enumerate((g0, g1, g2, g3)):
        rows = pl.ds(aligned((me ^ k) * local, local), local)
        ref[...] = nt(low, mat_ref[rows, :]).astype(BF)
    sums = jnp.concatenate(
        [
            jnp.sum(low.astype(F32), axis=0, keepdims=True),
            jnp.sum(slope * unit, axis=0, keepdims=True),
            jnp.sum(slope, axis=0, keepdims=True),
            jnp.sum(branch_ref[...].astype(F32), axis=0, keepdims=True),
        ],
        axis=0,
    )

    @pl.when(step == 0)
    def _():
        sums_ref[...] = sums

    @pl.when(step > 0)
    def _():
        sums_ref[...] += sums


def mixed_back(place, own, oth, hidden, branch, gain, mat):
    block, width = own.shape
    local = width // 4
    rows = 256

    def tile(size):
        return pl.BlockSpec((rows, size), lambda i, place: (i, 0))

    def whole(height):
        return pl.BlockSpec((height, width), lambda i, place: (0, 0))

    return pl.pallas_call(
        mixed_back_kernel,
        out_shape=(
            jax.ShapeDtypeStruct((block, width), F32),
            jax.ShapeDtypeStruct((block, width), BF),
        )
        + (jax.ShapeDtypeStruct((block, local), BF),) * 4
        + (jax.ShapeDtypeStruct((4, width), F32),),
        grid_spec=pltpu.PrefetchScalarGridSpec(
            num_scalar_prefetch=1,
            grid=(block // rows,),
            in_specs=[tile(width)] * 4 + [whole(1), whole(width)],
            out_specs=(tile(width), tile(width)) + (tile(local),) * 4 + (whole(4),),
        ),
        name="mixed_back",
    )(place, own, oth, hidden, branch, gain, mat)


def first_back_kernel(tiles, place, grad_ref, unit_ref, mat_ref, *refs):
    step = pl.program_id(0)
    count = len(tiles)
    out_refs, sums_ref = refs[:count], refs[count]
    part = nt(grad_ref[...], mat_ref[...])
    low = part.astype(BF)
    for i in range(count):

        @pl.when(step == i)
        def _():
            out_refs[i][...] = low

    sums = jnp.concatenate(
        [
            jnp.sum(part * unit_ref[...].astype(F32), axis=0, keepdims=True),
            jnp.sum(part, axis=0, keepdims=True),
        ],
        axis=0,
    )

    @pl.when(step == 0)
    def _():
        sums_ref[...] = sums

    @pl.when(step > 0)
    def _():
        sums_ref[...] += sums


def first_back(tiles, groups, grad, unit, mat):
    total, outs = grad.shape
    width = mat.shape[0]
    rows = 256
    table = jnp.asarray(tiles, jnp.int32)
    del groups

    def at(i, place):
        return (place[i], 0)

    return pl.pallas_call(
        functools.partial(first_back_kernel, tiles),
        out_shape=tuple(jax.ShapeDtypeStruct((rows, width), BF) for _ in tiles)
        + (jax.ShapeDtypeStruct((2, width), F32),),
        grid_spec=pltpu.PrefetchScalarGridSpec(
            num_scalar_prefetch=1,
            grid=(len(tiles),),
            in_specs=[
                pl.BlockSpec((rows, outs), at),
                pl.BlockSpec((rows, width), at),
                pl.BlockSpec((width, outs), lambda i, place: (0, 0)),
            ],
            out_specs=tuple(pl.BlockSpec((rows, width), lambda i, place: (0, 0)) for _ in tiles)
            + (pl.BlockSpec((2, width), lambda i, place: (0, 0)),),
        ),
        name="first_back",
    )(table, grad, unit, mat)


def gather_sum_kernel(place, *refs):
    floor = place[1]
    fa, xa, la, fb, yb, lb, pa, xp, lpa, pb, yp, lpb, o0, o1, o2, o3, fc, proj = refs
    chunk = fc.shape[1] // 2
    hw = chunk // 2
    fc[:, :chunk] = fa[...].astype(F32) + xa[...].astype(F32) + la[...].astype(F32)
    fc[:, chunk:] = fb[...].astype(F32) + yb[...].astype(F32) + lb[...].astype(F32)
    proj[:chunk, :] = pa[...].astype(F32) + xp[...].astype(F32) + lpa[...].astype(F32)
    proj[chunk:, :] = pb[...].astype(F32) + yp[...].astype(F32) + lpb[...].astype(F32)
    rows = fc.shape[0] // 4
    for k, out in enumerate((o0, o1, o2, o3)):
        out[:rows, :] = fc[pl.ds(aligned((floor ^ k) * rows, rows), rows), :].astype(BF)
        piece = proj[pl.ds(aligned((floor ^ k) * hw, hw), hw), :].astype(BF)
        out[rows : rows + hw, :] = piece[:, : 2 * chunk]
        out[rows + hw :, :] = piece[:, 2 * chunk :]


def gather_sum(place, fc_parts, proj_parts):
    width = fc_parts[0].shape[0]
    chunk = width // 4
    fc_spec = pl.BlockSpec((width, chunk), lambda i, place: (0, 0))
    proj_spec = pl.BlockSpec((chunk, width), lambda i, place: (0, 0))
    out = jax.ShapeDtypeStruct((width // 2, 2 * chunk), BF)
    return pl.pallas_call(
        gather_sum_kernel,
        out_shape=(out,) * 4,
        grid_spec=pltpu.PrefetchScalarGridSpec(
            num_scalar_prefetch=1,
            grid=(1,),
            in_specs=[fc_spec] * 6 + [proj_spec] * 6,
            out_specs=(pl.BlockSpec(out.shape, lambda i, place: (0, 0)),) * 4,
            scratch_shapes=[pltpu.VMEM((width, 2 * chunk), F32), pltpu.VMEM((2 * chunk, width), F32)],
        ),
        name="gather_sum",
    )(place, *fc_parts, *proj_parts)


def floor_sum_kernel(place, r0, r1, r2, r3, kept_ref, sent_ref, total):
    core = place[2]
    total[...] = (
        r0[...].astype(F32) + r1[...].astype(F32) + r2[...].astype(F32) + r3[...].astype(F32)
    )
    own = sent_ref.shape[0]
    sent_ref[...] = total[pl.ds(aligned((1 - core) * own, own), own), :].astype(BF)
    kept_ref[:own, :] = total[pl.ds(aligned(core * own, own), own), :].astype(BF)
    kept_ref[own:, :] = total[2 * own :, :].astype(BF)


def floor_sum(place, parts):
    rows, cols = parts[0].shape
    own = rows // 4

    def whole(height):
        return pl.BlockSpec((height, cols), lambda i, place: (0, 0))

    return pl.pallas_call(
        floor_sum_kernel,
        out_shape=(
            jax.ShapeDtypeStruct((3 * own, cols), BF),
            jax.ShapeDtypeStruct((own, cols), BF),
        ),
        grid_spec=pltpu.PrefetchScalarGridSpec(
            num_scalar_prefetch=1,
            grid=(1,),
            in_specs=[whole(rows)] * 4,
            out_specs=(whole(3 * own), whole(own)),
            scratch_shapes=[pltpu.VMEM((rows, cols), F32)],
        ),
        name="floor_sum",
    )(place, *parts)


def spread_kernel(place, *refs):
    me, core = place[0], place[2]
    kept, moved, (fc_ref, proj_ref) = refs[:4], refs[4:8], refs[8:]
    own = moved[0].shape[0]
    hw = moved[0].shape[1] // 4
    for q in range(4):
        for ref, which in ((kept[q], core), (moved[q], 1 - core)):
            for z in range(4):
                lanes = pl.ds(aligned(z * 8 * hw + which * 4 * hw + (me ^ q) * hw, hw), hw)
                fc_ref[:, lanes] = ref[:own, z * hw : (z + 1) * hw].astype(F32)
        rows = pl.ds(aligned((me ^ q) * hw, hw), hw)
        proj_ref[rows, : 4 * hw] = kept[q][own : own + hw, :].astype(F32)
        proj_ref[rows, 4 * hw :] = kept[q][own + hw :, :].astype(F32)


def spread(place, kept, moved):
    own, cols = moved[0].shape
    hw = cols // 4

    def whole(shape):
        return pl.BlockSpec(shape, lambda i, place: (0, 0))

    fc_shape, proj_shape = (own, 32 * hw), (4 * hw, 8 * hw)
    return pl.pallas_call(
        spread_kernel,
        out_shape=(jax.ShapeDtypeStruct(fc_shape, F32), jax.ShapeDtypeStruct(proj_shape, F32)),
        grid_spec=pltpu.PrefetchScalarGridSpec(
            num_scalar_prefetch=1,
            grid=(1,),
            in_specs=[whole(kept[0].shape)] * 4 + [whole(moved[0].shape)] * 4,
            out_specs=(whole(fc_shape), whole(proj_shape)),
        ),
        name="spread",
    )(place, *kept, *moved)


def last_kernel(keep_ref, got_ref, last_ref, token_ref, hidden_ref, gain_ref, out_ref):
    slope = keep_ref[...].astype(F32) + got_ref[...].astype(F32) + last_ref[...].astype(F32)
    unit, scale = norm_stats(token_ref[...].astype(F32))
    out_ref[...] = hidden_ref[...] + norm_pull(unit, scale, slope * gain_ref[...])


def body_aligned(
    tokens,
    prompt_lens,
    cont_lens,
    gain_one,
    shift_one,
    w_qkv,
    bias_qv,
    w_out,
    bias_out,
    gain_two,
    shift_two,
    w_fc,
    bias_fc,
    w_proj,
    bias_proj,
    cotangent,
):
    ns = nz = 4
    nf = 8
    me = lax.axis_index("seq")
    owner = lax.axis_index("fsdp")
    floor = owner // 2
    core = owner % 2
    place = jnp.stack([me, floor, core]).astype(jnp.int32)
    toks, width = tokens.shape[1:]
    own = width // nf
    heads = H // ns
    local = width // ns
    hw = w_fc.shape[1] // (nf * ns)
    token_block = tokens[0]
    branch = cotangent[0]

    half = toks // 2
    tok_one = swap(token_block, "seq", 1)
    tok_two = swap(token_block, "seq", 2)
    tok_up = swap(tok_two[:half], "seq", 1)
    tok_low = swap(tok_one[half:], "seq", 2)

    vectors = [gain_one, shift_one, bias_qv, bias_out, gain_two, shift_two, bias_fc, bias_proj]
    packed = jnp.concatenate([v.reshape(-1, own) for v in vectors], axis=0)
    lines = packed.shape[0]
    packed = jnp.pad(packed.reshape(-1), (0, 16 * 3 * local - packed.size)).reshape(16, 3 * local)
    mine_qkv = pick(w_qkv.reshape(own, 3, ns, local), me, 2).reshape(own, 3 * local)
    sent_qkv = jnp.concatenate([mine_qkv, packed], axis=0)
    kept_qkv = jnp.stack([sent_qkv] + [swap(sent_qkv, "fsdp", 2 * k) for k in range(1, nz)])
    moved_qkv = swap(kept_qkv, "fsdp", 1)

    fc_mine, fc_sent, proj_share = pack(place, w_fc, w_proj)
    fc_other = swap(fc_sent, "fsdp", 1)
    fc_share = join(place, fc_mine, fc_other)
    fc_zero = jnp.concatenate([swap(fc_share, "fsdp", 2 * k) for k in range(1, nz)], axis=0)
    proj_zero = jnp.concatenate([swap(proj_share, "fsdp", 2 * k) for k in range(1, nz)], axis=0)
    kept_out = jnp.stack([w_out] + [swap(w_out, "fsdp", 2 * k) for k in range(1, nz)])
    moved_out = swap(kept_out, "fsdp", 1)
    fc_one = swap(fc_zero, "seq", 1)
    fc_two = swap(fc_zero, "seq", 2)
    fc_three = swap(fc_two, "seq", 1)
    proj_one = swap(proj_zero, "seq", 1)
    proj_two = swap(proj_zero, "seq", 2)
    proj_three = swap(proj_one, "seq", 2)
    branch_both = jnp.concatenate([swap(branch, "fsdp", 1), branch], axis=0)

    small = by_core(core, kept_qkv[:, own : own + 2], moved_qkv[:, own : own + 2], 1)
    small = xor_take(small, floor, 0).reshape(nf, -1).reshape(nf, lines, own)
    at = 0
    full = []
    for v in vectors:
        count = v.shape[0] // own
        full.append(small[:, at : at + count].reshape(1, -1).astype(F32))
        at += count
    gain_a, shift_a, qv_vec, out_vec, gain_b, shift_b, fc_vec, proj_vec = full
    qv_mine = pick(qv_vec.reshape(2, ns, local), me, 1)
    bias_all = jnp.concatenate([qv_mine[0], jnp.zeros((local,), F32), qv_mine[1]]).reshape(1, -1)
    fc_bias = xor_take(pick(fc_vec.reshape(nz, 2, ns, hw), core, 1), me, 1)
    order = [(q, 0) for q in (0, 2, 1, 3)] + [(q, 1) for q in range(4)]
    fc_bias = jnp.concatenate(
        [fc_bias[2 * part : 2 * part + 2, q].reshape(1, -1) for q, part in order], axis=1
    )

    first, unit_all, qkv = project(
        place, (token_block, tok_one, tok_two, tok_up, tok_low), kept_qkv, moved_qkv, gain_a, shift_a,
        bias_all,
    )
    lens = jnp.concatenate([prompt_lens, cont_lens[0], me.reshape(1)]).astype(jnp.int32)
    mixed_heads, log_norm = attend_forward(lens, qkv, heads)
    mixed_blocks = [mixed_heads] + [
        swap(mixed_heads[k * toks : (k + 1) * toks], "seq", k) for k in range(1, ns)
    ]
    hidden, second, mixed, out_mat = attn_out(
        place, mixed_blocks, kept_out, moved_out, token_block, out_vec, gain_b, shift_b
    )

    second_both = jnp.concatenate([swap(second, "fsdp", 1), second], axis=0)
    act, grad_pre, out_own, out_oth, back_own, back_oth, fc_bias_sum = feed(
        place, second_both, branch_both, fc_bias, fc_mine, fc_other,
        (fc_zero, fc_one, fc_two, fc_three), w_proj, (proj_zero, proj_one, proj_two, proj_three),
    )
    back_got = swap(back_oth, "fsdp", 1)
    out_got = swap(out_oth, "fsdp", 1)
    output = (hidden + out_own + proj_vec + out_got.astype(F32)).astype(BF)[None]
    grad_hidden, grad_attn, *grad_blocks, sums_two = mixed_back(
        place, back_own, back_got, hidden, branch, gain_b, out_mat
    )
    grad_heads = jnp.concatenate(
        [grad_blocks[0]] + [swap(grad_blocks[k], "seq", k) for k in range(1, ns)], axis=0
    )

    edge = 4 * hw
    fc_grads = [tn(second_both, grad_pre[:, i * edge : (i + 1) * edge]).astype(BF) for i in range(4)]
    proj_grads = [tn(act[:, i * edge : (i + 1) * edge], branch_both).astype(BF) for i in range(4)]
    chunk = 2 * hw
    fc_x = swap(fc_grads[1], "seq", 1)
    fc_y = swap(fc_grads[3], "seq", 2)
    proj_x = swap(proj_grads[1], "seq", 1)
    proj_y = swap(proj_grads[3], "seq", 2)

    def added(left, right):
        return (left.astype(F32) + right.astype(F32)).astype(BF)

    fc_last_y = swap(added(fc_grads[0][:, chunk:], fc_x[:, chunk:]), "seq", 2)
    fc_last_x = swap(added(fc_grads[2][:, chunk:], fc_y[:, chunk:]), "seq", 1)
    proj_last_y = swap(added(proj_grads[0][chunk:], proj_x[chunk:]), "seq", 2)
    proj_last_x = swap(added(proj_grads[2][chunk:], proj_y[chunk:]), "seq", 1)
    cuts = gather_sum(
        place,
        (fc_grads[0], fc_x, fc_last_y, fc_grads[2], fc_y, fc_last_x),
        (proj_grads[0], proj_x, proj_last_y, proj_grads[2], proj_y, proj_last_x),
    )
    kept, moved = floor_sum(
        place, [cuts[0]] + [swap(cuts[k], "fsdp", 2 * k) for k in range(1, nz)]
    )
    moved = swap(moved, "fsdp", 1)
    grad_w_fc, grad_w_proj = spread(
        place,
        [kept] + [swap(kept, "seq", k) for k in range(1, ns)],
        [moved] + [swap(moved, "seq", k) for k in range(1, ns)],
    )

    grad_q, grad_k, grad_v = attend_backward(lens, qkv, mixed_heads, grad_heads, log_norm, heads)
    grad_qkv = jnp.concatenate([grad_q, grad_k, grad_v], axis=1)
    qkv_mat = by_core(core, kept_qkv[:, :own], moved_qkv[:, :own], 1)
    qkv_mat = xor_take(qkv_mat, floor, 0).reshape(width, 3 * local)
    up1, up3, low2, low3, sums_early = first_back((2, 6, 5, 7), None, grad_qkv, unit_all, qkv_mat)
    got_x1, got_x3 = swap(up1, "seq", 1), swap(up3, "seq", 1)
    got_y2, got_y3 = swap(low2, "seq", 2), swap(low3, "seq", 2)
    up2, low1, up0, low0, sums_late = first_back((4, 3, 0, 1), None, grad_qkv, unit_all, qkv_mat)
    last_y = swap(added(up2, got_x3), "seq", 2)
    last_x = swap(added(low1, got_y3), "seq", 1)
    tile = pl.BlockSpec((half, width), lambda: (0, 0))

    def last(keep, got, end, rows):
        return pl.pallas_call(
            last_kernel,
            out_shape=jax.ShapeDtypeStruct((half, width), F32),
            in_specs=[tile] * 5 + [pl.BlockSpec((1, width), lambda: (0, 0))],
            out_specs=tile,
            name="last",
        )(keep, got, end, token_block[rows], grad_hidden[rows], gain_a)

    input_grad = jnp.concatenate(
        [
            last(up0, got_x1, last_y, slice(0, half)),
            last(low0, got_y2, last_x, slice(half, toks)),
        ],
        axis=0,
    )[None]

    def over_floors(grad):
        cut = grad.reshape(nz, 2, own, -1)
        total = pick(cut, core, 1).astype(F32) + swap(pick(cut, 1 - core, 1), "fsdp", 1).astype(F32)
        owned = pick(total, floor, 0)
        for k in range(1, nz):
            owned = owned + swap(pick(total, floor ^ k, 0).astype(BF), "fsdp", 2 * k).astype(F32)
        return owned

    grad_w_out = over_floors(tn(mixed, grad_attn).astype(BF))
    for bit in (1, 2):
        grad_w_out = grad_w_out + swap(grad_w_out.astype(BF), "seq", bit).astype(F32)

    in_owned = over_floors(tn(first, grad_qkv).astype(BF)).astype(BF)
    in_blocks = jnp.stack(
        [in_owned.reshape(own, 3, local)]
        + [swap(in_owned, "seq", k).reshape(own, 3, local) for k in range(1, ns)],
        axis=2,
    )
    grad_w_qkv = xor_take(in_blocks, me, 2).reshape(own, 3 * width).astype(F32)

    def placed(values):
        slots = jnp.arange(ns)[:, None] == me
        return jnp.where(slots, values[None, :], 0.0).reshape(-1)

    spots = {}
    for i, (q, part) in enumerate(order):
        spots[q, part] = fc_bias_sum[0, i * chunk : (i + 1) * chunk].reshape(2, hw)
    fc_bias_grad = jnp.stack(
        [jnp.concatenate([spots[q, 0], spots[q, 1]], axis=0) for q in range(ns)], axis=1
    )
    fc_bias_grad = xor_take(fc_bias_grad, me, 1)
    fc_bias_grad = jnp.where(
        (jnp.arange(2) == core)[None, :, None, None], fc_bias_grad[:, None], 0.0
    ).reshape(-1)
    sums_one = sums_early + sums_late
    vector_grads = [
        sums_one[0],
        sums_one[1],
        placed(jnp.sum(grad_q.astype(F32), axis=0)),
        placed(jnp.sum(grad_v.astype(F32), axis=0)),
        sums_two[0],
        sums_two[1],
        sums_two[2],
        fc_bias_grad,
        sums_two[3],
    ]
    vector_sum = jnp.concatenate([v.reshape(-1, width) for v in vector_grads], axis=0)
    for axis, size in (("seq", ns), ("fsdp", nf)):
        bit = 1
        while bit < size:
            vector_sum = vector_sum + swap(vector_sum, axis, bit)
            bit *= 2
    vector_sum = vector_sum.reshape(-1)
    outs = []
    at = 0
    for v in vectors:
        count = v.shape[0]
        outs.append(lax.dynamic_slice_in_dim(vector_sum, at + owner * count, count))
        at += nf * count
    (g_gain_one, g_shift_one, g_bias_qv, g_bias_out, g_gain_two, g_shift_two, g_bias_fc, g_bias_proj) = outs

    return (
        output,
        input_grad,
        g_gain_one,
        g_shift_one,
        grad_w_qkv,
        g_bias_qv,
        grad_w_out,
        g_bias_out,
        g_gain_two,
        g_shift_two,
        grad_w_fc,
        g_bias_fc,
        grad_w_proj,
        g_bias_proj,
    )


def body(*args):
    tokens, w_proj = args[0], args[13]
    fits = (
        lax.axis_size("seq") == 4
        and lax.axis_size("fsdp") == 8
        and tokens.shape[1:] == (512, 1024)
        and w_proj.shape == (512, 1024)
    )
    return body_aligned(*args) if fits else body_general(*args)


def solution(mesh):
    rows = P("fsdp", None)
    vec = P("fsdp")
    acts = P("fsdp", "seq", None)
    return jax.shard_map(
        body,
        mesh=mesh,
        in_specs=(
            acts, vec, rows, vec, vec, rows, vec, rows, vec, vec, vec, rows, vec, rows, vec, acts,
        ),
        out_specs=(
            acts, acts, vec, vec, rows, vec, rows, vec, vec, vec, rows, vec, rows, vec,
        ),
        check_vma=False,
    )
```

time: 909 us -> 582 us (0.64)
  Pallas kernels: 0 us -> 195 us
  matrix products: 169 us -> 28.2 us
  blocking collectives: 122 us -> 0 us
  other arithmetic: 153 us -> 34.1 us
  waiting for transfers between devices: 274 us -> 172 us
  local copies, waits for them, and re-layouts: 128 us -> 31.2 us
  starting transfers between devices: 35 us -> 111 us
  between operations: 18.5 us -> 2.74 us
    reduce_scatter x4 -> x0, waiting for transfers between devices: 209 us -> none  [the longest x1 90.3 us: body(): lax.psum_scatter(grad_w_fc.astype(jnp.bfloat16), 'fsdp', scatter_dimensio...]
    pallas_call x0 -> x15, Pallas kernels: none -> 195 us  [the longest x1 46.3 us: feed(): pl.pallas_call(functools.partial(feed_kernel, hw), out_shape=(jax.ShapeDt...]
    ppermute x0 -> x77, waiting for transfers between devices: none -> 172 us  [swap(): return lax.ppermute(values, axis, [(i, i ^ bits) for i in range(size)])]
    dot_general x36 -> x10, matrix products: 169 us -> 28.2 us  [tn(): lax.dot_general(left, right, (((0,), (0,)), ((), ())), preferred_element_...]
    ppermute x0 -> x77, starting transfers between devices: none -> 111 us  [swap(): return lax.ppermute(values, axis, [(i, i ^ bits) for i in range(size)])]
    all_gather x8 -> x0, blocking collectives: 85 us -> none  [the longest x1 13.5 us: body(): lax.all_gather(gain_one, 'fsdp', axis=0, tiled=True)]
    unnamed x14 -> x1, other arithmetic: 76.7 us -> 0.07 us
    unnamed x246 -> x155, local copies, waits for them, and re-layouts: 72.6 us -> 14.2 us
  transfers between devices with their start and end apart: 17 -> 77, of which waited for: 7 -> 30; matrix products, arithmetic and copies ran while one was open for 43% -> 13% of each run, Pallas kernels for 0% -> 26%
where the time goes in v1:
time: 582 us; the launch traced here: 574 us
  Pallas kernels  195 us (34%)
  waiting for transfers between devices  172 us (30%)
  starting transfers between devices  111 us (19%)
  other arithmetic  34.1 us (6%)
  local copies, waits for them, and re-layouts  31.2 us (5%)
  matrix products  28.2 us (5%)
    ppermute x77, waiting for transfers between devices, swap(): return lax.ppermute(values, axis, [(i, i ^ bits) for i in range(size)])  172 us
    ppermute x77, starting transfers between devices, swap(): return lax.ppermute(values, axis, [(i, i ^ bits) for i in range(size)])  111 us
    pallas_call x1, Pallas kernels, feed(): pl.pallas_call(functools.partial(feed_kernel, hw), out_shape=(jax.ShapeDt...  46.3 us
    pallas_call x1, Pallas kernels, attend_backward(): pl.pallas_call(functools.partial(backward_kernel, rows, block_rows, per_p...  40.4 us
    pallas_call x1, Pallas kernels, attend_forward(): pl.pallas_call(functools.partial(forward_kernel, rows, block_rows, per_pa...  38.5 us
    dot_general x10, matrix products, tn(): lax.dot_general(left, right, (((0,), (0,)), ((), ())), preferred_element_...  28.2 us
    pallas_call x2, Pallas kernels, first_back(): pl.pallas_call(functools.partial(first_back_kernel, tiles), out_shape=tup...  15.6 us
    unnamed x155, local copies, waits for them, and re-layouts  14.2 us
  transfers between devices with their start and end apart: 77, of which 30 were waited for; matrix products, arithmetic and copies ran while one was open for 13% of the time, Pallas kernels for 26%

profile of v1, /device:TPU:0, one launch (start us, length us, event | category | flops | bytes accessed | tf_op | source)
XLA Modules:
  0.0 574.2 jit_solution(18275722460206627974)
XLA Ops:
  2.8 3.1 collective-permute-start.4
  5.9 2.6 collective-permute-start.5
  10.0 3.4 pack_shares.1
  16.2 3.1 collective-permute-start.12
  19.2 5.4 collective-permute-done.5
  24.6 2.5 collective-permute-start.13
  27.1 13.5 %collective-permute-start.24 = (bf16[128,1024]{1,0:T(8,128)(2,1)}, bf16[128,1024]{1,0:T(8,128)(2,1)}, u32[]{:S(2)}, u32[]{:S(2)}) collective-permute-start(bf16[128,1024]{1,0:T(8,128)(2,1)} %get-tuple-element.67), channel_id=1, source_target_pairs={{0,2},{1,3},{2,0},{3,1},{4,6},{5,7},{6,4},{7,5},{8,10},{9,11},{10,... | collective-permute-start | bytes 786440 | tf_op jit(solution)/shard_map/ppermute | solution.py:26
  41.7 2.3 collective-permute-start.25
  45.6 2.3 join_rows.1
  47.9 9.7 %collective-permute-done.12 = bf16[128,1024]{1,0:T(8,128)(2,1)} collective-permute-done((bf16[128,1024]{1,0:T(8,128)(2,1)}, bf16[128,1024]{1,0:T(8,128)(2,1)}, u32[]{:S(2)}, u32[]{:S(2)}) %collective-permute-start.12) | collective-permute-done | bytes 262176 | tf_op jit(solution)/shard_map/ppermute | solution.py:26
  60.6 8.2 %collective-permute-done.25 = bf16[128,1024]{1,0:T(8,128)(2,1)} collective-permute-done((bf16[128,1024]{1,0:T(8,128)(2,1)}, bf16[128,1024]{1,0:T(8,128)(2,1)}, u32[]{:S(2)}, u32[]{:S(2)}) %collective-permute-start.25) | collective-permute-done | bytes 262176 | tf_op jit(solution)/shard_map/ppermute | solution.py:26
  68.8 5.7 collective-permute-start.19
  78.6 2.3 pad_maximum_fusion.1.kept_ref
  80.9 5.6 collective-permute-done.19
  89.1 5.5 collective-permute-done.20
  107.6 19.2 %collective-permute-done.2.up_ref = bf16[256,1024]{1,0:T(8,128)(2,1)S(1)} collective-permute-done((bf16[256,1024]{1,0:T(8,128)(2,1)}, bf16[256,1024]{1,0:T(8,128)(2,1)S(1)}, u32[]{:S(2)}, u32[]{:S(2)}) %collective-permute-start.2) | collective-permute-done | bytes 524320 | tf_op jit(solution)/shard_map/ppermute | solution.py:26
  126.8 2.1 collective-permute-done.3.low_ref
  129.7 12.0 %project.1 = (bf16[2048,1024]{1,0:T(8,128)(2,1)}, bf16[2048,1024]{1,0:T(8,128)(2,1)}, bf16[2048,768]{1,0:T(8,128)(2,1)}) custom-call(s32[3]{0:T(128)} %pad_add_fusion.place, bf16[512,1024]{1,0:T(8,128)(2,1)} %bitcast.169, bf16[512,1024]{1,0:T(8,128)(2,1)} %copy-done.16, bf16[512,1024]{1,0:T(8,128)(2,1)} %copy-done.15, bf16[256,1024]{1,0:T(8,128)(2,1)} %copy-done.33, ...), custom_call_target="tpu_custom_call" | custom-call | tf_op jit(solution)/shard_map/project/pallas_call | solution.py:837
  141.7 38.5 %attend_forward.1 = (bf16[2048,256]{1,0:T(8,128)(2,1)}, f32[2,8,1,512]{3,2,1,0:T(1,128)}) custom-call(s32[4]{0:T(128)} %pad_add_fusion.1.lens, bf16[2048,768]{1,0:T(8,128)(2,1)} %get-tuple-element.61.q_ref.k_ref.v_ref, bf16[2048,768]{1,0:T(8,128)(2,1)} %get-tuple-element.61.q_ref.k_ref.v_ref, bf16[2048,768]{1,0:T(8,128)(2,1)} %get-tuple-element.61.q_ref.k_ref.v_ref), custom_call_target="tpu_custom_call" | custom-call | tf_op jit(solution)/shard_map/attend_forward/pallas_call | solution.py:296
  187.8 3.7 collective-permute-done.10.m3
  192.1 5.1 collective-permute-done.8.m1
  198.4 7.1 %attn_out.1 = (f32[512,1024]{1,0:T(8,128)}, bf16[512,1024]{1,0:T(8,128)(2,1)}, bf16[512,1024]{1,0:T(8,128)(2,1)}, bf16[1024,1024]{1,0:T(8,128)(2,1)}) custom-call(s32[3]{0:T(128)} %pad_add_fusion.place, bf16[2048,256]{1,0:T(8,128)(2,1)} %get-tuple-element.62.m0.out_ref, bf16[512,256]{1,0:T(8,128)(2,1)} %copy-done.40, bf16[512,256]{1,0:T(8,128)(2,1)} %copy-done.41, ...), custom_call_target="tpu_custom_call" | custom-call | tf_op jit(solution)/shard_map/attn_out/pallas_call | solution.py:897
  206.4 2.1 collective-permute-done.15
  208.7 3.8 collective-permute-done.28.b2
  214.2 15.1 %collective-permute-done.29.b3 = bf16[384,1024]{1,0:T(8,128)(2,1)} collective-permute-done((bf16[384,1024]{1,0:T(8,128)(2,1)}, bf16[384,1024]{1,0:T(8,128)(2,1)}, u32[]{:S(2)}, u32[]{:S(2)}) %collective-permute-start.29) | collective-permute-done | bytes 786464 | tf_op jit(solution)/shard_map/ppermute | solution.py:26
  229.4 46.3 %feed.1 = (bf16[1024,2048]{1,0:T(8,128)(2,1)}, bf16[1024,2048]{1,0:T(8,128)(2,1)}, f32[512,1024]{1,0:T(8,128)}, bf16[512,1024]{1,0:T(8,128)(2,1)}, f32[512,1024]...) custom-call(s32[3]{0:T(128)} %pad_add_fusion.place, bf16[1024,1024]{1,0:T(8,128)(2,1)} %copy-done.6, ...), custom_call_target="tpu_custom_call" | custom-call | tf_op jit(solution)/shard_map/feed/pallas_call | solution.py:1010
  275.8 4.3 convolution_convert_fusion.6
  280.1 2.3 convolution_convert_fusion.7.refs_3_
  282.4 2.3 convolution_convert_fusion.8
  286.8 2.3 convolution_convert_fusion.4
  290.5 2.3 convolution_convert_fusion.2
  293.5 2.3 convolution_convert_fusion.5.refs_6_
  295.8 3.8 convolution_convert_fusion.3.refs_9_
  299.6 2.5 convolution_convert_fusion.9.refs_0_
  302.7 8.1 %mixed_back.1 = (f32[512,1024]{1,0:T(8,128)}, bf16[512,1024]{1,0:T(8,128)(2,1)}, bf16[512,256]{1,0:T(8,128)(2,1)}, bf16[512,256]{1,0:T(8,128)(2,1)}, bf16[512,25...) custom-call(s32[3]{0:T(128)} %pad_add_fusion.place, f32[512,1024]{1,0:T(8,128)} %get-tuple-element.70.own_ref, ...), custom_call_target="tpu_custom_call" | custom-call | tf_op jit(solution)/shard_map/mixed_back/pallas_call | solution.py:1082
  317.8 17.2 %collective-permute-done.63.refs_7_ = bf16[512,1024]{1,0:T(8,128)(2,1)} collective-permute-done((bf16[512,1024]{1,0:T(8,128)(2,1)}, bf16[512,1024]{1,0:T(8,128)(2,1)}, u32[]{:S(2)}, u32[]{:S(2)}) %collective-permute-start.63) | collective-permute-done | bytes 1048608 | tf_op jit(solution)/shard_map/ppermute | solution.py:26
  337.7 2.8 collective-permute-done.32
  341.7 4.5 collective-permute-done.34
  348.7 40.4 %attend_backward.1 = (bf16[2048,256]{1,0:T(8,128)(2,1)}, bf16[2048,256]{1,0:T(8,128)(2,1)}, bf16[2048,256]{1,0:T(8,128)(2,1)}) custom-call(s32[4]{0:T(128)} %pad_add_fusion.1.lens, bf16[2048,768]{1,0:T(8,128)(2,1)} %get-tuple-element.61.q_ref.k_ref.v_ref, bf16[2048,768]{1,0:T(8,128)(2,1)} %get-tuple-element.61.q_ref.k_ref.v_ref, ...), custom_call_target="tpu_custom_call" | custom-call | tf_op jit(solution)/shard_map/attend_backward/pallas_call | solution.py:328
  394.3 7.7 %first_back.3 = (bf16[256,1024]{1,0:T(8,128)(2,1)}, bf16[256,1024]{1,0:T(8,128)(2,1)}, bf16[256,1024]{1,0:T(8,128)(2,1)}, bf16[256,1024]{1,0:T(8,128)(2,1)}, f32[2,1024]{1,0:T(2,128)}) custom-call(s32[4]{0:T(128)} %constant.127.clone.place, bf16[2048,768]{1,0:T(8,128)(2,1)} %copy-done, bf16[2048,1024]{1,0:T(8,128)(2,1)} %get-tuple-element.81.unit_ref, ...), custom_call_target="tpu_custom_call" | custom-call | tf_op jit(solution)/shard_map/first_back/pallas_call | solution.py:1139
  402.0 7.9 %first_back.2 = (bf16[256,1024]{1,0:T(8,128)(2,1)}, bf16[256,1024]{1,0:T(8,128)(2,1)}, bf16[256,1024]{1,0:T(8,128)(2,1)}, bf16[256,1024]{1,0:T(8,128)(2,1)}, f32[2,1024]{1,0:T(2,128)}) custom-call(s32[4]{0:T(128)} %constant.128.clone.place, bf16[2048,768]{1,0:T(8,128)(2,1)} %copy-done, bf16[2048,1024]{1,0:T(8,128)(2,1)} %get-tuple-element.81.unit_ref, ...), custom_call_target="tpu_custom_call" | custom-call | tf_op jit(solution)/shard_map/first_back/pallas_call | solution.py:1139
  411.8 2.2 add_convert_fusion.1
  414.0 2.1 collective-permute-done.41
  417.4 3.6 fusion
  421.2 3.7 convolution_convert_fusion.1
  427.1 2.8 collective-permute-start.44
  429.9 6.1 %gather_sum.1 = (bf16[512,512]{1,0:T(8,128)(2,1)}, bf16[512,512]{1,0:T(8,128)(2,1)}, bf16[512,512]{1,0:T(8,128)(2,1)}, bf16[512,512]{1,0:T(8,128)(2,1)}) custom-call(s32[3]{0:T(128)} %pad_add_fusion.place, bf16[1024,512]{1,0:T(8,128)(2,1)} %copy-done.20, bf16[1024,512]{1,0:T(8,128)(2,1)} %collective-permute-done.59.refs_1_, ...), custom_call_target="tpu_custom_call" | custom-call | tf_op jit(solution)/shard_map/gather_sum/pallas_call | solution.py:1181
  436.2 2.2 collective-permute-start.68
  438.4 2.5 convolution_convert_fusion
  442.8 22.4 %collective-permute-done.45 = f32[12,1024]{1,0:T(8,128)S(1)} collective-permute-done((f32[12,1024]{1,0:T(8,128)S(1)}, f32[12,1024]{1,0:T(8,128)S(1)}, u32[]{:S(2)}, u32[]{:S(2)}) %collective-permute-start.45) | collective-permute-done | bytes 49184 | tf_op jit(solution)/shard_map/ppermute | solution.py:26
  471.0 2.2 add_convert_fusion.6
  473.2 8.5 %collective-permute-done.69.r3 = bf16[512,512]{1,0:T(8,128)(2,1)} collective-permute-done((bf16[512,512]{1,0:T(8,128)(2,1)}, bf16[512,512]{1,0:T(8,128)(2,1)}, u32[]{:S(2)}, u32[]{:S(2)}) %collective-permute-start.69) | collective-permute-done | bytes 524320 | tf_op jit(solution)/shard_map/ppermute | solution.py:26
  483.1 3.5 floor_sum.1
  488.8 8.4 %collective-permute-start.47 = (bf16[128,768]{0,1:T(8,128)(2,1)S(1)}, bf16[128,768]{0,1:T(8,128)(2,1)S(1)}, u32[]{:S(2)}, u32[]{:S(2)}) collective-permute-start(bf16[128,768]{0,1:T(8,128)(2,1)S(1)} %get-tuple-element.129), channel_id=1, source_target_pairs={{0,2},{1,3},{2,0},{3,1},{4,6},{5,7},{6,4},{7,5},{8,10},{9,11},{10,... | collective-permute-start | bytes 589832 | tf_op jit(solution)/shard_map/ppermute | solution.py:26
  499.1 7.2 %collective-permute-start.48 = (bf16[128,768]{0,1:T(8,128)(2,1)S(1)}, bf16[128,768]{0,1:T(8,128)(2,1)S(1)}, u32[]{:S(2)}, u32[]{:S(2)}) collective-permute-start(bf16[128,768]{0,1:T(8,128)(2,1)S(1)} %get-tuple-element.131), channel_id=1, source_target_pairs={{0,4},{1,5},{2,6},{3,7},{4,0},{5,1},{6,2},{7,3},{8,12},{9,13},{10,... | collective-permute-start | bytes 589832 | tf_op jit(solution)/shard_map/ppermute | solution.py:26
  509.9 8.6 %collective-permute-done.48 = bf16[128,768]{0,1:T(8,128)(2,1)S(1)} collective-permute-done((bf16[128,768]{0,1:T(8,128)(2,1)S(1)}, bf16[128,768]{0,1:T(8,128)(2,1)S(1)}, u32[]{:S(2)}, u32[]{:S(2)}) %collective-permute-start.48) | collective-permute-done | bytes 196640 | tf_op jit(solution)/shard_map/ppermute | solution.py:26
  523.0 3.2 collective-permute-done.75.refs_6_
  527.3 3.0 collective-permute-done.76.refs_7_
  536.5 3.7 last.2
  540.1 3.7 last.3
  545.3 4.8 collective-permute-done.55
  558.6 4.6 spread.1
  564.3 2.2 collective-permute-done.57
  569.8 3.3 collective-permute-done.58
  (374 shorter events, 116.4 us)
Async XLA Ops:
  2.8 13.4 %collective-permute-start.4 = (bf16[144,768]{1,0:T(8,128)(2,1)S(1)}, bf16[144,768]{1,0:T(8,128)(2,1)S(1)}, u32[]{:S(2)}, u32[]{:S(2)}) collective-permute-start(bf16[144,768]{1,0:T(8,128)(2,1)S(1)} %get-tuple-element.148), channel_id=1, source_target_pairs={{0,2},{1,3},{2,0},{3,1},{4,6},{5,7},{6,4},{7,5},{8,10},{9,11},{10,... | collective-permute-start | bytes 663560 | tf_op jit(solution)/shard_map/ppermute | solution.py:26
  5.9 18.7 %collective-permute-start.5 = (bf16[144,768]{1,0:T(8,128)(2,1)S(1)}, bf16[144,768]{1,0:T(8,128)(2,1)S(1)}, u32[]{:S(2)}, u32[]{:S(2)}) collective-permute-start(bf16[144,768]{1,0:T(8,128)(2,1)S(1)} %get-tuple-element.148), channel_id=1, source_target_pairs={{0,4},{1,5},{2,6},{3,7},{4,0},{5,1},{6,2},{7,3},{8,12},{9,13},{10,... | collective-permute-start | bytes 663560 | tf_op jit(solution)/shard_map/ppermute | solution.py:26
  8.5 18.6 %collective-permute-start.6 = (bf16[144,768]{1,0:T(8,128)(2,1)S(1)}, bf16[144,768]{1,0:T(8,128)(2,1)S(1)}, u32[]{:S(2)}, u32[]{:S(2)}) collective-permute-start(bf16[144,768]{1,0:T(8,128)(2,1)S(1)} %get-tuple-element.148), channel_id=1, source_target_pairs={{0,6},{1,7},{2,4},{3,5},{4,2},{5,3},{6,0},{7,1},{8,14},{9,15},{10,... | collective-permute-start | bytes 663560 | tf_op jit(solution)/shard_map/ppermute | solution.py:26
  8.5 33.2 %collective-permute-start.11 = (bf16[128,1024]{1,0:T(8,128)(2,1)}, bf16[128,1024]{1,0:T(8,128)(2,1)S(1)}, u32[]{:S(2)}, u32[]{:S(2)}) collective-permute-start(bf16[128,1024]{1,0:T(8,128)(2,1)} %param.25), channel_id=1, source_target_pairs={{0,2},{1,3},{2,0},{3,1},{4,6},{5,7},{6,4},{7,5},{8,10},{9,11},{10,... | collective-permute-start | bytes 786440 | tf_op jit(solution)/shard_map/ppermute | solution.py:26
  13.4 30.7 %collective-permute-start.17 = (bf16[128,2048]{1,0:T(8,128)(2,1)}, bf16[128,2048]{1,0:T(8,128)(2,1)S(1)}, u32[]{:S(2)}, u32[]{:S(2)}) collective-permute-start(bf16[128,2048]{1,0:T(8,128)(2,1)} %get-tuple-element.66), channel_id=1, source_target_pairs={{0,1},{1,0},{2,3},{3,2},{4,5},{5,4},{6,7},{7,6},{8,9},{9,8},{10,11... | collective-permute-start | bytes 1572872 | tf_op jit(solution)/shard_map/ppermute | solution.py:26
  16.2 41.4 %collective-permute-start.12 = (bf16[128,1024]{1,0:T(8,128)(2,1)}, bf16[128,1024]{1,0:T(8,128)(2,1)}, u32[]{:S(2)}, u32[]{:S(2)}) collective-permute-start(bf16[128,1024]{1,0:T(8,128)(2,1)} %param.25), channel_id=1, source_target_pairs={{0,4},{1,5},{2,6},{3,7},{4,0},{5,1},{6,2},{7,3},{8,12},{9,13},{10,... | collective-permute-start | bytes 786440 | tf_op jit(solution)/shard_map/ppermute | solution.py:26
  24.6 34.5 %collective-permute-start.13 = (bf16[128,1024]{1,0:T(8,128)(2,1)}, bf16[128,1024]{1,0:T(8,128)(2,1)}, u32[]{:S(2)}, u32[]{:S(2)}) collective-permute-start(bf16[128,1024]{1,0:T(8,128)(2,1)} %param.25), channel_id=1, source_target_pairs={{0,6},{1,7},{2,4},{3,5},{4,2},{5,3},{6,0},{7,1},{8,14},{9,15},{10,... | collective-permute-start | bytes 786440 | tf_op jit(solution)/shard_map/ppermute | solution.py:26
  27.1 33.5 %collective-permute-start.24 = (bf16[128,1024]{1,0:T(8,128)(2,1)}, bf16[128,1024]{1,0:T(8,128)(2,1)}, u32[]{:S(2)}, u32[]{:S(2)}) collective-permute-start(bf16[128,1024]{1,0:T(8,128)(2,1)} %get-tuple-element.67), channel_id=1, source_target_pairs={{0,2},{1,3},{2,0},{3,1},{4,6},{5,7},{6,4},{7,5},{8,10},{9,11},{10,... | collective-permute-start | bytes 786440 | tf_op jit(solution)/shard_map/ppermute | solution.py:26
  41.7 27.1 %collective-permute-start.25 = (bf16[128,1024]{1,0:T(8,128)(2,1)}, bf16[128,1024]{1,0:T(8,128)(2,1)}, u32[]{:S(2)}, u32[]{:S(2)}) collective-permute-start(bf16[128,1024]{1,0:T(8,128)(2,1)} %get-tuple-element.67), channel_id=1, source_target_pairs={{0,4},{1,5},{2,6},{3,7},{4,0},{5,1},{6,2},{7,3},{8,12},{9,13},{10,... | collective-permute-start | bytes 786440 | tf_op jit(solution)/shard_map/ppermute | solution.py:26
  44.0 24.8 %collective-permute-start.26 = (bf16[128,1024]{1,0:T(8,128)(2,1)}, bf16[128,1024]{1,0:T(8,128)(2,1)S(1)}, u32[]{:S(2)}, u32[]{:S(2)}) collective-permute-start(bf16[128,1024]{1,0:T(8,128)(2,1)} %get-tuple-element.67), channel_id=1, source_target_pairs={{0,6},{1,7},{2,4},{3,5},{4,2},{5,3},{6,0},{7,1},{8,14},{9,15},{10,... | collective-permute-start | bytes 786440 | tf_op jit(solution)/shard_map/ppermute | solution.py:26
  57.6 37.9 %collective-permute-start.1 = (bf16[512,1024]{1,0:T(8,128)(2,1)S(1)}, bf16[512,1024]{1,0:T(8,128)(2,1)S(1)}, u32[]{:S(2)}, u32[]{:S(2)}) collective-permute-start(bf16[512,1024]{1,0:T(8,128)(2,1)S(1)} %bitcast.171), channel_id=1, source_target_pairs={{0,16},{8,24},{16,0},{24,8},{1,17},{9,25},{17,1},{25,9},{2,18},{10... | collective-permute-start | bytes 3145736 | tf_op jit(solution)/shard_map/ppermute | solution.py:26
  59.1 38.7 %collective-permute-start = (bf16[512,1024]{1,0:T(8,128)(2,1)S(1)}, bf16[512,1024]{1,0:T(8,128)(2,1)S(1)}, u32[]{:S(2)}, u32[]{:S(2)}) collective-permute-start(bf16[512,1024]{1,0:T(8,128)(2,1)S(1)} %bitcast.172), channel_id=1, source_target_pairs={{0,8},{8,0},{16,24},{24,16},{1,9},{9,1},{17,25},{25,17},{2,10},{10... | collective-permute-start | bytes 3145736 | tf_op jit(solution)/shard_map/ppermute | solution.py:26
  60.6 39.6 %collective-permute-start.16 = (bf16[512,1024]{1,0:T(8,128)(2,1)}, bf16[512,1024]{1,0:T(8,128)(2,1)S(1)}, u32[]{:S(2)}, u32[]{:S(2)}) collective-permute-start(bf16[512,1024]{1,0:T(8,128)(2,1)} %bitcast.174), channel_id=1, source_target_pairs={{0,1},{1,0},{2,3},{3,2},{4,5},{5,4},{6,7},{7,6},{8,9},{9,8},{10,11... | collective-permute-start | bytes 3145736 | tf_op jit(solution)/shard_map/ppermute | solution.py:26
  68.8 17.6 %collective-permute-start.19 = (bf16[256,512]{1,0:T(8,128)(2,1)}, bf16[256,512]{1,0:T(8,128)(2,1)S(1)}, u32[]{:S(2)}, u32[]{:S(2)}) collective-permute-start(bf16[256,512]{1,0:T(8,128)(2,1)} %join_rows.1), channel_id=1, source_target_pairs={{0,4},{1,5},{2,6},{3,7},{4,0},{5,1},{6,2},{7,3},{8,12},{9,13},{10,... | collective-permute-start | bytes 786440 | tf_op jit(solution)/shard_map/ppermute | solution.py:26
  77.0 25.3 %collective-permute-start.7 = (bf16[4,144,768]{2,1,0:T(8,128)(2,1)S(1)}, bf16[4,144,768]{2,1,0:T(8,128)(2,1)S(1)}, u32[]{:S(2)}, u32[]{:S(2)}) collective-permute-start(bf16[4,144,768]{2,1,0:T(8,128)(2,1)S(1)} %pad_maximum_fusion.3.kept_ref), channel_id=1, source_target_pairs={{0,1},{1,0},{2,3},{3,2},{4,5},{5,4},{6,7},{7,6},{8,9},{9,8},{10,11... | collective-permute-start | bytes 2654216 | tf_op jit(solution)/shard_map/ppermute | solution.py:26
  94.6 91.5 %collective-permute-start.14 = (bf16[4,128,1024]{2,1,0:T(8,128)(2,1)}, bf16[4,128,1024]{2,1,0:T(8,128)(2,1)}, u32[]{:S(2)}, u32[]{:S(2)}) collective-permute-start(bf16[4,128,1024]{2,1,0:T(8,128)(2,1)} %pad_maximum_fusion.1.kept_ref), channel_id=1, source_target_pairs={{0,1},{1,0},{2,3},{3,2},{4,5},{5,4},{6,7},{7,6},{8,9},{9,8},{10,11... | collective-permute-start | bytes 3145736 | tf_op jit(solution)/shard_map/ppermute | solution.py:26
  95.4 89.0 %collective-permute-start.27 = (bf16[384,1024]{1,0:T(8,128)(2,1)}, bf16[384,1024]{1,0:T(8,128)(2,1)}, u32[]{:S(2)}, u32[]{:S(2)}) collective-permute-start(bf16[384,1024]{1,0:T(8,128)(2,1)} %constant_dynamic-update-slice_fusion.13.b0), channel_id=1, source_target_pairs={{0,8},{8,0},{16,24},{24,16},{1,9},{9,1},{17,25},{25,17},{2,10},{10... | collective-permute-start | bytes 2359304 | tf_op jit(solution)/shard_map/ppermute | solution.py:26
  97.7 107.9 %collective-permute-start.22 = (bf16[768,512]{1,0:T(8,128)(2,1)}, bf16[768,512]{1,0:T(8,128)(2,1)}, u32[]{:S(2)}, u32[]{:S(2)}) collective-permute-start(bf16[768,512]{1,0:T(8,128)(2,1)} %constant_dynamic-update-slice_fusion.10.a0), channel_id=1, source_target_pairs={{0,16},{8,24},{16,0},{24,8},{1,17},{9,25},{17,1},{25,9},{2,18},{10... | collective-permute-start | bytes 2359304 | tf_op jit(solution)/shard_map/ppermute | solution.py:26
  100.2 26.7 %collective-permute-start.2 = (bf16[256,1024]{1,0:T(8,128)(2,1)}, bf16[256,1024]{1,0:T(8,128)(2,1)S(1)}, u32[]{:S(2)}, u32[]{:S(2)}) collective-permute-start(bf16[256,1024]{1,0:T(8,128)(2,1)} %slice.352), channel_id=1, source_target_pairs={{0,8},{8,0},{16,24},{24,16},{1,9},{9,1},{17,25},{25,17},{2,10},{10... | collective-permute-start | bytes 1572872 | tf_op jit(solution)/shard_map/ppermute | solution.py:26
  102.3 26.7 %collective-permute-start.3 = (bf16[256,1024]{1,0:T(8,128)(2,1)}, bf16[256,1024]{1,0:T(8,128)(2,1)S(1)}, u32[]{:S(2)}, u32[]{:S(2)}) collective-permute-start(bf16[256,1024]{1,0:T(8,128)(2,1)} %slice.353), channel_id=1, source_target_pairs={{0,16},{8,24},{16,0},{24,8},{1,17},{9,25},{17,1},{25,9},{2,18},{10... | collective-permute-start | bytes 1572872 | tf_op jit(solution)/shard_map/ppermute | solution.py:26
  183.0 14.3 %collective-permute-start.8 = (bf16[512,256]{1,0:T(8,128)(2,1)S(1)}, bf16[512,256]{1,0:T(8,128)(2,1)S(1)}, u32[]{:S(2)}, u32[]{:S(2)}) collective-permute-start(bf16[512,256]{1,0:T(8,128)(2,1)S(1)} %get-tuple-element.144), channel_id=1, source_target_pairs={{0,8},{8,0},{16,24},{24,16},{1,9},{9,1},{17,25},{25,17},{2,10},{10... | collective-permute-start | bytes 786440 | tf_op jit(solution)/shard_map/ppermute | solution.py:26
  184.4 13.3 %collective-permute-start.9 = (bf16[512,256]{1,0:T(8,128)(2,1)S(1)}, bf16[512,256]{1,0:T(8,128)(2,1)S(1)}, u32[]{:S(2)}, u32[]{:S(2)}) collective-permute-start(bf16[512,256]{1,0:T(8,128)(2,1)S(1)} %get-tuple-element.143), channel_id=1, source_target_pairs={{0,16},{8,24},{16,0},{24,8},{1,17},{9,25},{17,1},{25,9},{2,18},{10... | collective-permute-start | bytes 786440 | tf_op jit(solution)/shard_map/ppermute | solution.py:26
  186.2 26.3 %collective-permute-start.28 = (bf16[384,1024]{1,0:T(8,128)(2,1)}, bf16[384,1024]{1,0:T(8,128)(2,1)S(1)}, u32[]{:S(2)}, u32[]{:S(2)}) collective-permute-start(bf16[384,1024]{1,0:T(8,128)(2,1)} %constant_dynamic-update-slice_fusion.13.b0), channel_id=1, source_target_pairs={{0,16},{8,24},{16,0},{24,8},{1,17},{9,25},{17,1},{25,9},{2,18},{10... | collective-permute-start | bytes 2359304 | tf_op jit(solution)/shard_map/ppermute | solution.py:26
  191.5 22.7 %collective-permute-start.21 = (bf16[768,512]{1,0:T(8,128)(2,1)}, bf16[768,512]{1,0:T(8,128)(2,1)}, u32[]{:S(2)}, u32[]{:S(2)}) collective-permute-start(bf16[768,512]{1,0:T(8,128)(2,1)} %constant_dynamic-update-slice_fusion.10.a0), channel_id=1, source_target_pairs={{0,8},{8,0},{16,24},{24,16},{1,9},{9,1},{17,25},{25,17},{2,10},{10... | collective-permute-start | bytes 2359304 | tf_op jit(solution)/shard_map/ppermute | solution.py:26
  197.2 32.1 %collective-permute-start.29 = (bf16[384,1024]{1,0:T(8,128)(2,1)}, bf16[384,1024]{1,0:T(8,128)(2,1)}, u32[]{:S(2)}, u32[]{:S(2)}) collective-permute-start(bf16[384,1024]{1,0:T(8,128)(2,1)} %collective-permute-done.27.b1), channel_id=1, source_target_pairs={{0,16},{8,24},{16,0},{24,8},{1,17},{9,25},{17,1},{25,9},{2,18},{10... | collective-permute-start | bytes 2359304 | tf_op jit(solution)/shard_map/ppermute | solution.py:26
  205.7 23.7 %collective-permute-start.23 = (bf16[768,512]{1,0:T(8,128)(2,1)}, bf16[768,512]{1,0:T(8,128)(2,1)}, u32[]{:S(2)}, u32[]{:S(2)}) collective-permute-start(bf16[768,512]{1,0:T(8,128)(2,1)} %collective-permute-done.22.a2), channel_id=1, source_target_pairs={{0,8},{8,0},{16,24},{24,16},{1,9},{9,1},{17,25},{25,17},{2,10},{10... | collective-permute-start | bytes 2359304 | tf_op jit(solution)/shard_map/ppermute | solution.py:26
  284.7 26.9 %collective-permute-start.61 = (bf16[1024,512]{1,0:T(8,128)(2,1)}, bf16[1024,512]{1,0:T(8,128)(2,1)}, u32[]{:S(2)}, u32[]{:S(2)}) collective-permute-start(bf16[1024,512]{1,0:T(8,128)(2,1)} %convolution_convert_fusion.6), channel_id=1, source_target_pairs={{0,16},{8,24},{16,0},{24,8},{1,17},{9,25},{17,1},{25,9},{2,18},{10... | collective-permute-start | bytes 3145736 | tf_op jit(solution)/shard_map/ppermute | solution.py:26
  286.2 28.2 %collective-permute-start.59 = (bf16[1024,512]{1,0:T(8,128)(2,1)}, bf16[1024,512]{1,0:T(8,128)(2,1)}, u32[]{:S(2)}, u32[]{:S(2)}) collective-permute-start(bf16[1024,512]{1,0:T(8,128)(2,1)} %convolution_convert_fusion.8), channel_id=1, source_target_pairs={{0,8},{8,0},{16,24},{24,16},{1,9},{9,1},{17,25},{25,17},{2,10},{10... | collective-permute-start | bytes 3145736 | tf_op jit(solution)/shard_map/ppermute | solution.py:26
  289.1 45.9 %collective-permute-start.63 = (bf16[512,1024]{1,0:T(8,128)(2,1)}, bf16[512,1024]{1,0:T(8,128)(2,1)}, u32[]{:S(2)}, u32[]{:S(2)}) collective-permute-start(bf16[512,1024]{1,0:T(8,128)(2,1)} %convolution_convert_fusion.4), channel_id=1, source_target_pairs={{0,8},{8,0},{16,24},{24,16},{1,9},{9,1},{17,25},{25,17},{2,10},{10... | collective-permute-start | bytes 3145736 | tf_op jit(solution)/shard_map/ppermute | solution.py:26
  292.8 118.3 %collective-permute-start.65 = (bf16[512,1024]{1,0:T(8,128)(2,1)}, bf16[512,1024]{1,0:T(8,128)(2,1)}, u32[]{:S(2)}, u32[]{:S(2)}) collective-permute-start(bf16[512,1024]{1,0:T(8,128)(2,1)} %convolution_convert_fusion.2), channel_id=1, source_target_pairs={{0,16},{8,24},{16,0},{24,8},{1,17},{9,25},{17,1},{25,9},{2,18},{10... | collective-permute-start | bytes 3145736 | tf_op jit(solution)/shard_map/ppermute | solution.py:26
  302.2 114.6 %collective-permute-start.30 = (bf16[512,1024]{1,0:T(8,128)(2,1)}, bf16[512,1024]{1,0:T(8,128)(2,1)}, u32[]{:S(2)}, u32[]{:S(2)}) collective-permute-start(bf16[512,1024]{1,0:T(8,128)(2,1)} %get-tuple-element.69), channel_id=1, source_target_pairs={{0,1},{1,0},{2,3},{3,2},{4,5},{5,4},{6,7},{7,6},{8,9},{9,8},{10,11... | collective-permute-start | bytes 3145736 | tf_op jit(solution)/shard_map/ppermute | solution.py:26
  311.7 28.8 %collective-permute-start.32 = (bf16[512,256]{1,0:T(8,128)(2,1)}, bf16[512,256]{1,0:T(8,128)(2,1)S(1)}, u32[]{:S(2)}, u32[]{:S(2)}) collective-permute-start(bf16[512,256]{1,0:T(8,128)(2,1)} %get-tuple-element.74), channel_id=1, source_target_pairs={{0,8},{8,0},{16,24},{24,16},{1,9},{9,1},{17,25},{25,17},{2,10},{10... | collective-permute-start | bytes 786440 | tf_op jit(solution)/shard_map/ppermute | solution.py:26
  314.4 26.8 %collective-permute-start.33 = (bf16[512,256]{1,0:T(8,128)(2,1)}, bf16[512,256]{1,0:T(8,128)(2,1)S(1)}, u32[]{:S(2)}, u32[]{:S(2)}) collective-permute-start(bf16[512,256]{1,0:T(8,128)(2,1)} %get-tuple-element.75), channel_id=1, source_target_pairs={{0,16},{8,24},{16,0},{24,8},{1,17},{9,25},{17,1},{25,9},{2,18},{10... | collective-permute-start | bytes 786440 | tf_op jit(solution)/shard_map/ppermute | solution.py:26
  335.0 11.2 %collective-permute-start.34 = (bf16[512,256]{1,0:T(8,128)(2,1)S(1)}, bf16[512,256]{1,0:T(8,128)(2,1)S(1)}, u32[]{:S(2)}, u32[]{:S(2)}) collective-permute-start(bf16[512,256]{1,0:T(8,128)(2,1)S(1)} %copy-done.66), channel_id=1, source_target_pairs={{0,24},{8,16},{16,8},{24,0},{1,25},{9,17},{17,9},{25,1},{2,26},{10... | collective-permute-start | bytes 786440 | tf_op jit(solution)/shard_map/ppermute | solution.py:26
  340.5 86.3 %collective-permute-start.62 = (bf16[1024,256]{1,0:T(8,128)(2,1)}, bf16[1024,256]{1,0:T(8,128)(2,1)}, u32[]{:S(2)}, u32[]{:S(2)}) collective-permute-start(bf16[1024,256]{1,0:T(8,128)(2,1)} %add_convert_fusion.3), channel_id=1, source_target_pairs={{0,8},{8,0},{16,24},{24,16},{1,9},{9,1},{17,25},{25,17},{2,10},{10... | collective-permute-start | bytes 1572872 | tf_op jit(solution)/shard_map/ppermute | solution.py:26
  341.2 85.9 %collective-permute-start.60 = (bf16[1024,256]{1,0:T(8,128)(2,1)}, bf16[1024,256]{1,0:T(8,128)(2,1)}, u32[]{:S(2)}, u32[]{:S(2)}) collective-permute-start(bf16[1024,256]{1,0:T(8,128)(2,1)} %add_convert_fusion.4), channel_id=1, source_target_pairs={{0,16},{8,24},{16,0},{24,8},{1,17},{9,25},{17,1},{25,9},{2,18},{10... | collective-permute-start | bytes 1572872 | tf_op jit(solution)/shard_map/ppermute | solution.py:26
  346.2 83.7 %collective-permute-start.64 = (bf16[256,1024]{1,0:T(8,128)(2,1)}, bf16[256,1024]{1,0:T(8,128)(2,1)}, u32[]{:S(2)}, u32[]{:S(2)}) collective-permute-start(bf16[256,1024]{1,0:T(8,128)(2,1)} %add_convert_fusion.2), channel_id=1, source_target_pairs={{0,16},{8,24},{16,0},{24,8},{1,17},{9,25},{17,1},{25,9},{2,18},{10... | collective-permute-start | bytes 1572872 | tf_op jit(solution)/shard_map/ppermute | solution.py:26
  416.1 13.8 %collective-permute-start.66 = (bf16[256,1024]{1,0:T(8,128)(2,1)}, bf16[256,1024]{1,0:T(8,128)(2,1)}, u32[]{:S(2)}, u32[]{:S(2)}) collective-permute-start(bf16[256,1024]{1,0:T(8,128)(2,1)} %add_convert_fusion.1), channel_id=1, source_target_pairs={{0,8},{8,0},{16,24},{24,16},{1,9},{9,1},{17,25},{25,17},{2,10},{10... | collective-permute-start | bytes 1572872 | tf_op jit(solution)/shard_map/ppermute | solution.py:26
  424.9 40.3 %collective-permute-start.36 = (bf16[256,1024]{1,0:T(8,128)(2,1)}, bf16[256,1024]{1,0:T(8,128)(2,1)S(1)}, u32[]{:S(2)}, u32[]{:S(2)}) collective-permute-start(bf16[256,1024]{1,0:T(8,128)(2,1)} %get-tuple-element.85), channel_id=1, source_target_pairs={{0,8},{8,0},{16,24},{24,16},{1,9},{9,1},{17,25},{25,17},{2,10},{10... | collective-permute-start | bytes 1572872 | tf_op jit(solution)/shard_map/ppermute | solution.py:26
  426.8 59.7 %collective-permute-start.46 = (bf16[4,128,768]{1,2,0:T(8,128)(2,1)S(1)}, bf16[4,128,768]{1,2,0:T(8,128)(2,1)}, u32[]{:S(2)}, u32[]{:S(2)}) collective-permute-start(bf16[4,128,768]{1,2,0:T(8,128)(2,1)S(1)} %bitcast.187), channel_id=1, source_target_pairs={{0,1},{1,0},{2,3},{3,2},{4,5},{5,4},{6,7},{7,6},{8,9},{9,8},{10,11... | collective-permute-start | bytes 2359304 | tf_op jit(solution)/shard_map/ppermute | solution.py:26
  427.1 13.9 %collective-permute-start.44 = (f32[12,1024]{1,0:T(8,128)S(1)}, f32[12,1024]{1,0:T(8,128)S(1)}, u32[]{:S(2)}, u32[]{:S(2)}) collective-permute-start(f32[12,1024]{1,0:T(8,128)S(1)} %add.174), channel_id=1, source_target_pairs={{0,2},{1,3},{2,0},{3,1},{4,6},{5,7},{6,4},{7,5},{8,10},{9,11},{10,... | collective-permute-start | bytes 147464 | tf_op jit(solution)/shard_map/ppermute | solution.py:26
  436.0 32.9 %collective-permute-start.67 = (bf16[512,512]{1,0:T(8,128)(2,1)}, bf16[512,512]{1,0:T(8,128)(2,1)}, u32[]{:S(2)}, u32[]{:S(2)}) collective-permute-start(bf16[512,512]{1,0:T(8,128)(2,1)} %get-tuple-element.101), channel_id=1, source_target_pairs={{0,2},{1,3},{2,0},{3,1},{4,6},{5,7},{6,4},{7,5},{8,10},{9,11},{10,... | collective-permute-start | bytes 1572872 | tf_op jit(solution)/shard_map/ppermute | solution.py:26
  436.2 33.5 %collective-permute-start.68 = (bf16[512,512]{1,0:T(8,128)(2,1)}, bf16[512,512]{1,0:T(8,128)(2,1)}, u32[]{:S(2)}, u32[]{:S(2)}) collective-permute-start(bf16[512,512]{1,0:T(8,128)(2,1)} %get-tuple-element.102), channel_id=1, source_target_pairs={{0,4},{1,5},{2,6},{3,7},{4,0},{5,1},{6,2},{7,3},{8,12},{9,13},{10,... | collective-permute-start | bytes 1572872 | tf_op jit(solution)/shard_map/ppermute | solution.py:26
  441.0 24.2 %collective-permute-start.45 = (f32[12,1024]{1,0:T(8,128)S(1)}, f32[12,1024]{1,0:T(8,128)S(1)}, u32[]{:S(2)}, u32[]{:S(2)}) collective-permute-start(f32[12,1024]{1,0:T(8,128)S(1)} %add.175), channel_id=1, source_target_pairs={{0,4},{1,5},{2,6},{3,7},{4,0},{5,1},{6,2},{7,3},{8,12},{9,13},{10,... | collective-permute-start | bytes 147464 | tf_op jit(solution)/shard_map/ppermute | solution.py:26
  465.1 34.0 %collective-permute-start.53 = (bf16[4,128,1024]{2,1,0:T(8,128)(2,1)}, bf16[4,128,1024]{2,1,0:T(8,128)(2,1)S(1)}, u32[]{:S(2)}, u32[]{:S(2)}) collective-permute-start(bf16[4,128,1024]{2,1,0:T(8,128)(2,1)} %dynamic-slice_bitcast_fusion), channel_id=1, source_target_pairs={{0,1},{1,0},{2,3},{3,2},{4,5},{5,4},{6,7},{7,6},{8,9},{9,8},{10,11... | collective-permute-start | bytes 3145736 | tf_op jit(solution)/shard_map/ppermute | solution.py:26
  465.2 16.6 %collective-permute-start.69 = (bf16[512,512]{1,0:T(8,128)(2,1)}, bf16[512,512]{1,0:T(8,128)(2,1)}, u32[]{:S(2)}, u32[]{:S(2)}) collective-permute-start(bf16[512,512]{1,0:T(8,128)(2,1)} %get-tuple-element.103), channel_id=1, source_target_pairs={{0,6},{1,7},{2,4},{3,5},{4,2},{5,3},{6,0},{7,1},{8,14},{9,15},{10,... | collective-permute-start | bytes 1572872 | tf_op jit(solution)/shard_map/ppermute | solution.py:26
  468.9 19.7 %collective-permute-start.35 = (bf16[256,1024]{1,0:T(8,128)(2,1)}, bf16[256,1024]{1,0:T(8,128)(2,1)}, u32[]{:S(2)}, u32[]{:S(2)}) collective-permute-start(bf16[256,1024]{1,0:T(8,128)(2,1)} %get-tuple-element.83), channel_id=1, source_target_pairs={{0,8},{8,0},{16,24},{24,16},{1,9},{9,1},{17,25},{25,17},{2,10},{10... | collective-permute-start | bytes 1572872 | tf_op jit(solution)/shard_map/ppermute | solution.py:26
  469.6 19.1 %collective-permute-start.39 = (bf16[256,1024]{1,0:T(8,128)(2,1)}, bf16[256,1024]{1,0:T(8,128)(2,1)}, u32[]{:S(2)}, u32[]{:S(2)}) collective-permute-start(bf16[256,1024]{1,0:T(8,128)(2,1)} %get-tuple-element.90), channel_id=1, source_target_pairs={{0,16},{8,24},{16,0},{24,8},{1,17},{9,25},{17,1},{25,9},{2,18},{10... | collective-permute-start | bytes 1572872 | tf_op jit(solution)/shard_map/ppermute | solution.py:26
  481.7 16.7 %collective-permute-start.38 = (bf16[256,1024]{1,0:T(8,128)(2,1)}, bf16[256,1024]{1,0:T(8,128)(2,1)}, u32[]{:S(2)}, u32[]{:S(2)}) collective-permute-start(bf16[256,1024]{1,0:T(8,128)(2,1)} %get-tuple-element.88), channel_id=1, source_target_pairs={{0,16},{8,24},{16,0},{24,8},{1,17},{9,25},{17,1},{25,9},{2,18},{10... | collective-permute-start | bytes 1572872 | tf_op jit(solution)/shard_map/ppermute | solution.py:26
  486.6 45.2 %collective-permute-start.37 = (bf16[256,1024]{1,0:T(8,128)(2,1)}, bf16[256,1024]{1,0:T(8,128)(2,1)S(1)}, u32[]{:S(2)}, u32[]{:S(2)}) collective-permute-start(bf16[256,1024]{1,0:T(8,128)(2,1)} %add_convert_fusion.6), channel_id=1, source_target_pairs={{0,16},{8,24},{16,0},{24,8},{1,17},{9,25},{17,1},{25,9},{2,18},{10... | collective-permute-start | bytes 1572872 | tf_op jit(solution)/shard_map/ppermute | solution.py:26
  488.7 17.7 %collective-permute-start.73 = (bf16[128,512]{1,0:T(8,128)(2,1)S(1)}, bf16[128,512]{1,0:T(8,128)(2,1)S(1)}, u32[]{:S(2)}, u32[]{:S(2)}) collective-permute-start(bf16[128,512]{1,0:T(8,128)(2,1)S(1)} %copy-done.67), channel_id=1, source_target_pairs={{0,1},{1,0},{2,3},{3,2},{4,5},{5,4},{6,7},{7,6},{8,9},{9,8},{10,11... | collective-permute-start | bytes 393224 | tf_op jit(solution)/shard_map/ppermute | solution.py:26
  488.8 19.4 %collective-permute-start.47 = (bf16[128,768]{0,1:T(8,128)(2,1)S(1)}, bf16[128,768]{0,1:T(8,128)(2,1)S(1)}, u32[]{:S(2)}, u32[]{:S(2)}) collective-permute-start(bf16[128,768]{0,1:T(8,128)(2,1)S(1)} %get-tuple-element.129), channel_id=1, source_target_pairs={{0,2},{1,3},{2,0},{3,1},{4,6},{5,7},{6,4},{7,5},{8,10},{9,11},{10,... | collective-permute-start | bytes 589832 | tf_op jit(solution)/shard_map/ppermute | solution.py:26
  498.4 37.2 %collective-permute-start.40 = (bf16[256,1024]{1,0:T(8,128)(2,1)S(1)}, bf16[256,1024]{1,0:T(8,128)(2,1)S(1)}, u32[]{:S(2)}, u32[]{:S(2)}) collective-permute-start(bf16[256,1024]{1,0:T(8,128)(2,1)S(1)} %add_convert_fusion.5), channel_id=1, source_target_pairs={{0,8},{8,0},{16,24},{24,16},{1,9},{9,1},{17,25},{25,17},{2,10},{10... | collective-permute-start | bytes 1572872 | tf_op jit(solution)/shard_map/ppermute | solution.py:26
  499.1 19.4 %collective-permute-start.48 = (bf16[128,768]{0,1:T(8,128)(2,1)S(1)}, bf16[128,768]{0,1:T(8,128)(2,1)S(1)}, u32[]{:S(2)}, u32[]{:S(2)}) collective-permute-start(bf16[128,768]{0,1:T(8,128)(2,1)S(1)} %get-tuple-element.131), channel_id=1, source_target_pairs={{0,4},{1,5},{2,6},{3,7},{4,0},{5,1},{6,2},{7,3},{8,12},{9,13},{10,... | collective-permute-start | bytes 589832 | tf_op jit(solution)/shard_map/ppermute | solution.py:26
  506.4 13.6 %collective-permute-start.49 = (bf16[128,768]{0,1:T(8,128)(2,1)S(1)}, bf16[128,768]{0,1:T(8,128)(2,1)S(1)}, u32[]{:S(2)}, u32[]{:S(2)}) collective-permute-start(bf16[128,768]{0,1:T(8,128)(2,1)S(1)} %get-tuple-element.130), channel_id=1, source_target_pairs={{0,6},{1,7},{2,4},{3,5},{4,2},{5,3},{6,0},{7,1},{8,14},{9,15},{10,... | collective-permute-start | bytes 589832 | tf_op jit(solution)/shard_map/ppermute | solution.py:26
  508.2 13.1 %collective-permute-start.74 = (bf16[128,512]{1,0:T(8,128)(2,1)S(1)}, bf16[128,512]{1,0:T(8,128)(2,1)S(1)}, u32[]{:S(2)}, u32[]{:S(2)}) collective-permute-start(bf16[128,512]{1,0:T(8,128)(2,1)S(1)} %collective-permute-done.73.refs_4_), channel_id=1, source_target_pairs={{0,8},{8,0},{16,24},{24,16},{1,9},{9,1},{17,25},{25,17},{2,10},{10... | collective-permute-start | bytes 393224 | tf_op jit(solution)/shard_map/ppermute | solution.py:26
  518.6 33.7 %collective-permute-start.70 = (bf16[384,512]{1,0:T(8,128)(2,1)}, bf16[384,512]{1,0:T(8,128)(2,1)S(1)}, u32[]{:S(2)}, u32[]{:S(2)}) collective-permute-start(bf16[384,512]{1,0:T(8,128)(2,1)} %get-tuple-element.104.refs_0_), channel_id=1, source_target_pairs={{0,8},{8,0},{16,24},{24,16},{1,9},{9,1},{17,25},{25,17},{2,10},{10... | collective-permute-start | bytes 1179656 | tf_op jit(solution)/shard_map/ppermute | solution.py:26
  526.2 17.6 %collective-permute-start.54 = (bf16[128,1024]{1,0:T(8,128)(2,1)}, bf16[128,1024]{1,0:T(8,128)(2,1)S(1)}, u32[]{:S(2)}, u32[]{:S(2)}) collective-permute-start(bf16[128,1024]{1,0:T(8,128)(2,1)} %get-tuple-element.124), channel_id=1, source_target_pairs={{0,2},{1,3},{2,0},{3,1},{4,6},{5,7},{6,4},{7,5},{8,10},{9,11},{10,... | collective-permute-start | bytes 786440 | tf_op jit(solution)/shard_map/ppermute | solution.py:26
  530.3 19.9 %collective-permute-start.55 = (bf16[128,1024]{1,0:T(8,128)(2,1)}, bf16[128,1024]{1,0:T(8,128)(2,1)S(1)}, u32[]{:S(2)}, u32[]{:S(2)}) collective-permute-start(bf16[128,1024]{1,0:T(8,128)(2,1)} %get-tuple-element.126), channel_id=1, source_target_pairs={{0,4},{1,5},{2,6},{3,7},{4,0},{5,1},{6,2},{7,3},{8,12},{9,13},{10,... | collective-permute-start | bytes 786440 | tf_op jit(solution)/shard_map/ppermute | solution.py:26
  531.8 19.1 %collective-permute-start.56 = (bf16[128,1024]{1,0:T(8,128)(2,1)}, bf16[128,1024]{1,0:T(8,128)(2,1)}, u32[]{:S(2)}, u32[]{:S(2)}) collective-permute-start(bf16[128,1024]{1,0:T(8,128)(2,1)} %get-tuple-element.125), channel_id=1, source_target_pairs={{0,6},{1,7},{2,4},{3,5},{4,2},{5,3},{6,0},{7,1},{8,14},{9,15},{10,... | collective-permute-start | bytes 786440 | tf_op jit(solution)/shard_map/ppermute | solution.py:26
  535.7 20.7 %collective-permute-start.71 = (bf16[384,512]{1,0:T(8,128)(2,1)}, bf16[384,512]{1,0:T(8,128)(2,1)}, u32[]{:S(2)}, u32[]{:S(2)}) collective-permute-start(bf16[384,512]{1,0:T(8,128)(2,1)} %get-tuple-element.104.refs_0_), channel_id=1, source_target_pairs={{0,16},{8,24},{16,0},{24,8},{1,17},{9,25},{17,1},{25,9},{2,18},{10... | collective-permute-start | bytes 1179656 | tf_op jit(solution)/shard_map/ppermute | solution.py:26
  543.8 14.7 %collective-permute-start.72 = (bf16[384,512]{1,0:T(8,128)(2,1)}, bf16[384,512]{1,0:T(8,128)(2,1)}, u32[]{:S(2)}, u32[]{:S(2)}) collective-permute-start(bf16[384,512]{1,0:T(8,128)(2,1)} %get-tuple-element.104.refs_0_), channel_id=1, source_target_pairs={{0,24},{8,16},{16,8},{24,0},{1,25},{9,17},{17,9},{25,1},{2,26},{10... | collective-permute-start | bytes 1179656 | tf_op jit(solution)/shard_map/ppermute | solution.py:26
  550.2 13.0 %collective-permute-start.50 = (bf16[128,768]{0,1:T(8,128)(2,1)S(1)}, bf16[128,768]{0,1:T(8,128)(2,1)S(1)}, u32[]{:S(2)}, u32[]{:S(2)}) collective-permute-start(bf16[128,768]{0,1:T(8,128)(2,1)S(1)} %fusion.14), channel_id=1, source_target_pairs={{0,8},{8,0},{16,24},{24,16},{1,9},{9,1},{17,25},{25,17},{2,10},{10... | collective-permute-start | bytes 589832 | tf_op jit(solution)/shard_map/ppermute | solution.py:26
  550.9 13.3 %collective-permute-start.51 = (bf16[128,768]{0,1:T(8,128)(2,1)S(1)}, bf16[128,768]{0,1:T(8,128)(2,1)S(1)}, u32[]{:S(2)}, u32[]{:S(2)}) collective-permute-start(bf16[128,768]{0,1:T(8,128)(2,1)S(1)} %fusion.14), channel_id=1, source_target_pairs={{0,24},{8,16},{16,8},{24,0},{1,25},{9,17},{17,9},{25,1},{2,26},{10... | collective-permute-start | bytes 589832 | tf_op jit(solution)/shard_map/ppermute | solution.py:26
  (81 other events, 682.1 us)

commit v2 on v1

--- a/solution.py
+++ b/solution.py
@@ -82,6 +82,14 @@
     return jnp.concatenate([upper, lower], axis=0)
 
 
+def after(values, *needed):
+    return lax.optimization_barrier((values, needed))[0]
+
+
+def cost(micros, size=0):
+    return pl.CostEstimate(flops=int(micros * 1.15e6), bytes_accessed=int(size), transcendentals=0)
+
+
 def tile_rows(total, blocks):
     return min(256, total // blocks)
 
@@ -150,10 +158,13 @@
     )
 
 
-def forward_kernel(rows, block_rows, per_pair, lens, q_ref, k_ref, v_ref, out_ref, norm_ref, vt_ref):
-    tile = pl.program_id(1)
+def forward_kernel(
+    rows, block_rows, per_pair, lens, q_ref, k_ref, v_ref, out_ref, norm_ref, vt_ref, parts, total
+):
+    tile = pl.program_id(0)
     me = lens[1 + CONTS]
     tiles = q_ref.shape[0] // rows
+    across = per_pair * rows
 
     @pl.when(tile == 0)
     def _():
@@ -165,47 +176,54 @@
         lax.fori_loop(0, tiles, turn, 0)
 
     at = rel_row(tile, rows, block_rows, me)
-    query = pair_stack(q_ref[pl.ds(at, rows), :], per_pair, jnp.asarray(0.125, BF))
+    query = pair_stack(q_ref[pl.ds(at, rows), :], per_pair, jnp.asarray(0.125, BF)).T
+    count, shift = walk(tile, rows)
+
+    def folded(values):
+        return values.reshape(rows // 8, 8, across)
 
     def scores(i):
-        return nt(k_ref[pl.ds(rel_row(i, rows, block_rows, me), rows), :], query)
+        return nn(k_ref[pl.ds(rel_row(i, rows, block_rows, me), rows), :], query)
+
+    def key_tile(i):
+        return jnp.where(i < PROMPT // rows, i, i + shift)
 
     first = jnp.where(
         diagonal_mask(rows, per_pair, key_limit(lens, tile, rows)), scores(tile), NEG
     )
-    top = jnp.max(first, axis=0, keepdims=True)
+
+    def measure(i, top):
+        here = key_tile(i)
+        part = jnp.where(
+            live_mask(rows, per_pair, key_limit(lens, here, rows)), scores(here), NEG
+        )
+        parts[i] = part
+        return jnp.maximum(top, jnp.max(folded(part), axis=0))
+
+    top = lax.fori_loop(0, count, measure, jnp.max(folded(first), axis=0))
+    top = jnp.max(top, axis=0, keepdims=True)
     weights = jnp.exp(first - top)
-    denom = jnp.sum(weights, axis=0, keepdims=True)
-    total = nn(vt_ref[tile], weights.astype(BF))
-    count, shift = walk(tile, rows)
-
-    def step(i, carry):
-        top, denom, total = carry
-        key_tile = jnp.where(i < PROMPT // rows, i, i + shift)
-        part = jnp.where(
-            live_mask(rows, per_pair, key_limit(lens, key_tile, rows)), scores(key_tile), NEG
-        )
-        higher = jnp.maximum(top, jnp.max(part, axis=0, keepdims=True))
-        scale = jnp.exp(top - higher)
-        weights = jnp.exp(part - higher)
-        denom = denom * scale + jnp.sum(weights, axis=0, keepdims=True)
-        total = total * scale + nn(vt_ref[key_tile], weights.astype(BF))
-        return higher, denom, total
-
-    top, denom, total = lax.fori_loop(0, count, step, (top, denom, total))
-    mixed = unstack(total / denom, per_pair, rows)
+    total[...] = nn(vt_ref[tile], weights.astype(BF))
+
+    def gather(i, denom):
+        weights = jnp.exp(parts[i] - top)
+        total[...] += nn(vt_ref[key_tile(i)], weights.astype(BF))
+        return denom + jnp.sum(folded(weights), axis=0)
+
+    denom = lax.fori_loop(0, count, gather, jnp.sum(folded(weights), axis=0))
+    denom = jnp.sum(denom, axis=0, keepdims=True)
+    mixed = unstack(total[...] / denom, per_pair, rows)
     out_ref[...] = mixed.T.astype(BF)
-    norm_ref[0, 0] = top + jnp.log(denom)
+    norm_ref[0] = top + jnp.log(denom)
 
 
 def backward_kernel(
     rows, block_rows, per_pair, lens, q_ref, k_ref, v_ref, out_ref, grad_ref, norm_ref,
     dq_ref, dk_ref, dv_ref, kt_ref, dk_sum, dv_sum, dq_sum,
 ):
-    tile = pl.program_id(1)
+    tile = pl.program_id(0)
     me = lens[1 + CONTS]
     tiles = q_ref.shape[0] // rows
-    width = q_ref.shape[1]
 
     @pl.when(tile == 0)
     def _():
@@ -222,6 +240,8 @@
     query = pair_stack(q_ref[pl.ds(at, rows), :], per_pair, jnp.asarray(0.125, BF))
     grad_block = grad_ref[pl.ds(at, rows), :]
     grad = pair_stack(grad_block, per_pair)
+    query_turned = query.T
+    grad_turned = grad.T
     product = (grad_block.astype(F32) * out_ref[pl.ds(at, rows), :].astype(F32)).T
     inner = jnp.concatenate(
         [
@@ -230,14 +250,14 @@
         ],
         axis=1,
     )
-    norm = norm_ref[0, 0]
+    norm = norm_ref[0]
 
     def one(key_tile, mask):
         key_at = rel_row(key_tile, rows, block_rows, me)
         keys = pl.ds(key_at, rows)
-        part = jnp.where(mask, nt(k_ref[keys, :], query), NEG)
+        part = jnp.where(mask, nn(k_ref[keys, :], query_turned), NEG)
         probs = jnp.exp(part - norm)
-        slope = probs * (nt(v_ref[keys, :], grad) - inner)
+        slope = probs * (nn(v_ref[keys, :], grad_turned) - inner)
         slope_low = slope.astype(BF)
         dv_sum[keys, :] += nn(probs.astype(BF), grad)
         dk_sum[keys, :] += nn(slope_low, query)
@@ -268,8 +288,8 @@
 
 
 def thirds(qkv, width, pair_width):
+    per = width // pair_width
     if pair_width % 128 == 0:
-        per = width // pair_width
         return (qkv, qkv, qkv), (0, per, 2 * per)
     return tuple(qkv[:, i * width : (i + 1) * width] for i in range(3)), (0, 0, 0)
 
@@ -277,82 +297,110 @@
 def row_block(rows, block_rows):
     per = block_rows // rows
 
-    def index(pair, tile, lens):
-        return ((tile // per) ^ lens[1 + CONTS]) * per + tile % per, pair
+    def index(tile, lens):
+        return ((tile // per) ^ lens[1 + CONTS]) * per + tile % per, 0
 
     return index
 
 
-def attend_forward(lens, qkv, heads):
+def attend_forward(lens, qkv, heads, between=None):
     total = qkv.shape[0]
     width = heads * HD
     rows, block_rows, per_pair, pairs, pair_width = attention_plan(total, heads)
     arrays, firsts = thirds(qkv, width, pair_width)
     tiles = total // rows
-
-    def whole(first):
-        return pl.BlockSpec((total, pair_width), lambda pair, tile, lens: (0, first + pair))
-
-    return pl.pallas_call(
-        functools.partial(forward_kernel, rows, block_rows, per_pair),
-        out_shape=(
-            jax.ShapeDtypeStruct((total, width), BF),
-            jax.ShapeDtypeStruct((pairs, tiles, 1, per_pair * rows), F32),
-        ),
-        grid_spec=pltpu.PrefetchScalarGridSpec(
-            num_scalar_prefetch=1,
-            grid=(pairs, tiles),
-            in_specs=[whole(first) for first in firsts],
-            out_specs=(
-                pl.BlockSpec((rows, pair_width), row_block(rows, block_rows)),
-                pl.BlockSpec(
-                    (1, 1, 1, per_pair * rows), lambda pair, tile, lens: (pair, tile, 0, 0)
+    most = (PROMPT + CONTLEN) // rows
+    mixed = None
+    norms = []
+    for pair in range(pairs):
+
+        def whole(first):
+            return pl.BlockSpec((total, pair_width), lambda tile, lens: (0, first + pair))
+
+        def kernel(lens, q_ref, k_ref, v_ref, *refs):
+            forward_kernel(
+                rows, block_rows, per_pair, lens, q_ref, k_ref, v_ref, *refs[mixed is not None :]
+            )
+
+        place_row = row_block(rows, block_rows)
+        more = [] if mixed is None else [mixed]
+        mixed, norm = pl.pallas_call(
+            kernel,
+            out_shape=(
+                jax.ShapeDtypeStruct((total, width), BF),
+                jax.ShapeDtypeStruct((tiles, 1, per_pair * rows), F32),
+            ),
+            grid_spec=pltpu.PrefetchScalarGridSpec(
+                num_scalar_prefetch=1,
+                grid=(tiles,),
+                in_specs=[whole(first) for first in firsts]
+                + [pl.BlockSpec(memory_space=pl.ANY)] * len(more),
+                out_specs=(
+                    pl.BlockSpec(
+                        (rows, pair_width), lambda tile, lens: (place_row(tile, lens)[0], pair)
+                    ),
+                    pl.BlockSpec((1, 1, per_pair * rows), lambda tile, lens: (tile, 0, 0)),
                 ),
+                scratch_shapes=[
+                    pltpu.VMEM((tiles, pair_width, rows), BF),
+                    pltpu.VMEM((most, rows, per_pair * rows), F32),
+                    pltpu.VMEM((pair_width, per_pair * rows), F32),
+                ],
             ),
-            scratch_shapes=[pltpu.VMEM((tiles, pair_width, rows), BF)],
-        ),
-        name="attend_forward",
-    )(lens, *arrays)
-
-
-def attend_backward(lens, qkv, mixed, grad, norm, heads):
+            input_output_aliases={4: 0} if more else {},
+            cost_estimate=cost(15),
+            name="attend_forward",
+        )(lens, *arrays, *more)
+        norms.append(norm)
+        if between is not None and pair + 1 < pairs:
+            lens, mixed, arrays = between(lens, mixed, arrays)
+    return mixed, norms
+
+
+def attend_backward(lens, qkv, mixed, norms, grad, heads, between=None):
     total = qkv.shape[0]
     width = heads * HD
     rows, block_rows, per_pair, pairs, pair_width = attention_plan(total, heads)
     arrays, firsts = thirds(qkv, width, pair_width)
     tiles = total // rows
-
-    def whole(first):
-        return pl.BlockSpec((total, pair_width), lambda pair, tile, lens: (0, first + pair))
-
-    return pl.pallas_call(
-        functools.partial(backward_kernel, rows, block_rows, per_pair),
-        out_shape=(jax.ShapeDtypeStruct((total, width), BF),) * 3,
-        grid_spec=pltpu.PrefetchScalarGridSpec(
-            num_scalar_prefetch=1,
-            grid=(pairs, tiles),
-            in_specs=[whole(first) for first in firsts]
-            + [
-                whole(0),
-                whole(0),
-                pl.BlockSpec(
-                    (1, 1, 1, per_pair * rows), lambda pair, tile, lens: (pair, tile, 0, 0)
+    made = []
+    for pair in range(pairs):
+
+        def whole(first):
+            return pl.BlockSpec((total, pair_width), lambda tile, lens: (0, first))
+
+        made.append(
+            pl.pallas_call(
+                functools.partial(backward_kernel, rows, block_rows, per_pair),
+                out_shape=(jax.ShapeDtypeStruct((total, pair_width), BF),) * 3,
+                grid_spec=pltpu.PrefetchScalarGridSpec(
+                    num_scalar_prefetch=1,
+                    grid=(tiles,),
+                    in_specs=[whole(first + pair) for first in firsts]
+                    + [
+                        whole(pair),
+                        whole(pair),
+                        pl.BlockSpec((1, 1, per_pair * rows), lambda tile, lens: (tile, 0, 0)),
+                    ],
+                    out_specs=(
+                        pl.BlockSpec((rows, pair_width), row_block(rows, block_rows)),
+                        whole(0),
+                        whole(0),
+                    ),
+                    scratch_shapes=[
+                        pltpu.VMEM((tiles, pair_width, rows), BF),
+                        pltpu.VMEM((total, pair_width), F32),
+                        pltpu.VMEM((total, pair_width), F32),
+                        pltpu.VMEM((pair_width, per_pair * rows), F32),
+                    ],
                 ),
-            ],
-            out_specs=(
-                pl.BlockSpec((rows, pair_width), row_block(rows, block_rows)),
-                whole(0),
-                whole(0),
-            ),
-            scratch_shapes=[
-                pltpu.VMEM((tiles, pair_width, rows), BF),
-                pltpu.VMEM((total, pair_width), F32),
-                pltpu.VMEM((total, pair_width), F32),
-                pltpu.VMEM((pair_width, per_pair * rows), F32),
-            ],
-        ),
-        name="attend_backward",
-    )(lens, *arrays, mixed, grad, norm)
+                cost_estimate=cost(18),
+                name="attend_backward",
+            )(lens, *arrays, mixed, grad, norms[pair])
+        )
+        if between is not None and pair + 1 < pairs:
+            lens, made[-1], grad = between(lens, made[-1], grad)
+    return made
 
 
 def norm_stats(values):
@@ -522,7 +570,7 @@
     )
     qkv = (jnp.dot(first, qkv_mat, preferred_element_type=F32) + bias_all).astype(BF)
     lens = jnp.concatenate([prompt_lens, cont_lens[0], me.reshape(1)]).astype(jnp.int32)
-    mixed_heads, log_norm = attend_forward(lens, qkv, heads)
+    mixed_heads, norms = attend_forward(lens, qkv, heads)
 
     def to_tokens(values):
         return jnp.concatenate(
@@ -566,7 +614,10 @@
     grad_mixed = nt(grad_attn, out_mat).astype(BF)
     grad_heads = to_heads(grad_mixed)
 
-    grad_q, grad_k, grad_v = attend_backward(lens, qkv, mixed_heads, grad_heads, log_norm, heads)
+    backward = attend_backward(lens, qkv, mixed_heads, norms, grad_heads, heads)
+    grad_q, grad_k, grad_v = (
+        jnp.concatenate([part[i] for part in backward], axis=1) for i in range(3)
+    )
     grad_qkv = jnp.concatenate([grad_q, grad_k, grad_v], axis=1)
     grad_first_part = nt(grad_qkv, qkv_mat).astype(BF)
     grad_first = plane_scatter(
@@ -719,7 +770,7 @@
     return pl.multiple_of(value, size)
 
 
-def pack_kernel(hw, place, fc_ref, proj_ref, mine_ref, other_ref, share_ref):
+def pack_kernel(hw, place, fc_ref, proj_ref, out_mat_ref, mine_ref, other_ref, share_ref):
     me, core = place[0], place[2]
     for q in range(4):
         for z in range(4):
@@ -728,9 +779,10 @@
                 source = aligned(z * 8 * hw + which * 4 * hw + (me ^ q) * hw, hw)
                 out_ref[:, target : target + hw] = fc_ref[:, pl.ds(source, hw)]
     share_ref[...] = proj_ref[...]
-
-
-def pack(place, w_fc, w_proj):
+    other_ref[:, 16 * hw :] = out_mat_ref[...]
+
+
+def pack(place, w_fc, w_proj, w_out):
     own, hidden_all = w_fc.shape
     hw, width = w_proj.shape[0] // 4, w_proj.shape[1]
 
@@ -738,54 +790,92 @@
         return pl.BlockSpec(shape, lambda i, place: (0, 0))
 
     half = jax.ShapeDtypeStruct((own, hidden_all // 2), BF)
+    more = jax.ShapeDtypeStruct((own, hidden_all // 2 + width), BF)
     return pl.pallas_call(
         functools.partial(pack_kernel, hw),
-        out_shape=(half, half, jax.ShapeDtypeStruct((hw, width), BF)),
+        out_shape=(half, more, jax.ShapeDtypeStruct((hw, width), BF)),
         grid_spec=pltpu.PrefetchScalarGridSpec(
             num_scalar_prefetch=1,
             grid=(1,),
             in_specs=[
                 whole((own, hidden_all)),
                 pl.BlockSpec((hw, width), lambda i, place: (place[0], 0)),
+                whole(w_out.shape),
             ],
-            out_specs=(whole(half.shape), whole(half.shape), whole((hw, width))),
+            out_specs=(whole(half.shape), whole(more.shape), whole((hw, width))),
         ),
+        cost_estimate=cost(3),
         name="pack_shares",
-    )(place, w_fc, w_proj)
-
-
-def join_kernel(place, m0, m1, o0, o1, out_ref):
+    )(place, w_fc, w_proj, w_out)
+
+
+def join_kernel(place, m0, m1, o0, o1, mine_out, l0, l1, out_ref):
     core = place[2]
     own, chunk = m0.shape
+    part = mine_out.shape[0]
     for refs, which in (((m0, m1), core), ((o0, o1), 1 - core)):
         rows = pl.ds(aligned(which * own, own), own)
         for half in range(2):
             out_ref[rows, half * chunk : (half + 1) * chunk] = refs[half][...]
-
-
-def join(place, mine, other):
+    wide = 2 * chunk
+    for parts, which in (
+        ((mine_out[:, :wide], mine_out[:, wide:]), core),
+        ((l0[...], l1[...]), 1 - core),
+    ):
+        for half in range(2):
+            rows = pl.ds(aligned(2 * own + which * 2 * part + half * part, part), part)
+            out_ref[rows, :] = parts[half]
+
+
+def join(place, mine, other, w_out):
     own, hidden = mine.shape
     chunk = hidden // 8
+    part = own // 4
+    rows = 2 * own + 4 * part
     pieces = [
         pl.BlockSpec((own, chunk), lambda i, place, at=hidden_at(0, half, 1): (0, at))
         for half in range(2)
     ]
+    quarters = [
+        pl.BlockSpec((part, 2 * chunk), lambda i, place, at=4 + half: (place[0], at))
+        for half in range(2)
+    ]
     return pl.pallas_call(
         join_kernel,
-        out_shape=jax.ShapeDtypeStruct((2 * own, hidden // 4), BF),
+        out_shape=jax.ShapeDtypeStruct((rows, 2 * chunk), BF),
         grid_spec=pltpu.PrefetchScalarGridSpec(
             num_scalar_prefetch=1,
             grid=(1,),
-            in_specs=pieces * 2,
-            out_specs=pl.BlockSpec((2 * own, hidden // 4), lambda i, place: (0, 0)),
+            in_specs=pieces * 2
+            + [pl.BlockSpec((part, w_out.shape[1]), lambda i, place: (place[0], 0))]
+            + quarters,
+            out_specs=pl.BlockSpec((rows, 2 * chunk), lambda i, place: (0, 0)),
         ),
+        cost_estimate=cost(2),
         name="join_rows",
-    )(place, mine, mine, other, other)
+    )(place, mine, mine, other, other, w_out, other, other)
+
+
+def joined_kernel(*refs):
+    at = 0
+    for ref in refs[:-1]:
+        refs[-1][at : at + ref.shape[0], :] = ref[...]
+        at += ref.shape[0]
+
+
+def joined(parts):
+    rows = sum(part.shape[0] for part in parts)
+    return pl.pallas_call(
+        joined_kernel,
+        out_shape=jax.ShapeDtypeStruct((rows, parts[0].shape[1]), parts[0].dtype),
+        cost_estimate=cost(1),
+        name="joined",
+    )(*parts)
 
 
 def project_kernel(
     place, own_ref, one_ref, two_ref, up_ref, low_ref, kept_ref, moved_ref, gain_ref, shift_ref,
-    bias_ref, first_ref, unit_ref, qkv_ref, toks, mat, sems,
+    bias_ref, first_ref, unit_ref, qkv_ref, turned_ref, toks, mat, sems,
 ):
     step = pl.program_id(0)
     floor, core = place[1], place[2]
@@ -820,6 +910,10 @@
     unit_ref[...] = unit.astype(BF)
     qkv_ref[...] = (nn(first, mat[...]) + bias_ref[...]).astype(BF)
 
+    @pl.when(step == pl.num_programs(0) - 1)
+    def _():
+        turned_ref[...] = mat[...].T
+
 
 def project(place, blocks, kept, moved, gain, shift, bias):
     block, width = blocks[0].shape
@@ -840,42 +934,65 @@
             jax.ShapeDtypeStruct((total, width), BF),
             jax.ShapeDtypeStruct((total, width), BF),
             jax.ShapeDtypeStruct((total, outs), BF),
+            jax.ShapeDtypeStruct((outs, width), BF),
         ),
         grid_spec=pltpu.PrefetchScalarGridSpec(
             num_scalar_prefetch=1,
             grid=(total // rows,),
             in_specs=[raw] * 7 + [line(width), line(width), line(outs)],
-            out_specs=(tile(width), tile(width), tile(outs)),
+            out_specs=(
+                tile(width),
+                tile(width),
+                tile(outs),
+                pl.BlockSpec((outs, width), lambda i, place: (0, 0)),
+            ),
             scratch_shapes=[
                 pltpu.VMEM((total, width), BF),
                 pltpu.VMEM((width, outs), BF),
                 pltpu.SemaphoreType.DMA((13,)),
             ],
         ),
+        cost_estimate=cost(12),
         name="project",
     )(place, *blocks, kept, moved, gain, shift, bias)
 
 
-def attn_out_kernel(
-    place, m0, m1, m2, m3, kept_ref, moved_ref, token_ref, bias_ref, gain_ref, shift_ref,
-    hidden_ref, second_ref, mixed_ref, mat_ref, mixed, sems,
-):
+def attn_out_kernel(part, place, *refs):
+    mixed_refs, (mine_ref, other_ref), shares = refs[:4], refs[4:6], refs[6:10]
+    token_ref, bias_ref, gain_ref, shift_ref = refs[10:14]
+    hidden_ref, second_ref, mixed_ref, mat_ref, mixed, sems = refs[14:]
     step = pl.program_id(0)
     me, floor, core = place[0], place[1], place[2]
-    local = m1.shape[1]
-    own = mat_ref.shape[0] // 8
-    block = m1.shape[0]
+    local = mixed_refs[0].shape[1]
+    own, width = mine_ref.shape
+    block = mixed.shape[0]
+    wide = width // 2
+    rows_each = 2 * own + 4 * part
 
     @pl.when(step == 0)
     def _():
         made = []
-        for k, ref in enumerate((m0, m1, m2, m3)):
+        for k, ref in enumerate(mixed_refs):
             lanes = pl.ds(aligned((me ^ k) * local, local), local)
             made.append((ref.at[pl.ds(0, block), :], mixed.at[:, lanes]))
-        for k in range(4):
-            for ref, which in ((kept_ref, core), (moved_ref, 1 - core)):
-                row = aligned((floor ^ k) * 2 * own + which * own, own)
-                made.append((ref.at[k], mat_ref.at[pl.ds(row, own), :]))
+        for source, which in (
+            (mine_ref, core),
+            (other_ref.at[:, pl.ds(other_ref.shape[1] - width, width)], 1 - core),
+        ):
+            row = aligned(floor * 2 * own + which * own, own)
+            made.append((source, mat_ref.at[pl.ds(row, own), :]))
+        for q in range(4):
+            for k in range(1, 4):
+                for which in range(2):
+                    row = aligned((floor ^ k) * 2 * own + which * own + (me ^ q) * part, part)
+                    for half in range(2):
+                        at = (k - 1) * rows_each + 2 * own + which * 2 * part + half * part
+                        made.append(
+                            (
+                                shares[q].at[pl.ds(at, part), :],
+                                mat_ref.at[pl.ds(row, part), pl.ds(half * wide, wide)],
+                            )
+                        )
         for copy in start_all(made, sems):
             copy.wait()
 
@@ -888,14 +1005,14 @@
     second_ref[...] = (unit * gain_ref[...] + shift_ref[...]).astype(BF)
 
 
-def attn_out(place, mixed, kept, moved, tokens, bias, gain, shift):
+def attn_out(place, mixed, mine, other, shares, tokens, bias, gain, shift):
     block, width = tokens.shape
     rows = 256
     raw = pl.BlockSpec(memory_space=pl.ANY)
     line = pl.BlockSpec((1, width), lambda i, place: (0, 0))
     tile = pl.BlockSpec((rows, width), lambda i, place: (i, 0))
     return pl.pallas_call(
-        attn_out_kernel,
+        functools.partial(attn_out_kernel, mine.shape[0] // 4),
         out_shape=(
             jax.ShapeDtypeStruct((block, width), F32),
             jax.ShapeDtypeStruct((block, width), BF),
@@ -905,132 +1022,161 @@
         grid_spec=pltpu.PrefetchScalarGridSpec(
             num_scalar_prefetch=1,
             grid=(block // rows,),
-            in_specs=[raw] * 6 + [tile, line, line, line],
+            in_specs=[raw] * 10 + [tile, line, line, line],
             out_specs=(tile, tile, tile, pl.BlockSpec((width, width), lambda i, place: (0, 0))),
-            scratch_shapes=[pltpu.VMEM((block, width), BF), pltpu.SemaphoreType.DMA((12,))],
+            scratch_shapes=[pltpu.VMEM((block, width), BF), pltpu.SemaphoreType.DMA((54,))],
         ),
+        cost_estimate=cost(7),
         name="attn_out",
-    )(place, *mixed, kept, moved, tokens, bias, gain, shift)
+    )(place, *mixed, mine, other, *shares, tokens, bias, gain, shift)
 
 
 def feed_kernel(
-    hw, place, second_ref, branch_ref, bias_ref, mine_ref, other_ref, a0, a1, a2, a3, proj_ref,
-    b0, b1, b2, b3, act_ref, slope_ref, out_own, out_oth, back_own, back_oth, colsum_ref,
-    fc, proj, sems,
+    hw, place, second_ref, branch_ref, bias_a, bias_b, mine_ref, other_ref, a0, a1, a2, a3, proj_ref,
+    b0, b1, b2, b3, act_a, act_b, slope_a, slope_b, out_own, out_oth, back_own, back_oth, sum_a, sum_b,
+    fc, proj, fc_turned, proj_turned, total, back, sems,
 ):
     step = pl.program_id(0)
     me, floor, core = place[0], place[1], place[2]
     own = mine_ref.shape[0]
     chunk = 2 * hw
-    steps = pl.num_programs(0)
-
-    @pl.when(step == 0)
-    def _():
+    rows_each = a0.shape[0] // 3
+
+    def copies(q):
         made = []
         for ref, which in ((mine_ref, core), (other_ref, 1 - core)):
             row = aligned(floor * 2 * own + which * own, own)
-            made.append((ref, fc.at[pl.ds(row, own), :]))
-        for q, ref in enumerate((a0, a1, a2, a3)):
-            for k in range(1, 4):
-                row = aligned((floor ^ k) * 2 * own, 2 * own)
-                for half in range(2):
-                    made.append(
-                        (
-                            ref.at[pl.ds((k - 1) * 2 * own, 2 * own), pl.ds(half * chunk, chunk)],
-                            fc.at[pl.ds(row, 2 * own), pl.ds(hidden_at(q, half, chunk), chunk)],
-                        )
+            for half in range(2):
+                made.append(
+                    (
+                        ref.at[:, pl.ds(hidden_at(q, half, chunk), chunk)],
+                        fc.at[q, pl.ds(row, own), pl.ds(half * chunk, chunk)],
                     )
-        for q, ref in enumerate((b0, b1, b2, b3)):
-            for k in range(4):
-                z = floor ^ k
-                row = jnp.where(z < 2, hidden_at(q, 0, chunk), hidden_at(q, 1, chunk)) + (z % 2) * hw
-                if k == 0:
-                    source = proj_ref.at[pl.ds(aligned((me ^ q) * hw, hw), hw), :]
-                else:
-                    source = ref.at[pl.ds((k - 1) * hw, hw), :]
-                made.append((source, proj.at[pl.ds(aligned(row, hw), hw), :]))
-        for copy in start_all(made, sems):
-            copy.wait()
-
-    second = second_ref[...]
-    branch = branch_ref[...]
-    total = None
-    back = None
-    span = 4 * hw
-    for q in range(fc.shape[1] // span):
-        here = pl.ds(q * span, span)
-        pre = nn(second, fc[:, here]) + bias_ref[:, here]
+                )
+        for k in range(1, 4):
+            row = aligned((floor ^ k) * 2 * own, 2 * own)
+            source = (a0, a1, a2, a3)[q].at[pl.ds((k - 1) * rows_each, 2 * own), :]
+            made.append((source, fc.at[q, pl.ds(row, 2 * own), :]))
+        for k in range(4):
+            if k == 0:
+                source = proj_ref.at[pl.ds(aligned((me ^ q) * hw, hw), hw), :]
+            else:
+                source = (b0, b1, b2, b3)[q].at[pl.ds((k - 1) * hw, hw), :]
+            made.append((source, proj.at[q, pl.ds(aligned((floor ^ k) * hw, hw), hw), :]))
+        return [
+            pltpu.make_async_copy(source, target, sems.at[q, i])
+            for i, (source, target) in enumerate(made)
+        ]
+
+    @pl.when(step == 0)
+    def _():
+        for q in range(4):
+            for copy in copies(q):
+                copy.start()
+
+    for q in range(4):
+
+        @pl.when(step == q)
+        def _():
+            for copy in copies(q):
+                copy.wait()
+
+    fc_turned[...] = fc[step].T
+    proj_turned[...] = proj[step].T
+    bias = jnp.concatenate([bias_a[...], bias_b[...]], axis=1)
+    both = second_ref.shape[0]
+    rows = both // 2
+    partial = None
+    for start in range(0, both, rows):
+        here = slice(start, start + rows)
+        pre = nn(second_ref[here, :], fc[step]) + bias
         value, bend = gelu_both(pre)
         act = value.astype(BF)
-        act_ref[:, here] = act
-        slope_full = nt(branch, proj[here, :]) * bend
+        act_a[here, :] = act[:, :chunk]
+        act_b[here, :] = act[:, chunk:]
+        slope_full = nn(branch_ref[here, :], proj_turned[...]) * bend
         slope = slope_full.astype(BF)
-        slope_ref[:, here] = slope
-        partial = jnp.sum(slope_full, axis=0, keepdims=True)
+        slope_a[here, :] = slope[:, :chunk]
+        slope_b[here, :] = slope[:, chunk:]
+        more = jnp.sum(slope_full, axis=0, keepdims=True)
+        partial = more if partial is None else partial + more
+        out_part = nn(act, proj[step])
+        back_part = nn(slope, fc_turned[...])
 
         @pl.when(step == 0)
         def _():
-            colsum_ref[:, here] = partial
+            total[here, :] = out_part
+            back[here, :] = back_part
 
         @pl.when(step > 0)
         def _():
-            colsum_ref[:, here] += partial
-
-        more = nn(act, proj[here, :])
-        total = more if total is None else total + more
-        more = nt(slope, fc[:, here])
-        back = more if back is None else back + more
-
-    @pl.when(step < steps // 2)
+            total[here, :] += out_part
+            back[here, :] += back_part
+
+    sum_a[...] = partial[:, :chunk]
+    sum_b[...] = partial[:, chunk:]
+
+    @pl.when(step == 3)
     def _():
-        out_oth[...] = total.astype(BF)
-        back_oth[...] = back.astype(BF)
-
-    @pl.when(step >= steps // 2)
-    def _():
-        out_own[...] = total
-        back_own[...] = back
+        half = both // 2
+        out_oth[...] = total[:half].astype(BF)
+        back_oth[...] = back[:half].astype(BF)
+        out_own[...] = total[half:]
+        back_own[...] = back[half:]
 
 
 def feed(place, second, branch, bias, mine, other, shares, w_proj, proj_shares):
     both, width = second.shape
     hidden = mine.shape[1]
     hw = hidden // 16
-    rows = 256
-    steps = both // rows
-    half = steps // 2
+    chunk = 2 * hw
     raw = pl.BlockSpec(memory_space=pl.ANY)
 
-    def tile(size):
-        return pl.BlockSpec((rows, size), lambda i, place: (i, 0))
-
-    line = pl.BlockSpec((1, hidden), lambda i, place: (0, 0))
-    early = pl.BlockSpec((rows, width), lambda i, place: (jnp.minimum(i, half - 1), 0))
-    late = pl.BlockSpec((rows, width), lambda i, place: (jnp.maximum(i - half, 0), 0))
+    def whole(height):
+        return pl.BlockSpec((height, width), lambda i, place: (0, 0))
+
+    def upper(height):
+        return pl.BlockSpec((height, chunk), lambda i, place: (0, (i % 2) * 2 + i // 2))
+
+    def lower(height, first=0):
+        return pl.BlockSpec((height, chunk), lambda i, place: (0, first + i))
+
+    half = jax.ShapeDtypeStruct((both, hidden // 2), BF)
+    line = jax.ShapeDtypeStruct((1, hidden // 2), F32)
     return pl.pallas_call(
         functools.partial(feed_kernel, hw),
         out_shape=(
-            jax.ShapeDtypeStruct((both, hidden), BF),
-            jax.ShapeDtypeStruct((both, hidden), BF),
+            half,
+            half,
+            half,
+            half,
             jax.ShapeDtypeStruct((both // 2, width), F32),
             jax.ShapeDtypeStruct((both // 2, width), BF),
             jax.ShapeDtypeStruct((both // 2, width), F32),
             jax.ShapeDtypeStruct((both // 2, width), BF),
-            jax.ShapeDtypeStruct((1, hidden), F32),
+            line,
+            line,
         ),
         grid_spec=pltpu.PrefetchScalarGridSpec(
             num_scalar_prefetch=1,
-            grid=(steps,),
-            in_specs=[tile(width), tile(width), line] + [raw] * 11,
-            out_specs=(tile(hidden), tile(hidden), late, early, late, early, line),
+            grid=(4,),
+            in_specs=[whole(both), whole(both), upper(1), lower(1, 4)] + [raw] * 11,
+            out_specs=(upper(both), lower(both), upper(both), lower(both))
+            + (whole(both // 2),) * 4
+            + (upper(1), lower(1)),
             scratch_shapes=[
-                pltpu.VMEM((width, hidden), BF),
-                pltpu.VMEM((hidden, width), BF),
-                pltpu.SemaphoreType.DMA((42,)),
+                pltpu.VMEM((4, width, 2 * chunk), BF),
+                pltpu.VMEM((4, 2 * chunk, width), BF),
+                pltpu.VMEM((2 * chunk, width), BF),
+                pltpu.VMEM((width, 2 * chunk), BF),
+                pltpu.VMEM((both, width), F32),
+                pltpu.VMEM((both, width), F32),
+                pltpu.SemaphoreType.DMA((4, 11)),
             ],
         ),
+        cost_estimate=cost(35),
         name="feed",
-    )(place, second, branch, bias, mine, other, *shares, w_proj, *proj_shares)
+    )(place, second, branch, bias, bias, mine, other, *shares, w_proj, *proj_shares)
 
 
 def mixed_back_kernel(
@@ -1071,7 +1217,7 @@
 def mixed_back(place, own, oth, hidden, branch, gain, mat):
     block, width = own.shape
     local = width // 4
-    rows = 256
+    rows = block
 
     def tile(size):
         return pl.BlockSpec((rows, size), lambda i, place: (i, 0))
@@ -1093,19 +1239,20 @@
             in_specs=[tile(width)] * 4 + [whole(1), whole(width)],
             out_specs=(tile(width), tile(width)) + (tile(local),) * 4 + (whole(4),),
         ),
+        cost_estimate=cost(7),
         name="mixed_back",
     )(place, own, oth, hidden, branch, gain, mat)
 
 
 def first_back_kernel(tiles, place, grad_ref, unit_ref, mat_ref, *refs):
     step = pl.program_id(0)
-    count = len(tiles)
+    count = len(tiles) // 2
     out_refs, sums_ref = refs[:count], refs[count]
-    part = nt(grad_ref[...], mat_ref[...])
+    part = nn(grad_ref[...], mat_ref[...])
     low = part.astype(BF)
     for i in range(count):
 
-        @pl.when(step == i)
+        @pl.when(step // 2 == i)
         def _():
             out_refs[i][...] = low
 
@@ -1126,19 +1273,18 @@
         sums_ref[...] += sums
 
 
-def first_back(tiles, groups, grad, unit, mat):
+def first_back(tiles, grad, unit, mat):
     total, outs = grad.shape
-    width = mat.shape[0]
+    width = mat.shape[1]
     rows = 256
     table = jnp.asarray(tiles, jnp.int32)
-    del groups
 
     def at(i, place):
         return (place[i], 0)
 
     return pl.pallas_call(
         functools.partial(first_back_kernel, tiles),
-        out_shape=tuple(jax.ShapeDtypeStruct((rows, width), BF) for _ in tiles)
+        out_shape=tuple(jax.ShapeDtypeStruct((2 * rows, width), BF) for _ in tiles[::2])
         + (jax.ShapeDtypeStruct((2, width), F32),),
         grid_spec=pltpu.PrefetchScalarGridSpec(
             num_scalar_prefetch=1,
@@ -1146,121 +1292,93 @@
             in_specs=[
                 pl.BlockSpec((rows, outs), at),
                 pl.BlockSpec((rows, width), at),
-                pl.BlockSpec((width, outs), lambda i, place: (0, 0)),
+                pl.BlockSpec((outs, width), lambda i, place: (0, 0)),
             ],
-            out_specs=tuple(pl.BlockSpec((rows, width), lambda i, place: (0, 0)) for _ in tiles)
+            out_specs=tuple(
+                pl.BlockSpec((rows, width), lambda i, place, g=g: (jnp.clip(i - 2 * g, 0, 1), 0))
+                for g in range(len(tiles) // 2)
+            )
             + (pl.BlockSpec((2, width), lambda i, place: (0, 0)),),
         ),
+        cost_estimate=cost(5),
         name="first_back",
     )(table, grad, unit, mat)
 
 
-def gather_sum_kernel(place, *refs):
+def gather_fc_kernel(place, fa, xa, la, fb, yb, lb, o0, o1, o2, o3, fc):
     floor = place[1]
-    fa, xa, la, fb, yb, lb, pa, xp, lpa, pb, yp, lpb, o0, o1, o2, o3, fc, proj = refs
     chunk = fc.shape[1] // 2
-    hw = chunk // 2
     fc[:, :chunk] = fa[...].astype(F32) + xa[...].astype(F32) + la[...].astype(F32)
     fc[:, chunk:] = fb[...].astype(F32) + yb[...].astype(F32) + lb[...].astype(F32)
+    rows = fc.shape[0] // 4
+    for k, out in enumerate((o0, o1, o2, o3)):
+        out[...] = fc[pl.ds(aligned((floor ^ k) * rows, rows), rows), :].astype(BF)
+
+
+def gather_proj_kernel(place, pa, xp, lpa, pb, yp, lpb, o0, o1, o2, o3, proj):
+    floor = place[1]
+    chunk = proj.shape[0] // 2
     proj[:chunk, :] = pa[...].astype(F32) + xp[...].astype(F32) + lpa[...].astype(F32)
     proj[chunk:, :] = pb[...].astype(F32) + yp[...].astype(F32) + lpb[...].astype(F32)
-    rows = fc.shape[0] // 4
+    rows = proj.shape[0] // 4
     for k, out in enumerate((o0, o1, o2, o3)):
-        out[:rows, :] = fc[pl.ds(aligned((floor ^ k) * rows, rows), rows), :].astype(BF)
-        piece = proj[pl.ds(aligned((floor ^ k) * hw, hw), hw), :].astype(BF)
-        out[rows : rows + hw, :] = piece[:, : 2 * chunk]
-        out[rows + hw :, :] = piece[:, 2 * chunk :]
-
-
-def gather_sum(place, fc_parts, proj_parts):
-    width = fc_parts[0].shape[0]
-    chunk = width // 4
-    fc_spec = pl.BlockSpec((width, chunk), lambda i, place: (0, 0))
-    proj_spec = pl.BlockSpec((chunk, width), lambda i, place: (0, 0))
-    out = jax.ShapeDtypeStruct((width // 2, 2 * chunk), BF)
+        out[...] = proj[pl.ds(aligned((floor ^ k) * rows, rows), rows), :].astype(BF)
+
+
+def gather_sum(place, kernel, parts, shape, block):
+    out = jax.ShapeDtypeStruct((shape[0] // 4, shape[1]), BF)
     return pl.pallas_call(
-        gather_sum_kernel,
+        kernel,
         out_shape=(out,) * 4,
         grid_spec=pltpu.PrefetchScalarGridSpec(
             num_scalar_prefetch=1,
             grid=(1,),
-            in_specs=[fc_spec] * 6 + [proj_spec] * 6,
+            in_specs=[pl.BlockSpec(block, lambda i, place: (0, 0))] * 6,
             out_specs=(pl.BlockSpec(out.shape, lambda i, place: (0, 0)),) * 4,
-            scratch_shapes=[pltpu.VMEM((width, 2 * chunk), F32), pltpu.VMEM((2 * chunk, width), F32)],
+            scratch_shapes=[pltpu.VMEM(shape, F32)],
         ),
+        cost_estimate=cost(3),
         name="gather_sum",
-    )(place, *fc_parts, *proj_parts)
-
-
-def floor_sum_kernel(place, r0, r1, r2, r3, kept_ref, sent_ref, total):
-    core = place[2]
-    total[...] = (
-        r0[...].astype(F32) + r1[...].astype(F32) + r2[...].astype(F32) + r3[...].astype(F32)
-    )
-    own = sent_ref.shape[0]
-    sent_ref[...] = total[pl.ds(aligned((1 - core) * own, own), own), :].astype(BF)
-    kept_ref[:own, :] = total[pl.ds(aligned(core * own, own), own), :].astype(BF)
-    kept_ref[own:, :] = total[2 * own :, :].astype(BF)
-
-
-def floor_sum(place, parts):
-    rows, cols = parts[0].shape
-    own = rows // 4
-
-    def whole(height):
-        return pl.BlockSpec((height, cols), lambda i, place: (0, 0))
+    )(place, *parts)
+
+
+def spread_fc_kernel(place, *refs):
+    me, core = place[0], place[2]
+    finals, fc_ref = refs[:4], refs[4]
+    own = fc_ref.shape[0]
+    hw = finals[0].shape[1] // 4
+    for q in range(4):
+        for part, which in ((0, core), (1, 1 - core)):
+            for z in range(4):
+                lanes = pl.ds(aligned(z * 8 * hw + which * 4 * hw + (me ^ q) * hw, hw), hw)
+                block = finals[q][part * own : (part + 1) * own, z * hw : (z + 1) * hw]
+                fc_ref[:, lanes] = block.astype(F32)
+
+
+def spread_proj_kernel(place, *refs):
+    me = place[0]
+    finals, proj_ref = refs[:4], refs[4]
+    hw = finals[0].shape[0]
+    for q in range(4):
+        proj_ref[pl.ds(aligned((me ^ q) * hw, hw), hw), :] = finals[q][...].astype(F32)
+
+
+def spread(place, kernel, finals, shape):
+    def whole(shape):
+        return pl.BlockSpec(shape, lambda i, place: (0, 0))
 
     return pl.pallas_call(
-        floor_sum_kernel,
-        out_shape=(
-            jax.ShapeDtypeStruct((3 * own, cols), BF),
-            jax.ShapeDtypeStruct((own, cols), BF),
-        ),
+        kernel,
+        out_shape=jax.ShapeDtypeStruct(shape, F32),
         grid_spec=pltpu.PrefetchScalarGridSpec(
             num_scalar_prefetch=1,
             grid=(1,),
-            in_specs=[whole(rows)] * 4,
-            out_specs=(whole(3 * own), whole(own)),
-            scratch_shapes=[pltpu.VMEM((rows, cols), F32)],
+            in_specs=[whole(finals[0].shape)] * 4,
+            out_specs=whole(shape),
         ),
-        name="floor_sum",
-    )(place, *parts)
-
-
-def spread_kernel(place, *refs):
-    me, core = place[0], place[2]
-    kept, moved, (fc_ref, proj_ref) = refs[:4], refs[4:8], refs[8:]
-    own = moved[0].shape[0]
-    hw = moved[0].shape[1] // 4
-    for q in range(4):
-        for ref, which in ((kept[q], core), (moved[q], 1 - core)):
-            for z in range(4):
-                lanes = pl.ds(aligned(z * 8 * hw + which * 4 * hw + (me ^ q) * hw, hw), hw)
-                fc_ref[:, lanes] = ref[:own, z * hw : (z + 1) * hw].astype(F32)
-        rows = pl.ds(aligned((me ^ q) * hw, hw), hw)
-        proj_ref[rows, : 4 * hw] = kept[q][own : own + hw, :].astype(F32)
-        proj_ref[rows, 4 * hw :] = kept[q][own + hw :, :].astype(F32)
-
-
-def spread(place, kept, moved):
-    own, cols = moved[0].shape
-    hw = cols // 4
-
-    def whole(shape):
-        return pl.BlockSpec(shape, lambda i, place: (0, 0))
-
-    fc_shape, proj_shape = (own, 32 * hw), (4 * hw, 8 * hw)
-    return pl.pallas_call(
-        spread_kernel,
-        out_shape=(jax.ShapeDtypeStruct(fc_shape, F32), jax.ShapeDtypeStruct(proj_shape, F32)),
-        grid_spec=pltpu.PrefetchScalarGridSpec(
-            num_scalar_prefetch=1,
-            grid=(1,),
-            in_specs=[whole(kept[0].shape)] * 4 + [whole(moved[0].shape)] * 4,
-            out_specs=(whole(fc_shape), whole(proj_shape)),
-        ),
+        cost_estimate=cost(2),
         name="spread",
-    )(place, *kept, *moved)
+    )(place, *finals)
 
 
 def last_kernel(keep_ref, got_ref, last_ref, token_ref, hidden_ref, gain_ref, out_ref):
@@ -1303,34 +1421,28 @@
     branch = cotangent[0]
 
     half = toks // 2
-    tok_one = swap(token_block, "seq", 1)
-    tok_two = swap(token_block, "seq", 2)
-    tok_up = swap(tok_two[:half], "seq", 1)
-    tok_low = swap(tok_one[half:], "seq", 2)
-
     vectors = [gain_one, shift_one, bias_qv, bias_out, gain_two, shift_two, bias_fc, bias_proj]
     packed = jnp.concatenate([v.reshape(-1, own) for v in vectors], axis=0)
     lines = packed.shape[0]
     packed = jnp.pad(packed.reshape(-1), (0, 16 * 3 * local - packed.size)).reshape(16, 3 * local)
     mine_qkv = pick(w_qkv.reshape(own, 3, ns, local), me, 2).reshape(own, 3 * local)
     sent_qkv = jnp.concatenate([mine_qkv, packed], axis=0)
-    kept_qkv = jnp.stack([sent_qkv] + [swap(sent_qkv, "fsdp", 2 * k) for k in range(1, nz)])
+    tok_one = swap(token_block, "seq", 1)
+    tok_two = swap(token_block, "seq", 2)
+    got_qkv = [swap(sent_qkv, "fsdp", 2 * k) for k in range(1, nz)]
+    fc_mine, fc_sent, proj_share = pack(place, w_fc, w_proj, w_out)
+    fc_other = swap(fc_sent, "fsdp", 1)
+    fc_share = join(place, fc_mine, fc_other, w_out)
+
+    tok_one, tok_two, got_qkv, fc_share, proj_share = lax.optimization_barrier(
+        (tok_one, tok_two, got_qkv, fc_share, proj_share)
+    )
+    tok_up = swap(tok_two[:half], "seq", 1)
+    tok_low = swap(tok_one[half:], "seq", 2)
+    kept_qkv = jnp.stack([sent_qkv, *got_qkv])
     moved_qkv = swap(kept_qkv, "fsdp", 1)
-
-    fc_mine, fc_sent, proj_share = pack(place, w_fc, w_proj)
-    fc_other = swap(fc_sent, "fsdp", 1)
-    fc_share = join(place, fc_mine, fc_other)
-    fc_zero = jnp.concatenate([swap(fc_share, "fsdp", 2 * k) for k in range(1, nz)], axis=0)
-    proj_zero = jnp.concatenate([swap(proj_share, "fsdp", 2 * k) for k in range(1, nz)], axis=0)
-    kept_out = jnp.stack([w_out] + [swap(w_out, "fsdp", 2 * k) for k in range(1, nz)])
-    moved_out = swap(kept_out, "fsdp", 1)
-    fc_one = swap(fc_zero, "seq", 1)
-    fc_two = swap(fc_zero, "seq", 2)
-    fc_three = swap(fc_two, "seq", 1)
-    proj_one = swap(proj_zero, "seq", 1)
-    proj_two = swap(proj_zero, "seq", 2)
-    proj_three = swap(proj_one, "seq", 2)
-    branch_both = jnp.concatenate([swap(branch, "fsdp", 1), branch], axis=0)
+    moved_qkv, fc_share = lax.optimization_barrier((moved_qkv, fc_share))
+    fc_got = [swap(fc_share, "fsdp", 2 * k) for k in range(1, nz)]
 
     small = by_core(core, kept_qkv[:, own : own + 2], moved_qkv[:, own : own + 2], 1)
     small = xor_take(small, floor, 0).reshape(nf, -1).reshape(nf, lines, own)
@@ -1349,113 +1461,207 @@
         [fc_bias[2 * part : 2 * part + 2, q].reshape(1, -1) for q, part in order], axis=1
     )
 
-    first, unit_all, qkv = project(
+    first, unit_all, qkv, qkv_turned = project(
         place, (token_block, tok_one, tok_two, tok_up, tok_low), kept_qkv, moved_qkv, gain_a, shift_a,
         bias_all,
     )
     lens = jnp.concatenate([prompt_lens, cont_lens[0], me.reshape(1)]).astype(jnp.int32)
-    mixed_heads, log_norm = attend_forward(lens, qkv, heads)
+
+    qkv, fc_got, proj_share = lax.optimization_barrier((qkv, fc_got, proj_share))
+    fc_zero = joined(fc_got)
+    fc_one = swap(fc_zero, "seq", 1)
+    fc_two = swap(fc_zero, "seq", 2)
+    proj_got = [swap(proj_share, "fsdp", 2 * k) for k in range(1, nz)]
+    ends = {}
+
+    def between(lens, mixed, arrays):
+        (mixed, arrays, one, two, got) = lax.optimization_barrier(
+            (mixed, arrays, fc_one, fc_two, proj_got)
+        )
+        cut = one.shape[0] // 2
+        ends["fc"] = (one, two, swap(two[:cut], "seq", 1), swap(one[cut:], "seq", 2))
+        zero = joined(got)
+        ends["proj"] = (zero, swap(zero, "seq", 1), swap(zero, "seq", 2))
+        return lens, mixed, arrays
+
+    mixed_heads, norms = attend_forward(lens, qkv, heads, between)
+    fc_one, fc_two, fc_up, fc_low = ends["fc"]
+    proj_zero, proj_one, proj_two = ends["proj"]
+
+    mixed_heads, fc_up, fc_low, proj_one, proj_two = lax.optimization_barrier(
+        (mixed_heads, fc_up, fc_low, proj_one, proj_two)
+    )
     mixed_blocks = [mixed_heads] + [
         swap(mixed_heads[k * toks : (k + 1) * toks], "seq", k) for k in range(1, ns)
     ]
+    fc_three = joined([fc_up, fc_low])
+    shares = (fc_zero, fc_one, fc_two, fc_three)
+    cut = proj_one.shape[0] // 2
+    proj_three = joined([swap(proj_two[:cut], "seq", 1), swap(proj_one[cut:], "seq", 2)])
     hidden, second, mixed, out_mat = attn_out(
-        place, mixed_blocks, kept_out, moved_out, token_block, out_vec, gain_b, shift_b
-    )
-
+        place, mixed_blocks, w_out, fc_other, shares, token_block, out_vec, gain_b, shift_b
+    )
+
+    second, branch_sent = lax.optimization_barrier((second, branch))
     second_both = jnp.concatenate([swap(second, "fsdp", 1), second], axis=0)
-    act, grad_pre, out_own, out_oth, back_own, back_oth, fc_bias_sum = feed(
+    branch_both = jnp.concatenate([swap(branch_sent, "fsdp", 1), branch], axis=0)
+    *hiddens, out_own, out_oth, back_own, back_oth, sum_upper, sum_lower = feed(
         place, second_both, branch_both, fc_bias, fc_mine, fc_other,
-        (fc_zero, fc_one, fc_two, fc_three), w_proj, (proj_zero, proj_one, proj_two, proj_three),
+        shares, w_proj, (proj_zero, proj_one, proj_two, proj_three),
     )
     back_got = swap(back_oth, "fsdp", 1)
     out_got = swap(out_oth, "fsdp", 1)
-    output = (hidden + out_own + proj_vec + out_got.astype(F32)).astype(BF)[None]
     grad_hidden, grad_attn, *grad_blocks, sums_two = mixed_back(
         place, back_own, back_got, hidden, branch, gain_b, out_mat
     )
-    grad_heads = jnp.concatenate(
-        [grad_blocks[0]] + [swap(grad_blocks[k], "seq", k) for k in range(1, ns)], axis=0
-    )
+
+    def added(left, right):
+        return (left.astype(F32) + right.astype(F32)).astype(BF)
+
+    def halves(values, index):
+        pair = values.reshape(2, values.shape[0] // 2, values.shape[1])
+        return pick(pair, index, 0).astype(F32), pick(pair, 1 - index, 0).astype(BF)
+
+    def core_halves(grad):
+        cut = grad.reshape(nz, 2, own, -1)
+        mine, sent = pick(cut, core, 1), pick(cut, 1 - core, 1)
+        return mine.reshape(nz * own, -1), sent.reshape(nz * own, -1)
 
     edge = 4 * hw
-    fc_grads = [tn(second_both, grad_pre[:, i * edge : (i + 1) * edge]).astype(BF) for i in range(4)]
-    proj_grads = [tn(act[:, i * edge : (i + 1) * edge], branch_both).astype(BF) for i in range(4)]
     chunk = 2 * hw
+    head_got = [swap(grad_blocks[k], "seq", k) for k in range(1, ns)]
+    hiddens, branch_late = after((hiddens, branch_both), grad_blocks)
+    acts, slopes = (
+        [v[:, i * edge : (i + 1) * edge] for v in pair for i in range(2)]
+        for pair in (hiddens[:2], hiddens[2:])
+    )
+    proj_grads = [None] * 4
+    for i in (1, 3, 0, 2):
+        proj_grads[i] = tn(acts[i], branch_late).astype(BF)
+
+    proj_grads, slopes, second_late, mixed_late, attn_late, head_got, out_got = after(
+        (proj_grads, slopes, second_both, mixed, grad_attn, head_got, out_got)
+    )
+    proj_x = swap(proj_grads[1], "seq", 1)
+    proj_y = swap(proj_grads[3], "seq", 2)
+    wo_mine, wo_sent = core_halves(tn(mixed_late, attn_late).astype(BF))
+    wo_got = swap(wo_sent, "fsdp", 1)
+    fc_grads = [None] * 4
+    for i in (1, 3, 0, 2):
+        fc_grads[i] = tn(second_late, slopes[i]).astype(BF)
+    output = (hidden + out_own + proj_vec + out_got.astype(F32)).astype(BF)
+
+    grad_heads = jnp.concatenate([grad_blocks[0], *head_got], axis=0)
+    grad_heads, fc_grads, wo_got, output = after((grad_heads, fc_grads, wo_got, output))
     fc_x = swap(fc_grads[1], "seq", 1)
     fc_y = swap(fc_grads[3], "seq", 2)
-    proj_x = swap(proj_grads[1], "seq", 1)
-    proj_y = swap(proj_grads[3], "seq", 2)
-
-    def added(left, right):
-        return (left.astype(F32) + right.astype(F32)).astype(BF)
-
-    fc_last_y = swap(added(fc_grads[0][:, chunk:], fc_x[:, chunk:]), "seq", 2)
-    fc_last_x = swap(added(fc_grads[2][:, chunk:], fc_y[:, chunk:]), "seq", 1)
-    proj_last_y = swap(added(proj_grads[0][chunk:], proj_x[chunk:]), "seq", 2)
-    proj_last_x = swap(added(proj_grads[2][chunk:], proj_y[chunk:]), "seq", 1)
+    wo_keep, wo_sent = halves(wo_mine.astype(F32) + wo_got.astype(F32), floor // 2)
+    wo_far = swap(wo_sent, "fsdp", 4)
+    back = {}
+
+    def between_back(lens, parts, grad):
+        parts, grad, x, y, far = after((parts, grad, proj_x, proj_y, wo_far))
+        back["proj"] = (
+            x,
+            y,
+            swap(added(proj_grads[2][chunk:], y[chunk:]), "seq", 1),
+            swap(added(proj_grads[0][chunk:], x[chunk:]), "seq", 2),
+        )
+        keep, sent = halves(wo_keep + far.astype(F32), floor % 2)
+        back["out"] = keep, swap(sent, "fsdp", 2)
+        return lens, parts, grad
+
+    backward = attend_backward(lens, qkv, mixed_heads, norms, grad_heads, heads, between_back)
+    proj_x, proj_y, proj_last_x, proj_last_y = back["proj"]
+    wo_keep, wo_near = back["out"]
+
+    backward, fc_x, fc_y, proj_x, proj_y, proj_last_x, proj_last_y, wo_near = after(
+        (backward, fc_x, fc_y, proj_x, proj_y, proj_last_x, proj_last_y, wo_near)
+    )
+    fc_far = [added(fc_grads[0][:, chunk:], fc_x[:, chunk:]), added(fc_grads[2][:, chunk:], fc_y[:, chunk:])]
+    fc_last_y = swap(fc_far[0], "seq", 2)
+    fc_last_x = swap(fc_far[1], "seq", 1)
     cuts = gather_sum(
-        place,
+        place, gather_proj_kernel,
+        (proj_grads[0], proj_x, proj_last_y, proj_grads[2], proj_y, proj_last_x),
+        (4 * hw, width), (chunk, width),
+    )
+    cuts_proj = [swap(cuts[k], "fsdp", 2 * k) for k in range(1, nz)]
+    grad_proj_kept = cuts[0]
+    backward = after(backward, fc_far, cuts)
+    grad_qkv = jnp.concatenate([part[i] for i in range(3) for part in backward], axis=1)
+    sent_x, sent_y, sums_early = first_back((2, 6, 5, 7), grad_qkv, unit_all, qkv_turned)
+    first_late, qkv_late = after((first, grad_qkv), sent_x)
+    wi_mine, wi_sent = core_halves(tn(first_late, qkv_late).astype(BF))
+
+    sent_x, sent_y, grad_qkv, fc_last_x, fc_last_y, wi_sent = after(
+        (sent_x, sent_y, grad_qkv, fc_last_x, fc_last_y, wi_sent)
+    )
+    got_x = swap(sent_x, "seq", 1)
+    got_y = swap(sent_y, "seq", 2)
+    cuts = gather_sum(
+        place, gather_fc_kernel,
         (fc_grads[0], fc_x, fc_last_y, fc_grads[2], fc_y, fc_last_x),
-        (proj_grads[0], proj_x, proj_last_y, proj_grads[2], proj_y, proj_last_x),
-    )
-    kept, moved = floor_sum(
-        place, [cuts[0]] + [swap(cuts[k], "fsdp", 2 * k) for k in range(1, nz)]
-    )
-    moved = swap(moved, "fsdp", 1)
-    grad_w_fc, grad_w_proj = spread(
-        place,
-        [kept] + [swap(kept, "seq", k) for k in range(1, ns)],
-        [moved] + [swap(moved, "seq", k) for k in range(1, ns)],
-    )
-
-    grad_q, grad_k, grad_v = attend_backward(lens, qkv, mixed_heads, grad_heads, log_norm, heads)
-    grad_qkv = jnp.concatenate([grad_q, grad_k, grad_v], axis=1)
-    qkv_mat = by_core(core, kept_qkv[:, :own], moved_qkv[:, :own], 1)
-    qkv_mat = xor_take(qkv_mat, floor, 0).reshape(width, 3 * local)
-    up1, up3, low2, low3, sums_early = first_back((2, 6, 5, 7), None, grad_qkv, unit_all, qkv_mat)
-    got_x1, got_x3 = swap(up1, "seq", 1), swap(up3, "seq", 1)
-    got_y2, got_y3 = swap(low2, "seq", 2), swap(low3, "seq", 2)
-    up2, low1, up0, low0, sums_late = first_back((4, 3, 0, 1), None, grad_qkv, unit_all, qkv_mat)
-    last_y = swap(added(up2, got_x3), "seq", 2)
-    last_x = swap(added(low1, got_y3), "seq", 1)
-    tile = pl.BlockSpec((half, width), lambda: (0, 0))
-
-    def last(keep, got, end, rows):
+        (width, 4 * hw), (width, chunk),
+    )
+    far_late, kept_late, sums_late = first_back((4, 3, 0, 1), grad_qkv, unit_all, qkv_turned)
+
+    cuts_proj, cuts, far_late, wi_sent = after((cuts_proj, cuts, far_late, wi_sent))
+    wi_got = swap(wi_sent, "fsdp", 1)
+    proj_owned = grad_proj_kept.astype(F32)
+    for part in cuts_proj:
+        proj_owned = proj_owned + part.astype(F32)
+    proj_owned = proj_owned.astype(BF)
+    cuts, wi_got = after((cuts, wi_got))
+    cuts_fc = [swap(cuts[k], "fsdp", 2 * k) for k in range(1, nz)]
+    fc_kept = cuts[0]
+
+    got_x, got_y, wi_got = after((got_x, got_y, wi_got))
+    last_y = swap(added(far_late[:half], got_x[half:]), "seq", 2)
+    last_x = swap(added(far_late[half:], got_y[half:]), "seq", 1)
+    wi_keep, wi_sent = halves(wi_mine.astype(F32) + wi_got.astype(F32), floor // 2)
+
+    last_x, last_y, proj_owned, wo_near = after((last_x, last_y, proj_owned, wo_near))
+    proj_finals = [proj_owned] + [swap(proj_owned, "seq", k) for k in range(1, ns)]
+
+    def last(at, end, got):
+        block = pl.BlockSpec((half, width), lambda i: (at, 0))
+        first_block = pl.BlockSpec((half, width), lambda i: (0, 0))
         return pl.pallas_call(
             last_kernel,
             out_shape=jax.ShapeDtypeStruct((half, width), F32),
-            in_specs=[tile] * 5 + [pl.BlockSpec((1, width), lambda: (0, 0))],
-            out_specs=tile,
+            grid=(1,),
+            in_specs=[block, first_block, first_block, block, block]
+            + [pl.BlockSpec((1, width), lambda i: (0, 0))],
+            out_specs=first_block,
+            cost_estimate=cost(3),
             name="last",
-        )(keep, got, end, token_block[rows], grad_hidden[rows], gain_a)
-
-    input_grad = jnp.concatenate(
-        [
-            last(up0, got_x1, last_y, slice(0, half)),
-            last(low0, got_y2, last_x, slice(half, toks)),
-        ],
-        axis=0,
-    )[None]
-
-    def over_floors(grad):
-        cut = grad.reshape(nz, 2, own, -1)
-        total = pick(cut, core, 1).astype(F32) + swap(pick(cut, 1 - core, 1), "fsdp", 1).astype(F32)
-        owned = pick(total, floor, 0)
-        for k in range(1, nz):
-            owned = owned + swap(pick(total, floor ^ k, 0).astype(BF), "fsdp", 2 * k).astype(F32)
-        return owned
-
-    grad_w_out = over_floors(tn(mixed, grad_attn).astype(BF))
+        )(kept_late, got, end, token_block, grad_hidden, gain_a)
+
+    input_grad = jnp.concatenate([last(0, last_y, got_x), last(1, last_x, got_y)], axis=0)[None]
+
+    cuts_fc, wi_sent, last_x = after((cuts_fc, wi_sent, last_x))
+    wi_far = swap(wi_sent, "fsdp", 4)
+    fc_owned = fc_kept.astype(F32)
+    for part in cuts_fc:
+        fc_owned = fc_owned + part.astype(F32)
+    fc_mine, fc_sent = halves(fc_owned, core)
+    fc_final = jnp.concatenate([fc_mine.astype(BF), swap(fc_sent, "fsdp", 1)], axis=0)
+    fc_finals = [fc_final] + [swap(fc_final, "seq", k) for k in range(1, ns)]
+    grad_w_out = wo_keep + wo_near.astype(F32)
     for bit in (1, 2):
         grad_w_out = grad_w_out + swap(grad_w_out.astype(BF), "seq", bit).astype(F32)
-
-    in_owned = over_floors(tn(first, grad_qkv).astype(BF)).astype(BF)
-    in_blocks = jnp.stack(
-        [in_owned.reshape(own, 3, local)]
-        + [swap(in_owned, "seq", k).reshape(own, 3, local) for k in range(1, ns)],
+    grad_w_proj = spread(place, spread_proj_kernel, proj_finals, (4 * hw, width))
+    wi_keep, wi_sent = halves(wi_keep + wi_far.astype(F32), floor % 2)
+    wi_owned = (wi_keep + swap(wi_sent, "fsdp", 2).astype(F32)).astype(BF)
+    wi_blocks = jnp.stack(
+        [wi_owned.reshape(own, 3, local)]
+        + [swap(wi_owned, "seq", k).reshape(own, 3, local) for k in range(1, ns)],
         axis=2,
     )
-    grad_w_qkv = xor_take(in_blocks, me, 2).reshape(own, 3 * width).astype(F32)
+    grad_w_qkv = xor_take(wi_blocks, me, 2).reshape(own, 3 * width).astype(F32)
+    grad_w_fc = spread(place, spread_fc_kernel, fc_finals, (own, 32 * hw))
+    output = output[None]
 
     def placed(values):
         slots = jnp.arange(ns)[:, None] == me
@@ -1463,7 +1669,8 @@
 
     spots = {}
     for i, (q, part) in enumerate(order):
-        spots[q, part] = fc_bias_sum[0, i * chunk : (i + 1) * chunk].reshape(2, hw)
+        here = (sum_upper, sum_lower)[part][0, (i % 4) * chunk : (i % 4 + 1) * chunk]
+        spots[q, part] = here.reshape(2, hw)
     fc_bias_grad = jnp.stack(
         [jnp.concatenate([spots[q, 0], spots[q, 1]], axis=0) for q in range(ns)], axis=1
     )
@@ -1472,11 +1679,12 @@
         (jnp.arange(2) == core)[None, :, None, None], fc_bias_grad[:, None], 0.0
     ).reshape(-1)
     sums_one = sums_early + sums_late
+    qkv_sum = jnp.sum(grad_qkv.astype(F32), axis=0)
     vector_grads = [
         sums_one[0],
         sums_one[1],
-        placed(jnp.sum(grad_q.astype(F32), axis=0)),
-        placed(jnp.sum(grad_v.astype(F32), axis=0)),
+        placed(qkv_sum[:local]),
+        placed(qkv_sum[2 * local :]),
         sums_two[0],
         sums_two[1],
         sums_two[2],
@@ -1484,6 +1692,7 @@
         sums_two[3],
     ]
     vector_sum = jnp.concatenate([v.reshape(-1, width) for v in vector_grads], axis=0)
+    vector_sum = after(vector_sum, cuts_fc)
     for axis, size in (("seq", ns), ("fsdp", nf)):
         bit = 1
         while bit < size:

time: 582 us -> 494 us (0.85)
  waiting for transfers between devices: 172 us -> 92.4 us
  starting transfers between devices: 111 us -> 89.5 us
    ppermute x77 -> x74, waiting for transfers between devices: 172 us -> 92.4 us  [swap(): return lax.ppermute(values, axis, [(i, i ^ bits) for i in range(size)])]
    ppermute x77 -> x74, starting transfers between devices: 111 us -> 89.5 us  [swap(): return lax.ppermute(values, axis, [(i, i ^ bits) for i in range(size)])]
    unnamed x155 -> x165, local copies, waits for them, and re-layouts: 14.2 us -> 17.5 us
    pallas_call x1 -> x2, Pallas kernels: 40.4 us -> 43.2 us  [attend_backward(): pl.pallas_call(functools.partial(backward_kernel, rows, block_rows, per_p...]
    convert_element_type x6 -> x5, other arithmetic: 11.6 us -> 10.2 us  [added(): return (left.astype(F32) + right.astype(F32)).astype(BF)]
    pallas_call x8 -> x14, Pallas kernels: 112 us -> 111 us  [the longest x2 39.4 us: attend_forward(): pl.pallas_call(kernel, out_shape=(jax.ShapeDtypeStruct((total, width), BF...]
  transfers between devices with their start and end apart: 77 -> 74, of which waited for: 30 -> 28; matrix products, arithmetic and copies ran while one was open for 13% -> 16% of each run, Pallas kernels for 26% -> 31%
where the time goes in v2:
time: 494 us; the launch traced here: 485 us
  Pallas kernels  199 us (40%)
  waiting for transfers between devices  92.4 us (19%)
  starting transfers between devices  89.5 us (18%)
  other arithmetic  39 us (8%)
  local copies, waits for them, and re-layouts  36.8 us (7%)
  matrix products  25.6 us (5%)
    ppermute x74, waiting for transfers between devices, swap(): return lax.ppermute(values, axis, [(i, i ^ bits) for i in range(size)])  92.4 us
    ppermute x74, starting transfers between devices, swap(): return lax.ppermute(values, axis, [(i, i ^ bits) for i in range(size)])  89.5 us
    pallas_call x2, Pallas kernels, attend_backward(): pl.pallas_call(functools.partial(backward_kernel, rows, block_rows, per_p...  43.2 us
    pallas_call x2, Pallas kernels, attend_forward(): pl.pallas_call(kernel, out_shape=(jax.ShapeDtypeStruct((total, width), BF...  39.4 us
    pallas_call x1, Pallas kernels, feed(): pl.pallas_call(functools.partial(feed_kernel, hw), out_shape=(half, half,...  34.5 us
    dot_general x10, matrix products, tn(): lax.dot_general(left, right, (((0,), (0,)), ((), ())), preferred_element_...  25.6 us
    unnamed x165, local copies, waits for them, and re-layouts  17.5 us
    pallas_call x2, Pallas kernels, first_back(): pl.pallas_call(functools.partial(first_back_kernel, tiles), out_shape=tup...  15.2 us
  transfers between devices with their start and end apart: 74, of which 28 were waited for; matrix products, arithmetic and copies ran while one was open for 16% of the time, Pallas kernels for 31%

profile of v2, /device:TPU:0, one launch (start us, length us, event | category | flops | bytes accessed | tf_op | source)
XLA Modules:
  0.0 485.5 jit_solution(17598667182060331918)
XLA Ops:
  0.6 3.0 collective-permute-start
  5.9 3.6 pack_shares.1
  9.4 2.3 copy.39
  15.4 2.6 collective-permute-start.3
  18.9 2.4 join_rows.1
  21.3 4.9 %collective-permute-done.2 = bf16[144,768]{1,0:T(8,128)(2,1)S(1)} collective-permute-done((bf16[144,768]{1,0:T(8,128)(2,1)}, bf16[144,768]{1,0:T(8,128)(2,1)S(1)}, u32[]{:S(2)}, u32[]{:S(2)}) %collective-permute-start.2) | collective-permute-done | bytes 221216 | tf_op jit(solution)/shard_map/ppermute | solution.py:26
  26.2 8.3 %collective-permute-done.3 = bf16[144,768]{1,0:T(8,128)(2,1)} collective-permute-done((bf16[144,768]{1,0:T(8,128)(2,1)}, bf16[144,768]{1,0:T(8,128)(2,1)}, u32[]{:S(2)}, u32[]{:S(2)}) %collective-permute-start.3) | collective-permute-done | bytes 221216 | tf_op jit(solution)/shard_map/ppermute | solution.py:26
  39.1 5.6 %collective-permute-start.10 = (bf16[384,512]{1,0:T(8,128)(2,1)}, bf16[384,512]{1,0:T(8,128)(2,1)}, u32[]{:S(2)}, u32[]{:S(2)}) collective-permute-start(bf16[384,512]{1,0:T(8,128)(2,1)} %join_rows.1), channel_id=1, source_target_pairs={{0,4},{1,5},{2,6},{3,7},{4,0},{5,1},{6,2},{7,3},{8,12},{9,13},{10,... | collective-permute-start | bytes 1179656 | tf_op jit(solution)/shard_map/ppermute | solution.py:26
  52.8 13.9 %project.1 = (bf16[2048,1024]{1,0:T(8,128)(2,1)}, bf16[2048,1024]{1,0:T(8,128)(2,1)}, bf16[2048,768]{1,0:T(8,128)(2,1)}, bf16[768,1024]{1,0:T(8,128)(2,1)}) custom-call(s32[3]{0:T(128)} %pad_add_fusion.place, bf16[512,1024]{1,0:T(8,128)(2,1)} %bitcast.166, bf16[512,1024]{1,0:T(8,128)(2,1)} %copy-done.18, bf16[512,1024]{1,0:T(8,128)(2,1)} %copy-done.19, ...), custom_call_target="tpu_custom_call" | custom-call | flops 13800000 | tf_op jit(solution)/shard_map/project/pallas_call | solution.py:931
  66.7 5.2 %collective-permute-done.10.refs_1_ = bf16[384,512]{1,0:T(8,128)(2,1)} collective-permute-done((bf16[384,512]{1,0:T(8,128)(2,1)}, bf16[384,512]{1,0:T(8,128)(2,1)}, u32[]{:S(2)}, u32[]{:S(2)}) %collective-permute-start.10) | collective-permute-done | bytes 393248 | tf_op jit(solution)/shard_map/ppermute | solution.py:26
  72.3 2.3 joined.4.refs_6_.a0
  77.7 7.7 %collective-permute-start.14 = (bf16[128,1024]{1,0:T(8,128)(2,1)S(1)}, bf16[128,1024]{1,0:T(8,128)(2,1)S(1)}, u32[]{:S(2)}, u32[]{:S(2)}) collective-permute-start(bf16[128,1024]{1,0:T(8,128)(2,1)S(1)} %copy-done.70), channel_id=1, source_target_pairs={{0,2},{1,3},{2,0},{3,1},{4,6},{5,7},{6,4},{7,5},{8,10},{9,11},{10,... | collective-permute-start | bytes 786440 | tf_op jit(solution)/shard_map/ppermute | solution.py:26
  85.4 2.4 collective-permute-start.16
  89.0 19.7 %attend_forward.2 = (bf16[2048,256]{1,0:T(8,128)(2,1)}, f32[8,1,512]{2,1,0:T(1,128)}) custom-call(s32[4]{0:T(128)} %pad_add_fusion.1.lens, bf16[2048,768]{1,0:T(8,128)(2,1)} %get-tuple-element.204.q_ref.k_ref.v_ref, bf16[2048,768]{1,0:T(8,128)(2,1)} %get-tuple-element.204.q_ref.k_ref.v_ref, bf16[2048,768]{1,0:T(8,128)(2,1)} %get-tuple-element.204.q_ref.k_ref.v_ref), custom_call_target="tpu_custom_call" | custom-call | flops 17250000 | tf_op jit(solution)/shard_map/attend_forward/pallas_call | solution.py:327
  109.5 2.3 joined.5.b0
  117.6 19.7 %attend_forward.3 = (bf16[2048,256]{1,0:T(8,128)(2,1)}, f32[8,1,512]{2,1,0:T(1,128)}) custom-call(s32[4]{0:T(128)} %pad_add_fusion.1.lens, bf16[2048,768]{1,0:T(8,128)(2,1)} %get-tuple-element.204.q_ref.k_ref.v_ref, bf16[2048,768]{1,0:T(8,128)(2,1)} %get-tuple-element.204.q_ref.k_ref.v_ref, ...), custom_call_target="tpu_custom_call", output_to_operand_aliasing={{0}: (4, {})} | custom-call | flops 17250000 | tf_op jit(solution)/shard_map/attend_forward/pallas_call | solution.py:327
  137.3 5.0 %collective-permute-done.17.refs_0_ = bf16[576,512]{1,0:T(8,128)(2,1)} collective-permute-done((bf16[576,512]{1,0:T(8,128)(2,1)}, bf16[576,512]{1,0:T(8,128)(2,1)}, u32[]{:S(2)}, u32[]{:S(2)}) %collective-permute-start.17) | collective-permute-done | bytes 589856 | tf_op jit(solution)/shard_map/ppermute | solution.py:26
  147.6 2.4 joined.6.refs_9_.a3
  150.0 2.2 collective-permute-done.21.refs_1_
  152.2 3.9 collective-permute-done.22.refs_2_
  156.9 7.5 %attn_out.1 = (f32[512,1024]{1,0:T(8,128)}, bf16[512,1024]{1,0:T(8,128)(2,1)}, bf16[512,1024]{1,0:T(8,128)(2,1)}, bf16[1024,1024]{1,0:T(8,128)(2,1)}) custom-call(s32[3]{0:T(128)} %pad_add_fusion.place, bf16[2048,256]{1,0:T(8,128)(2,1)} %get-tuple-element.212.refs_0_.out_ref, bf16[512,256]{1,0:T(8,128)(2,1)} %copy-done.44, bf16[512,256]{1,0:T(8,128)(2,1)} %copy-done.45, ...), custom_call_target="tpu_custom_call" | custom-call | flops 8050000 | tf_op jit(solution)/shard_map/attn_out/pallas_call | solution.py:1014
  168.0 9.3 %collective-permute-done.26.refs_0_ = bf16[192,1024]{1,0:T(8,128)(2,1)S(1)} collective-permute-done((bf16[192,1024]{1,0:T(8,128)(2,1)S(1)}, bf16[192,1024]{1,0:T(8,128)(2,1)S(1)}, u32[]{:S(2)}, u32[]{:S(2)}) %collective-permute-start.26) | collective-permute-done | bytes 393248 | tf_op jit(solution)/shard_map/ppermute | solution.py:26
  178.7 2.0 joined.7.b3
  183.4 3.5 pad_maximum_fusion.branch_ref
  186.8 34.5 %feed.1 = (bf16[1024,1024]{1,0:T(8,128)(2,1)}, bf16[1024,1024]{1,0:T(8,128)(2,1)}, bf16[1024,1024]{1,0:T(8,128)(2,1)}, bf16[1024,1024]{1,0:T(8,128)(2,1)}, f32[5...) custom-call(s32[3]{0:T(128)} %pad_add_fusion.place, ...), custom_call_target="tpu_custom_call" | custom-call | flops 40250000 | tf_op jit(solution)/shard_map/feed/pallas_call | solution.py:1146
  222.0 2.3 collective-permute-done.28.oth_ref
  225.2 8.3 %mixed_back.1 = (f32[512,1024]{1,0:T(8,128)}, bf16[512,1024]{1,0:T(8,128)(2,1)}, bf16[512,256]{1,0:T(8,128)(2,1)}, bf16[512,256]{1,0:T(8,128)(2,1)}, bf16[512,25...) custom-call(s32[3]{0:T(128)} %pad_add_fusion.place, f32[512,1024]{1,0:T(8,128)} %get-tuple-element.220.own_ref, ...), custom_call_target="tpu_custom_call" | custom-call | flops 8050000 | tf_op jit(solution)/shard_map/mixed_back/pallas_call | solution.py:1228
  233.5 3.6 convolution_convert_fusion.6
  242.1 2.2 convolution_convert_fusion.8
  244.7 2.2 convolution_convert_fusion.9.pa
  247.7 5.6 %collective-permute-done.30 = bf16[512,256]{1,0:T(8,128)(2,1)S(1)} collective-permute-done((bf16[512,256]{1,0:T(8,128)(2,1)S(1)}, bf16[512,256]{1,0:T(8,128)(2,1)S(1)}, u32[]{:S(2)}, u32[]{:S(2)}) %collective-permute-start.30) | collective-permute-done | bytes 262176 | tf_op jit(solution)/shard_map/ppermute | solution.py:26
  256.2 2.3 convolution_convert_fusion.2
  259.9 2.2 convolution_convert_fusion.4
  264.9 2.4 convolution_convert_fusion.5.fa
  267.3 2.9 add_convert_fusion
  271.7 2.2 collective-permute-start.36
  275.8 21.7 %attend_backward.2 = (bf16[2048,128]{1,0:T(8,128)(2,1)}, bf16[2048,128]{1,0:T(8,128)(2,1)}, bf16[2048,128]{1,0:T(8,128)(2,1)}) custom-call(s32[4]{0:T(128)} %pad_add_fusion.1.lens, bf16[2048,768]{1,0:T(8,128)(2,1)} %get-tuple-element.204.q_ref.k_ref.v_ref, bf16[2048,768]{1,0:T(8,128)(2,1)} %get-tuple-element.204.q_ref.k_ref.v_ref, ...), custom_call_target="tpu_custom_call" | custom-call | flops 20700000 | tf_op jit(solution)/shard_map/attend_backward/pallas_call | solution.py:373
  297.5 2.2 add_convert_fusion.5
  306.3 21.5 %attend_backward.3 = (bf16[2048,128]{1,0:T(8,128)(2,1)}, bf16[2048,128]{1,0:T(8,128)(2,1)}, bf16[2048,128]{1,0:T(8,128)(2,1)}) custom-call(s32[4]{0:T(128)} %pad_add_fusion.1.lens, bf16[2048,768]{1,0:T(8,128)(2,1)} %get-tuple-element.204.q_ref.k_ref.v_ref, bf16[2048,768]{1,0:T(8,128)(2,1)} %get-tuple-element.204.q_ref.k_ref.v_ref, ...), custom_call_target="tpu_custom_call" | custom-call | flops 20700000 | tf_op jit(solution)/shard_map/attend_backward/pallas_call | solution.py:373
  328.0 2.2 add_convert_fusion.3
  331.3 2.0 add_convert_fusion.4
  334.4 4.1 gather_sum.2
  347.7 7.6 %first_back.2 = (bf16[512,1024]{1,0:T(8,128)(2,1)}, bf16[512,1024]{1,0:T(8,128)(2,1)}, f32[2,1024]{1,0:T(2,128)}) custom-call(s32[4]{0:T(128)} %constant.153.clone.place, bf16[2048,768]{1,0:T(8,128)(2,1)} %copy-done.1, bf16[2048,1024]{1,0:T(8,128)(2,1)} %get-tuple-element.300.unit_ref, bf16[768,1024]{1,0:T(8,128)(2,1)} %get-tuple-element.301.mat_ref), custom_call_target="tpu_custom_call" | custom-call | flops 5750000 | tf_op jit(solution)/shard_map/first_back/pallas_call | solution.py:1285
  355.2 6.7 %convolution_convert_fusion.1 = bf16[1024,768]{1,0:T(8,128)(2,1)S(1)} fusion(bf16[2048,1024]{1,0:T(8,128)(2,1)} %get-tuple-element.305, bf16[2048,768]{1,0:T(8,128)(2,1)} %copy-done.1), kind=kOutput, calls=%fused_computation.6 | convolution fusion | flops 3222011904 | bytes 8912896 | tf_op jit(solution)/shard_map/dot_general | solution.py:432
  365.1 4.2 gather_sum.3
  369.3 7.6 %first_back.3 = (bf16[512,1024]{1,0:T(8,128)(2,1)}, bf16[512,1024]{1,0:T(8,128)(2,1)}, f32[2,1024]{1,0:T(2,128)}) custom-call(s32[4]{0:T(128)} %constant.154.clone.place, bf16[2048,768]{1,0:T(8,128)(2,1)} %copy-done.1, bf16[2048,1024]{1,0:T(8,128)(2,1)} %get-tuple-element.300.unit_ref, bf16[768,1024]{1,0:T(8,128)(2,1)} %get-tuple-element.301.mat_ref), custom_call_target="tpu_custom_call" | custom-call | flops 5750000 | tf_op jit(solution)/shard_map/first_back/pallas_call | solution.py:1285
  377.8 2.0 add_convert_fusion.7.refs_0_
  379.9 4.3 collective-permute-done.44.got_ref
  384.8 2.6 add_convert_fusion.1
  391.0 2.2 collective-permute-start.53
  402.1 6.9 %collective-permute-done.53 = bf16[256,512]{1,0:T(8,128)(2,1)S(1)} collective-permute-done((bf16[256,512]{1,0:T(8,128)(2,1)}, bf16[256,512]{1,0:T(8,128)(2,1)S(1)}, u32[]{:S(2)}, u32[]{:S(2)}) %collective-permute-start.53) | collective-permute-done | bytes 262176 | tf_op jit(solution)/shard_map/ppermute | solution.py:26
  411.4 2.0 collective-permute-done.55
  415.0 4.4 collective-permute-start.60
  420.3 3.7 last.3
  424.0 3.7 last.2
  429.3 3.1 maximum_bitcast_fusion
  432.5 6.6 %collective-permute-done.58 = f32[12,1024]{1,0:T(8,128)S(1)} collective-permute-done((f32[12,1024]{1,0:T(8,128)S(1)}, f32[12,1024]{1,0:T(8,128)S(1)}, u32[]{:S(2)}, u32[]{:S(2)}) %collective-permute-start.58) | collective-permute-done | bytes 49184 | tf_op jit(solution)/shard_map/ppermute | solution.py:26
  441.1 4.7 collective-permute-done.59
  451.7 3.6 collective-permute-done.65
  459.6 3.3 spread.3
  462.9 3.0 collective-permute-done.70.refs_3_
  466.6 3.5 spread.2
  476.7 2.2 collective-permute-done.62
  479.1 2.2 collective-permute-done.63
  (390 shorter events, 126.7 us)
Async XLA Ops:
  0.6 33.8 %collective-permute-start = (bf16[512,1024]{1,0:T(8,128)(2,1)}, bf16[512,1024]{1,0:T(8,128)(2,1)S(1)}, u32[]{:S(2)}, u32[]{:S(2)}) collective-permute-start(bf16[512,1024]{1,0:T(8,128)(2,1)} %bitcast.164), channel_id=1, source_target_pairs={{0,8},{8,0},{16,24},{24,16},{1,9},{9,1},{17,25},{25,17},{2,10},{10... | collective-permute-start | bytes 3145736 | tf_op jit(solution)/shard_map/ppermute | solution.py:26
  3.7 30.8 %collective-permute-start.1 = (bf16[512,1024]{1,0:T(8,128)(2,1)}, bf16[512,1024]{1,0:T(8,128)(2,1)S(1)}, u32[]{:S(2)}, u32[]{:S(2)}) collective-permute-start(bf16[512,1024]{1,0:T(8,128)(2,1)} %bitcast.165), channel_id=1, source_target_pairs={{0,16},{8,24},{16,0},{24,8},{1,17},{9,25},{17,1},{25,9},{2,18},{10... | collective-permute-start | bytes 3145736 | tf_op jit(solution)/shard_map/ppermute | solution.py:26
  13.8 12.4 %collective-permute-start.2 = (bf16[144,768]{1,0:T(8,128)(2,1)}, bf16[144,768]{1,0:T(8,128)(2,1)S(1)}, u32[]{:S(2)}, u32[]{:S(2)}) collective-permute-start(bf16[144,768]{1,0:T(8,128)(2,1)} %get-tuple-element.384), channel_id=1, source_target_pairs={{0,2},{1,3},{2,0},{3,1},{4,6},{5,7},{6,4},{7,5},{8,10},{9,11},{10,... | collective-permute-start | bytes 663560 | tf_op jit(solution)/shard_map/ppermute | solution.py:26
  15.4 19.0 %collective-permute-start.3 = (bf16[144,768]{1,0:T(8,128)(2,1)}, bf16[144,768]{1,0:T(8,128)(2,1)}, u32[]{:S(2)}, u32[]{:S(2)}) collective-permute-start(bf16[144,768]{1,0:T(8,128)(2,1)} %get-tuple-element.384), channel_id=1, source_target_pairs={{0,4},{1,5},{2,6},{3,7},{4,0},{5,1},{6,2},{7,3},{8,12},{9,13},{10,... | collective-permute-start | bytes 663560 | tf_op jit(solution)/shard_map/ppermute | solution.py:26
  18.0 16.5 %collective-permute-start.4 = (bf16[144,768]{1,0:T(8,128)(2,1)}, bf16[144,768]{1,0:T(8,128)(2,1)}, u32[]{:S(2)}, u32[]{:S(2)}) collective-permute-start(bf16[144,768]{1,0:T(8,128)(2,1)} %get-tuple-element.384), channel_id=1, source_target_pairs={{0,6},{1,7},{2,4},{3,5},{4,2},{5,3},{6,0},{7,1},{8,14},{9,15},{10,... | collective-permute-start | bytes 663560 | tf_op jit(solution)/shard_map/ppermute | solution.py:26
  37.2 14.4 %collective-permute-start.6 = (bf16[256,1024]{1,0:T(8,128)(2,1)}, bf16[256,1024]{1,0:T(8,128)(2,1)S(1)}, u32[]{:S(2)}, u32[]{:S(2)}) collective-permute-start(bf16[256,1024]{1,0:T(8,128)(2,1)} %slice.255), channel_id=1, source_target_pairs={{0,8},{8,0},{16,24},{24,16},{1,9},{9,1},{17,25},{25,17},{2,10},{10... | collective-permute-start | bytes 1572872 | tf_op jit(solution)/shard_map/ppermute | solution.py:26
  38.5 14.2 %collective-permute-start.7 = (bf16[256,1024]{1,0:T(8,128)(2,1)}, bf16[256,1024]{1,0:T(8,128)(2,1)}, u32[]{:S(2)}, u32[]{:S(2)}) collective-permute-start(bf16[256,1024]{1,0:T(8,128)(2,1)} %slice.256), channel_id=1, source_target_pairs={{0,16},{8,24},{16,0},{24,8},{1,17},{9,25},{17,1},{25,9},{2,18},{10... | collective-permute-start | bytes 1572872 | tf_op jit(solution)/shard_map/ppermute | solution.py:26
  39.1 32.8 %collective-permute-start.10 = (bf16[384,512]{1,0:T(8,128)(2,1)}, bf16[384,512]{1,0:T(8,128)(2,1)}, u32[]{:S(2)}, u32[]{:S(2)}) collective-permute-start(bf16[384,512]{1,0:T(8,128)(2,1)} %join_rows.1), channel_id=1, source_target_pairs={{0,4},{1,5},{2,6},{3,7},{4,0},{5,1},{6,2},{7,3},{8,12},{9,13},{10,... | collective-permute-start | bytes 1179656 | tf_op jit(solution)/shard_map/ppermute | solution.py:26
  44.7 27.2 %collective-permute-start.11 = (bf16[384,512]{1,0:T(8,128)(2,1)}, bf16[384,512]{1,0:T(8,128)(2,1)}, u32[]{:S(2)}, u32[]{:S(2)}) collective-permute-start(bf16[384,512]{1,0:T(8,128)(2,1)} %join_rows.1), channel_id=1, source_target_pairs={{0,6},{1,7},{2,4},{3,5},{4,2},{5,3},{6,0},{7,1},{8,14},{9,15},{10,... | collective-permute-start | bytes 1179656 | tf_op jit(solution)/shard_map/ppermute | solution.py:26
  46.0 26.3 %collective-permute-start.9 = (bf16[384,512]{1,0:T(8,128)(2,1)}, bf16[384,512]{1,0:T(8,128)(2,1)}, u32[]{:S(2)}, u32[]{:S(2)}) collective-permute-start(bf16[384,512]{1,0:T(8,128)(2,1)} %join_rows.1), channel_id=1, source_target_pairs={{0,2},{1,3},{2,0},{3,1},{4,6},{5,7},{6,4},{7,5},{8,10},{9,11},{10,... | collective-permute-start | bytes 1179656 | tf_op jit(solution)/shard_map/ppermute | solution.py:26
  74.7 34.0 %collective-permute-start.12 = (bf16[1152,512]{1,0:T(8,128)(2,1)}, bf16[1152,512]{1,0:T(8,128)(2,1)S(1)}, u32[]{:S(2)}, u32[]{:S(2)}) collective-permute-start(bf16[1152,512]{1,0:T(8,128)(2,1)} %joined.4.refs_6_.a0), channel_id=1, source_target_pairs={{0,8},{8,0},{16,24},{24,16},{1,9},{9,1},{17,25},{25,17},{2,10},{10... | collective-permute-start | bytes 3538952 | tf_op jit(solution)/shard_map/ppermute | solution.py:26
  76.1 32.6 %collective-permute-start.13 = (bf16[1152,512]{1,0:T(8,128)(2,1)}, bf16[1152,512]{1,0:T(8,128)(2,1)S(1)}, u32[]{:S(2)}, u32[]{:S(2)}) collective-permute-start(bf16[1152,512]{1,0:T(8,128)(2,1)} %joined.4.refs_6_.a0), channel_id=1, source_target_pairs={{0,16},{8,24},{16,0},{24,8},{1,17},{9,25},{17,1},{25,9},{2,18},{10... | collective-permute-start | bytes 3538952 | tf_op jit(solution)/shard_map/ppermute | solution.py:26
  77.7 31.0 %collective-permute-start.14 = (bf16[128,1024]{1,0:T(8,128)(2,1)S(1)}, bf16[128,1024]{1,0:T(8,128)(2,1)S(1)}, u32[]{:S(2)}, u32[]{:S(2)}) collective-permute-start(bf16[128,1024]{1,0:T(8,128)(2,1)S(1)} %copy-done.70), channel_id=1, source_target_pairs={{0,2},{1,3},{2,0},{3,1},{4,6},{5,7},{6,4},{7,5},{8,10},{9,11},{10,... | collective-permute-start | bytes 786440 | tf_op jit(solution)/shard_map/ppermute | solution.py:26
  85.4 23.3 %collective-permute-start.15 = (bf16[128,1024]{1,0:T(8,128)(2,1)S(1)}, bf16[128,1024]{1,0:T(8,128)(2,1)S(1)}, u32[]{:S(2)}, u32[]{:S(2)}) collective-permute-start(bf16[128,1024]{1,0:T(8,128)(2,1)S(1)} %copy-done.70), channel_id=1, source_target_pairs={{0,4},{1,5},{2,6},{3,7},{4,0},{5,1},{6,2},{7,3},{8,12},{9,13},{10,... | collective-permute-start | bytes 786440 | tf_op jit(solution)/shard_map/ppermute | solution.py:26
  85.4 23.3 %collective-permute-start.16 = (bf16[128,1024]{1,0:T(8,128)(2,1)S(1)}, bf16[128,1024]{1,0:T(8,128)(2,1)S(1)}, u32[]{:S(2)}, u32[]{:S(2)}) collective-permute-start(bf16[128,1024]{1,0:T(8,128)(2,1)S(1)} %copy-done.70), channel_id=1, source_target_pairs={{0,6},{1,7},{2,4},{3,5},{4,2},{5,3},{6,0},{7,1},{8,14},{9,15},{10,... | collective-permute-start | bytes 786440 | tf_op jit(solution)/shard_map/ppermute | solution.py:26
  111.8 30.8 %collective-permute-start.19 = (bf16[384,1024]{1,0:T(8,128)(2,1)}, bf16[384,1024]{1,0:T(8,128)(2,1)S(1)}, u32[]{:S(2)}, u32[]{:S(2)}) collective-permute-start(bf16[384,1024]{1,0:T(8,128)(2,1)} %joined.5.b0), channel_id=1, source_target_pairs={{0,8},{8,0},{16,24},{24,16},{1,9},{9,1},{17,25},{25,17},{2,10},{10... | collective-permute-start | bytes 2359304 | tf_op jit(solution)/shard_map/ppermute | solution.py:26
  112.4 30.2 %collective-permute-start.20 = (bf16[384,1024]{1,0:T(8,128)(2,1)}, bf16[384,1024]{1,0:T(8,128)(2,1)}, u32[]{:S(2)}, u32[]{:S(2)}) collective-permute-start(bf16[384,1024]{1,0:T(8,128)(2,1)} %joined.5.b0), channel_id=1, source_target_pairs={{0,16},{8,24},{16,0},{24,8},{1,17},{9,25},{17,1},{25,9},{2,18},{10... | collective-permute-start | bytes 2359304 | tf_op jit(solution)/shard_map/ppermute | solution.py:26
  113.7 28.6 %collective-permute-start.17 = (bf16[576,512]{1,0:T(8,128)(2,1)}, bf16[576,512]{1,0:T(8,128)(2,1)}, u32[]{:S(2)}, u32[]{:S(2)}) collective-permute-start(bf16[576,512]{1,0:T(8,128)(2,1)} %slice.270), channel_id=1, source_target_pairs={{0,8},{8,0},{16,24},{24,16},{1,9},{9,1},{17,25},{25,17},{2,10},{10... | collective-permute-start | bytes 1769480 | tf_op jit(solution)/shard_map/ppermute | solution.py:26
  116.1 26.5 %collective-permute-start.18 = (bf16[576,512]{1,0:T(8,128)(2,1)}, bf16[576,512]{1,0:T(8,128)(2,1)}, u32[]{:S(2)}, u32[]{:S(2)}) collective-permute-start(bf16[576,512]{1,0:T(8,128)(2,1)} %slice.271), channel_id=1, source_target_pairs={{0,16},{8,24},{16,0},{24,8},{1,17},{9,25},{17,1},{25,9},{2,18},{10... | collective-permute-start | bytes 1769480 | tf_op jit(solution)/shard_map/ppermute | solution.py:26
  145.6 10.5 %collective-permute-start.22 = (bf16[512,256]{1,0:T(8,128)(2,1)S(1)}, bf16[512,256]{1,0:T(8,128)(2,1)S(1)}, u32[]{:S(2)}, u32[]{:S(2)}) collective-permute-start(bf16[512,256]{1,0:T(8,128)(2,1)S(1)} %get-tuple-element.377), channel_id=1, source_target_pairs={{0,16},{8,24},{16,0},{24,8},{1,17},{9,25},{17,1},{25,9},{2,18},{10... | collective-permute-start | bytes 786440 | tf_op jit(solution)/shard_map/ppermute | solution.py:26
  146.1 10.0 %collective-permute-start.23 = (bf16[512,256]{1,0:T(8,128)(2,1)S(1)}, bf16[512,256]{1,0:T(8,128)(2,1)S(1)}, u32[]{:S(2)}, u32[]{:S(2)}) collective-permute-start(bf16[512,256]{1,0:T(8,128)(2,1)S(1)} %get-tuple-element.376), channel_id=1, source_target_pairs={{0,24},{8,16},{16,8},{24,0},{1,25},{9,17},{17,9},{25,1},{2,26},{10... | collective-permute-start | bytes 786440 | tf_op jit(solution)/shard_map/ppermute | solution.py:26
  164.4 16.4 %collective-permute-start.24 = (bf16[512,1024]{1,0:T(8,128)(2,1)}, bf16[512,1024]{1,0:T(8,128)(2,1)}, u32[]{:S(2)}, u32[]{:S(2)}) collective-permute-start(bf16[512,1024]{1,0:T(8,128)(2,1)} %get-tuple-element.216), channel_id=1, source_target_pairs={{0,1},{1,0},{2,3},{3,2},{4,5},{5,4},{6,7},{7,6},{8,9},{9,8},{10,11... | collective-permute-start | bytes 3145736 | tf_op jit(solution)/shard_map/ppermute | solution.py:26
  164.5 18.9 %collective-permute-start.25 = (bf16[512,1024]{1,0:T(8,128)(2,1)S(1)}, bf16[512,1024]{1,0:T(8,128)(2,1)}, u32[]{:S(2)}, u32[]{:S(2)}) collective-permute-start(bf16[512,1024]{1,0:T(8,128)(2,1)S(1)} %bitcast.180), channel_id=1, source_target_pairs={{0,1},{1,0},{2,3},{3,2},{4,5},{5,4},{6,7},{7,6},{8,9},{9,8},{10,11... | collective-permute-start | bytes 3145736 | tf_op jit(solution)/shard_map/ppermute | solution.py:26
  166.1 11.1 %collective-permute-start.26 = (bf16[192,1024]{1,0:T(8,128)(2,1)S(1)}, bf16[192,1024]{1,0:T(8,128)(2,1)S(1)}, u32[]{:S(2)}, u32[]{:S(2)}) collective-permute-start(bf16[192,1024]{1,0:T(8,128)(2,1)S(1)} %slice.293), channel_id=1, source_target_pairs={{0,8},{8,0},{16,24},{24,16},{1,9},{9,1},{17,25},{25,17},{2,10},{10... | collective-permute-start | bytes 1179656 | tf_op jit(solution)/shard_map/ppermute | solution.py:26
  166.8 10.8 %collective-permute-start.27 = (bf16[192,1024]{1,0:T(8,128)(2,1)S(1)}, bf16[192,1024]{1,0:T(8,128)(2,1)S(1)}, u32[]{:S(2)}, u32[]{:S(2)}) collective-permute-start(bf16[192,1024]{1,0:T(8,128)(2,1)S(1)} %slice.294), channel_id=1, source_target_pairs={{0,16},{8,24},{16,0},{24,8},{1,17},{9,25},{17,1},{25,9},{2,18},{10... | collective-permute-start | bytes 1179656 | tf_op jit(solution)/shard_map/ppermute | solution.py:26
  221.5 25.5 %collective-permute-start.32 = (bf16[512,1024]{1,0:T(8,128)(2,1)}, bf16[512,1024]{1,0:T(8,128)(2,1)}, u32[]{:S(2)}, u32[]{:S(2)}) collective-permute-start(bf16[512,1024]{1,0:T(8,128)(2,1)} %get-tuple-element.239), channel_id=1, source_target_pairs={{0,1},{1,0},{2,3},{3,2},{4,5},{5,4},{6,7},{7,6},{8,9},{9,8},{10,11... | collective-permute-start | bytes 3145736 | tf_op jit(solution)/shard_map/ppermute | solution.py:26
  238.5 9.2 %collective-permute-start.29 = (bf16[512,256]{1,0:T(8,128)(2,1)S(1)}, bf16[512,256]{1,0:T(8,128)(2,1)S(1)}, u32[]{:S(2)}, u32[]{:S(2)}) collective-permute-start(bf16[512,256]{1,0:T(8,128)(2,1)S(1)} %copy-done.73), channel_id=1, source_target_pairs={{0,8},{8,0},{16,24},{24,16},{1,9},{9,1},{17,25},{25,17},{2,10},{10... | collective-permute-start | bytes 786440 | tf_op jit(solution)/shard_map/ppermute | solution.py:26
  239.7 13.7 %collective-permute-start.30 = (bf16[512,256]{1,0:T(8,128)(2,1)S(1)}, bf16[512,256]{1,0:T(8,128)(2,1)S(1)}, u32[]{:S(2)}, u32[]{:S(2)}) collective-permute-start(bf16[512,256]{1,0:T(8,128)(2,1)S(1)} %copy-done.72), channel_id=1, source_target_pairs={{0,16},{8,24},{16,0},{24,8},{1,17},{9,25},{17,1},{25,9},{2,18},{10... | collective-permute-start | bytes 786440 | tf_op jit(solution)/shard_map/ppermute | solution.py:26
  240.3 13.1 %collective-permute-start.31 = (bf16[512,256]{1,0:T(8,128)(2,1)S(1)}, bf16[512,256]{1,0:T(8,128)(2,1)S(1)}, u32[]{:S(2)}, u32[]{:S(2)}) collective-permute-start(bf16[512,256]{1,0:T(8,128)(2,1)S(1)} %copy-done.71), channel_id=1, source_target_pairs={{0,24},{8,16},{16,8},{24,0},{1,25},{9,17},{17,9},{25,1},{2,26},{10... | collective-permute-start | bytes 786440 | tf_op jit(solution)/shard_map/ppermute | solution.py:26
  254.9 15.3 %collective-permute-start.33 = (bf16[512,1024]{1,0:T(8,128)(2,1)S(1)}, bf16[512,1024]{1,0:T(8,128)(2,1)S(1)}, u32[]{:S(2)}, u32[]{:S(2)}) collective-permute-start(bf16[512,1024]{1,0:T(8,128)(2,1)S(1)} %bitcast.195), channel_id=1, source_target_pairs={{0,1},{1,0},{2,3},{3,2},{4,5},{5,4},{6,7},{7,6},{8,9},{9,8},{10,11... | collective-permute-start | bytes 3145736 | tf_op jit(solution)/shard_map/ppermute | solution.py:26
  262.1 35.3 %collective-permute-start.34 = (bf16[512,1024]{1,0:T(8,128)(2,1)}, bf16[512,1024]{1,0:T(8,128)(2,1)}, u32[]{:S(2)}, u32[]{:S(2)}) collective-permute-start(bf16[512,1024]{1,0:T(8,128)(2,1)} %convolution_convert_fusion.8), channel_id=1, source_target_pairs={{0,8},{8,0},{16,24},{24,16},{1,9},{9,1},{17,25},{25,17},{2,10},{10... | collective-permute-start | bytes 3145736 | tf_op jit(solution)/shard_map/ppermute | solution.py:26
  263.1 34.4 %collective-permute-start.35 = (bf16[512,1024]{1,0:T(8,128)(2,1)}, bf16[512,1024]{1,0:T(8,128)(2,1)}, u32[]{:S(2)}, u32[]{:S(2)}) collective-permute-start(bf16[512,1024]{1,0:T(8,128)(2,1)} %convolution_convert_fusion.6), channel_id=1, source_target_pairs={{0,16},{8,24},{16,0},{24,8},{1,17},{9,25},{17,1},{25,9},{2,18},{10... | collective-permute-start | bytes 3145736 | tf_op jit(solution)/shard_map/ppermute | solution.py:26
  271.7 25.8 %collective-permute-start.36 = (bf16[256,1024]{1,0:T(8,128)(2,1)}, bf16[256,1024]{1,0:T(8,128)(2,1)}, u32[]{:S(2)}, u32[]{:S(2)}) collective-permute-start(bf16[256,1024]{1,0:T(8,128)(2,1)} %fusion.5), channel_id=1, source_target_pairs={{0,4},{1,5},{2,6},{3,7},{4,0},{5,1},{6,2},{7,3},{8,12},{9,13},{10,... | collective-permute-start | bytes 1572872 | tf_op jit(solution)/shard_map/ppermute | solution.py:26
  273.9 54.0 %collective-permute-start.37 = (bf16[1024,512]{1,0:T(8,128)(2,1)}, bf16[1024,512]{1,0:T(8,128)(2,1)}, u32[]{:S(2)}, u32[]{:S(2)}) collective-permute-start(bf16[1024,512]{1,0:T(8,128)(2,1)} %convolution_convert_fusion.4), channel_id=1, source_target_pairs={{0,8},{8,0},{16,24},{24,16},{1,9},{9,1},{17,25},{25,17},{2,10},{10... | collective-permute-start | bytes 3145736 | tf_op jit(solution)/shard_map/ppermute | solution.py:26
  275.1 52.8 %collective-permute-start.38 = (bf16[1024,512]{1,0:T(8,128)(2,1)}, bf16[1024,512]{1,0:T(8,128)(2,1)}, u32[]{:S(2)}, u32[]{:S(2)}) collective-permute-start(bf16[1024,512]{1,0:T(8,128)(2,1)} %convolution_convert_fusion.2), channel_id=1, source_target_pairs={{0,16},{8,24},{16,0},{24,8},{1,17},{9,25},{17,1},{25,9},{2,18},{10... | collective-permute-start | bytes 3145736 | tf_op jit(solution)/shard_map/ppermute | solution.py:26
  299.7 28.2 %collective-permute-start.40 = (bf16[256,1024]{1,0:T(8,128)(2,1)}, bf16[256,1024]{1,0:T(8,128)(2,1)S(1)}, u32[]{:S(2)}, u32[]{:S(2)}) collective-permute-start(bf16[256,1024]{1,0:T(8,128)(2,1)} %add_convert_fusion.5), channel_id=1, source_target_pairs={{0,16},{8,24},{16,0},{24,8},{1,17},{9,25},{17,1},{25,9},{2,18},{10... | collective-permute-start | bytes 1572872 | tf_op jit(solution)/shard_map/ppermute | solution.py:26
  302.3 25.6 %collective-permute-start.39 = (bf16[256,1024]{1,0:T(8,128)(2,1)S(1)}, bf16[256,1024]{1,0:T(8,128)(2,1)}, u32[]{:S(2)}, u32[]{:S(2)}) collective-permute-start(bf16[256,1024]{1,0:T(8,128)(2,1)S(1)} %add_convert_fusion.6), channel_id=1, source_target_pairs={{0,8},{8,0},{16,24},{24,16},{1,9},{9,1},{17,25},{25,17},{2,10},{10... | collective-permute-start | bytes 1572872 | tf_op jit(solution)/shard_map/ppermute | solution.py:26
  306.3 21.6 %collective-permute-start.41 = (bf16[128,1024]{1,0:T(8,128)(2,1)}, bf16[128,1024]{1,0:T(8,128)(2,1)S(1)}, u32[]{:S(2)}, u32[]{:S(2)}) collective-permute-start(bf16[128,1024]{1,0:T(8,128)(2,1)} %fusion.9), channel_id=1, source_target_pairs={{0,2},{1,3},{2,0},{3,1},{4,6},{5,7},{6,4},{7,5},{8,10},{9,11},{10,... | collective-permute-start | bytes 786440 | tf_op jit(solution)/shard_map/ppermute | solution.py:26
  330.2 33.0 %collective-permute-start.42 = (bf16[1024,256]{1,0:T(8,128)(2,1)}, bf16[1024,256]{1,0:T(8,128)(2,1)}, u32[]{:S(2)}, u32[]{:S(2)}) collective-permute-start(bf16[1024,256]{1,0:T(8,128)(2,1)} %add_convert_fusion.3), channel_id=1, source_target_pairs={{0,8},{8,0},{16,24},{24,16},{1,9},{9,1},{17,25},{25,17},{2,10},{10... | collective-permute-start | bytes 1572872 | tf_op jit(solution)/shard_map/ppermute | solution.py:26
  333.3 30.0 %collective-permute-start.43 = (bf16[1024,256]{1,0:T(8,128)(2,1)}, bf16[1024,256]{1,0:T(8,128)(2,1)}, u32[]{:S(2)}, u32[]{:S(2)}) collective-permute-start(bf16[1024,256]{1,0:T(8,128)(2,1)} %add_convert_fusion.4), channel_id=1, source_target_pairs={{0,16},{8,24},{16,0},{24,8},{1,17},{9,25},{17,1},{25,9},{2,18},{10... | collective-permute-start | bytes 1572872 | tf_op jit(solution)/shard_map/ppermute | solution.py:26
  338.5 38.4 %collective-permute-start.46 = (bf16[128,1024]{1,0:T(8,128)(2,1)}, bf16[128,1024]{1,0:T(8,128)(2,1)}, u32[]{:S(2)}, u32[]{:S(2)}) collective-permute-start(bf16[128,1024]{1,0:T(8,128)(2,1)} %get-tuple-element.291), channel_id=1, source_target_pairs={{0,2},{1,3},{2,0},{3,1},{4,6},{5,7},{6,4},{7,5},{8,10},{9,11},{10,... | collective-permute-start | bytes 786440 | tf_op jit(solution)/shard_map/ppermute | solution.py:26
  340.0 36.9 %collective-permute-start.47 = (bf16[128,1024]{1,0:T(8,128)(2,1)}, bf16[128,1024]{1,0:T(8,128)(2,1)}, u32[]{:S(2)}, u32[]{:S(2)}) collective-permute-start(bf16[128,1024]{1,0:T(8,128)(2,1)} %get-tuple-element.292), channel_id=1, source_target_pairs={{0,4},{1,5},{2,6},{3,7},{4,0},{5,1},{6,2},{7,3},{8,12},{9,13},{10,... | collective-permute-start | bytes 786440 | tf_op jit(solution)/shard_map/ppermute | solution.py:26
  341.3 35.6 %collective-permute-start.48 = (bf16[128,1024]{1,0:T(8,128)(2,1)}, bf16[128,1024]{1,0:T(8,128)(2,1)}, u32[]{:S(2)}, u32[]{:S(2)}) collective-permute-start(bf16[128,1024]{1,0:T(8,128)(2,1)} %get-tuple-element.293), channel_id=1, source_target_pairs={{0,6},{1,7},{2,4},{3,5},{4,2},{5,3},{6,0},{7,1},{8,14},{9,15},{10,... | collective-permute-start | bytes 786440 | tf_op jit(solution)/shard_map/ppermute | solution.py:26
  363.2 20.9 %collective-permute-start.44 = (bf16[512,1024]{1,0:T(8,128)(2,1)}, bf16[512,1024]{1,0:T(8,128)(2,1)}, u32[]{:S(2)}, u32[]{:S(2)}) collective-permute-start(bf16[512,1024]{1,0:T(8,128)(2,1)} %get-tuple-element.309), channel_id=1, source_target_pairs={{0,8},{8,0},{16,24},{24,16},{1,9},{9,1},{17,25},{25,17},{2,10},{10... | collective-permute-start | bytes 3145736 | tf_op jit(solution)/shard_map/ppermute | solution.py:26
  364.0 20.8 %collective-permute-start.45 = (bf16[512,1024]{1,0:T(8,128)(2,1)}, bf16[512,1024]{1,0:T(8,128)(2,1)}, u32[]{:S(2)}, u32[]{:S(2)}) collective-permute-start(bf16[512,1024]{1,0:T(8,128)(2,1)} %get-tuple-element.310), channel_id=1, source_target_pairs={{0,16},{8,24},{16,0},{24,8},{1,17},{9,25},{17,1},{25,9},{2,18},{10... | collective-permute-start | bytes 3145736 | tf_op jit(solution)/shard_map/ppermute | solution.py:26
  387.4 11.2 %collective-permute-start.50 = (bf16[256,1024]{1,0:T(8,128)(2,1)}, bf16[256,1024]{1,0:T(8,128)(2,1)}, u32[]{:S(2)}, u32[]{:S(2)}) collective-permute-start(bf16[256,1024]{1,0:T(8,128)(2,1)} %get-tuple-element.375), channel_id=1, source_target_pairs={{0,8},{8,0},{16,24},{24,16},{1,9},{9,1},{17,25},{25,17},{2,10},{10... | collective-permute-start | bytes 1572872 | tf_op jit(solution)/shard_map/ppermute | solution.py:26
  388.5 11.7 %collective-permute-start.51 = (bf16[256,1024]{1,0:T(8,128)(2,1)}, bf16[256,1024]{1,0:T(8,128)(2,1)S(1)}, u32[]{:S(2)}, u32[]{:S(2)}) collective-permute-start(bf16[256,1024]{1,0:T(8,128)(2,1)} %get-tuple-element.374), channel_id=1, source_target_pairs={{0,16},{8,24},{16,0},{24,8},{1,17},{9,25},{17,1},{25,9},{2,18},{10... | collective-permute-start | bytes 1572872 | tf_op jit(solution)/shard_map/ppermute | solution.py:26
  390.2 11.9 %collective-permute-start.52 = (bf16[256,512]{1,0:T(8,128)(2,1)}, bf16[256,512]{1,0:T(8,128)(2,1)S(1)}, u32[]{:S(2)}, u32[]{:S(2)}) collective-permute-start(bf16[256,512]{1,0:T(8,128)(2,1)} %get-tuple-element.340), channel_id=1, source_target_pairs={{0,2},{1,3},{2,0},{3,1},{4,6},{5,7},{6,4},{7,5},{8,10},{9,11},{10,... | collective-permute-start | bytes 786440 | tf_op jit(solution)/shard_map/ppermute | solution.py:26
  391.0 18.1 %collective-permute-start.53 = (bf16[256,512]{1,0:T(8,128)(2,1)}, bf16[256,512]{1,0:T(8,128)(2,1)S(1)}, u32[]{:S(2)}, u32[]{:S(2)}) collective-permute-start(bf16[256,512]{1,0:T(8,128)(2,1)} %get-tuple-element.341), channel_id=1, source_target_pairs={{0,4},{1,5},{2,6},{3,7},{4,0},{5,1},{6,2},{7,3},{8,12},{9,13},{10,... | collective-permute-start | bytes 786440 | tf_op jit(solution)/shard_map/ppermute | solution.py:26
  393.3 15.8 %collective-permute-start.54 = (bf16[256,512]{1,0:T(8,128)(2,1)}, bf16[256,512]{1,0:T(8,128)(2,1)S(1)}, u32[]{:S(2)}, u32[]{:S(2)}) collective-permute-start(bf16[256,512]{1,0:T(8,128)(2,1)} %get-tuple-element.342), channel_id=1, source_target_pairs={{0,6},{1,7},{2,4},{3,5},{4,2},{5,3},{6,0},{7,1},{8,14},{9,15},{10,... | collective-permute-start | bytes 786440 | tf_op jit(solution)/shard_map/ppermute | solution.py:26
  400.1 48.8 %collective-permute-start.71 = (bf16[128,1024]{1,0:T(8,128)(2,1)}, bf16[128,1024]{1,0:T(8,128)(2,1)}, u32[]{:S(2)}, u32[]{:S(2)}) collective-permute-start(bf16[128,1024]{1,0:T(8,128)(2,1)} %add_convert_fusion.7.refs_0_), channel_id=1, source_target_pairs={{0,8},{8,0},{16,24},{24,16},{1,9},{9,1},{17,25},{25,17},{2,10},{10... | collective-permute-start | bytes 786440 | tf_op jit(solution)/shard_map/ppermute | solution.py:26
  400.5 49.8 %collective-permute-start.72 = (bf16[128,1024]{1,0:T(8,128)(2,1)}, bf16[128,1024]{1,0:T(8,128)(2,1)}, u32[]{:S(2)}, u32[]{:S(2)}) collective-permute-start(bf16[128,1024]{1,0:T(8,128)(2,1)} %add_convert_fusion.7.refs_0_), channel_id=1, source_target_pairs={{0,16},{8,24},{16,0},{24,8},{1,17},{9,25},{17,1},{25,9},{2,18},{10... | collective-permute-start | bytes 786440 | tf_op jit(solution)/shard_map/ppermute | solution.py:26
  414.9 25.4 %collective-permute-start.67 = (bf16[128,512]{1,0:T(8,128)(2,1)S(1)}, bf16[128,512]{1,0:T(8,128)(2,1)S(1)}, u32[]{:S(2)}, u32[]{:S(2)}) collective-permute-start(bf16[128,512]{1,0:T(8,128)(2,1)S(1)} %get-tuple-element.382), channel_id=1, source_target_pairs={{0,1},{1,0},{2,3},{3,2},{4,5},{5,4},{6,7},{7,6},{8,9},{9,8},{10,11... | collective-permute-start | bytes 393224 | tf_op jit(solution)/shard_map/ppermute | solution.py:26
  415.0 31.9 %collective-permute-start.60 = (bf16[256,768]{1,0:T(8,128)(2,1)}, bf16[256,768]{1,0:T(8,128)(2,1)}, u32[]{:S(2)}, u32[]{:S(2)}) collective-permute-start(bf16[256,768]{1,0:T(8,128)(2,1)} %fusion.6), channel_id=1, source_target_pairs={{0,4},{1,5},{2,6},{3,7},{4,0},{5,1},{6,2},{7,3},{8,12},{9,13},{10,... | collective-permute-start | bytes 1179656 | tf_op jit(solution)/shard_map/ppermute | solution.py:26
  427.7 11.4 %collective-permute-start.58 = (f32[12,1024]{1,0:T(8,128)S(1)}, f32[12,1024]{1,0:T(8,128)S(1)}, u32[]{:S(2)}, u32[]{:S(2)}) collective-permute-start(f32[12,1024]{1,0:T(8,128)S(1)} %add.213), channel_id=1, source_target_pairs={{0,2},{1,3},{2,0},{3,1},{4,6},{5,7},{6,4},{7,5},{8,10},{9,11},{10,... | collective-permute-start | bytes 147464 | tf_op jit(solution)/shard_map/ppermute | solution.py:26
  439.1 17.3 %collective-permute-start.73 = (bf16[128,1024]{1,0:T(8,128)(2,1)}, bf16[128,1024]{1,0:T(8,128)(2,1)}, u32[]{:S(2)}, u32[]{:S(2)}) collective-permute-start(bf16[128,1024]{1,0:T(8,128)(2,1)} %add_convert_fusion.7.refs_0_), channel_id=1, source_target_pairs={{0,24},{8,16},{16,8},{24,0},{1,25},{9,17},{17,9},{25,1},{2,26},{10... | collective-permute-start | bytes 786440 | tf_op jit(solution)/shard_map/ppermute | solution.py:26
  445.7 9.5 %collective-permute-start.65 = (bf16[128,1024]{1,0:T(8,128)(2,1)}, bf16[128,1024]{1,0:T(8,128)(2,1)}, u32[]{:S(2)}, u32[]{:S(2)}) collective-permute-start(bf16[128,1024]{1,0:T(8,128)(2,1)} %fusion.11), channel_id=1, source_target_pairs={{0,8},{8,0},{16,24},{24,16},{1,9},{9,1},{17,25},{25,17},{2,10},{10... | collective-permute-start | bytes 786440 | tf_op jit(solution)/shard_map/ppermute | solution.py:26
  446.9 16.0 %collective-permute-start.68 = (bf16[256,512]{1,0:T(8,128)(2,1)}, bf16[256,512]{1,0:T(8,128)(2,1)}, u32[]{:S(2)}, u32[]{:S(2)}) collective-permute-start(bf16[256,512]{1,0:T(8,128)(2,1)} %pad_maximum_fusion.3.refs_0_), channel_id=1, source_target_pairs={{0,8},{8,0},{16,24},{24,16},{1,9},{9,1},{17,25},{25,17},{2,10},{10... | collective-permute-start | bytes 786440 | tf_op jit(solution)/shard_map/ppermute | solution.py:26
  449.0 13.9 %collective-permute-start.69 = (bf16[256,512]{1,0:T(8,128)(2,1)}, bf16[256,512]{1,0:T(8,128)(2,1)S(1)}, u32[]{:S(2)}, u32[]{:S(2)}) collective-permute-start(bf16[256,512]{1,0:T(8,128)(2,1)} %pad_maximum_fusion.3.refs_0_), channel_id=1, source_target_pairs={{0,16},{8,24},{16,0},{24,8},{1,17},{9,25},{17,1},{25,9},{2,18},{10... | collective-permute-start | bytes 786440 | tf_op jit(solution)/shard_map/ppermute | solution.py:26
  450.3 15.6 %collective-permute-start.70 = (bf16[256,512]{1,0:T(8,128)(2,1)}, bf16[256,512]{1,0:T(8,128)(2,1)S(1)}, u32[]{:S(2)}, u32[]{:S(2)}) collective-permute-start(bf16[256,512]{1,0:T(8,128)(2,1)} %pad_maximum_fusion.3.refs_0_), channel_id=1, source_target_pairs={{0,24},{8,16},{16,8},{24,0},{1,25},{9,17},{17,9},{25,1},{2,26},{10... | collective-permute-start | bytes 786440 | tf_op jit(solution)/shard_map/ppermute | solution.py:26
  455.2 14.9 %collective-permute-start.61 = (bf16[128,768]{1,0:T(8,128)(2,1)S(1)}, bf16[128,768]{1,0:T(8,128)(2,1)}, u32[]{:S(2)}, u32[]{:S(2)}) collective-permute-start(bf16[128,768]{1,0:T(8,128)(2,1)S(1)} %fusion.10), channel_id=1, source_target_pairs={{0,2},{1,3},{2,0},{3,1},{4,6},{5,7},{6,4},{7,5},{8,10},{9,11},{10,... | collective-permute-start | bytes 589832 | tf_op jit(solution)/shard_map/ppermute | solution.py:26
  456.4 18.3 %collective-permute-start.66 = (bf16[128,1024]{1,0:T(8,128)(2,1)S(1)}, bf16[128,1024]{1,0:T(8,128)(2,1)S(1)}, u32[]{:S(2)}, u32[]{:S(2)}) collective-permute-start(bf16[128,1024]{1,0:T(8,128)(2,1)S(1)} %fusion.8), channel_id=1, source_target_pairs={{0,16},{8,24},{16,0},{24,8},{1,17},{9,25},{17,1},{25,9},{2,18},{10... | collective-permute-start | bytes 786440 | tf_op jit(solution)/shard_map/ppermute | solution.py:26
  472.2 9.1 %collective-permute-start.63 = (bf16[128,768]{1,0:T(8,128)(2,1)S(1)}, bf16[128,768]{1,0:T(8,128)(2,1)S(1)}, u32[]{:S(2)}, u32[]{:S(2)}) collective-permute-start(bf16[128,768]{1,0:T(8,128)(2,1)S(1)} %fusion.7), channel_id=1, source_target_pairs={{0,24},{8,16},{16,8},{24,0},{1,25},{9,17},{17,9},{25,1},{2,26},{10... | collective-permute-start | bytes 589832 | tf_op jit(solution)/shard_map/ppermute | solution.py:26
  473.4 9.3 %collective-permute-start.64 = (bf16[128,768]{1,0:T(8,128)(2,1)S(1)}, bf16[128,768]{1,0:T(8,128)(2,1)S(1)}, u32[]{:S(2)}, u32[]{:S(2)}) collective-permute-start(bf16[128,768]{1,0:T(8,128)(2,1)S(1)} %fusion.7), channel_id=1, source_target_pairs={{0,16},{8,24},{16,0},{24,8},{1,17},{9,25},{17,1},{25,9},{2,18},{10... | collective-permute-start | bytes 589832 | tf_op jit(solution)/shard_map/ppermute | solution.py:26
  (84 other events, 809.7 us)
